TPU v7x, 32 devices: a whole 2x2x4 slice. The times are simulated.
32 devices in a mesh: dp: 8 (over z, y), tensor: 4 (over x, core).
Axes of the slice: x: 2, y: 2, z: 4, core: 2. Of those that a mesh axis runs over, the one named last changes fastest.
Arguments:
- hidden_in: bfloat16 [16384, 768], P(('dp', 'tensor')), may hold values from -6 to 6
- cotangent: bfloat16 [16384, 768], P(('dp', 'tensor')), may hold values from -6 to 6
- group_ids: int32 [16384], P(('dp', 'tensor')), may hold values from 0 to 15
- weight_table: float32 [8], replicated, may hold values from 0.3 to 3
- table_index: int32 [16], replicated, may hold values from 0 to 7
- qkv_weight: bfloat16 [768, 3, 768], P('dp', None, 'tensor'), may hold values from -0.21875 to 0.21875
- out_weight: bfloat16 [768, 768], P('tensor', 'dp'), may hold values from -0.75 to 0.75
- up_weight: bfloat16 [768, 3072], P('dp', 'tensor'), may hold values from -0.21875 to 0.21875
- down_weight: bfloat16 [3072, 768], P('tensor', 'dp'), may hold values from -0.109375 to 0.109375
- norm1_gain: bfloat16 [768], P('dp'), may hold values from 0.5 to 1.5
- norm1_bias: bfloat16 [768], P('dp'), may hold values from -1 to 1
- norm2_gain: bfloat16 [768], P('dp'), may hold values from 0.5 to 1.5
- norm2_bias: bfloat16 [768], P('dp'), may hold values from -1 to 1
Outputs:
- block_output: float32 [16384, 768], P(('dp', 'tensor'))
- input_grad: float32 [16384, 768], P(('dp', 'tensor'))
- qkv_weight_grad: float32 [768, 3, 768], P('dp', None, 'tensor')
- out_weight_grad: float32 [768, 768], P('tensor', 'dp')
- up_weight_grad: float32 [768, 3072], P('dp', 'tensor')
- down_weight_grad: float32 [3072, 768], P('tensor', 'dp')
- norm1_gain_grad: float32 [768], P(('dp', 'tensor'))
- norm1_bias_grad: float32 [768], P(('dp', 'tensor'))
- norm2_gain_grad: float32 [768], P(('dp', 'tensor'))
- norm2_bias_grad: float32 [768], P(('dp', 'tensor'))
- group_counts: float32 [16], replicated
All inputs are finite; a program needn't handle non-finite values.
Results may differ from a plain program's by a relative error of at most 0.017.
Values may be sent and summed in bfloat16 or wider, within the bound.
A program may use at most 128 MiB of HBM per device.

v0:
```python
import jax
import jax.numpy as jnp
from jax import lax
from jax.sharding import PartitionSpec as P

D = 768
HEAD_DIM = 64
LENGTH = 1024
SEQS = 2
GROUPS = 16
TABLE = 8


EPSILON = 1e-05
MASKED_SCORE = -1e30


def norm_forward(inputs, gain, shift):
    center = inputs - jnp.mean(inputs, -1, keepdims=True)
    inv_std = lax.rsqrt(jnp.mean(center * center, -1, keepdims=True) + EPSILON)
    normal_hat = center * inv_std
    return (normal_hat * gain + shift, normal_hat, inv_std)


def norm_backward(upper, normal_hat, inv_std, gain):
    scaled = upper * gain
    bracket = (
        scaled
        - jnp.mean(scaled, -1, keepdims=True)
        - normal_hat * jnp.mean(scaled * normal_hat, -1, keepdims=True)
    )
    return (inv_std * bracket, jnp.sum(upper * normal_hat, 0), jnp.sum(upper, 0))


def gelu_tanh(values):
    return jax.nn.gelu(values, approximate=True)


def causal_scores(query_block, key_block, first_row, factor):
    scores = (
        jnp.einsum("qhd,khd->hqk", query_block, key_block, preferred_element_type=jnp.float32)
        * factor
    )
    query_pos = first_row + lax.broadcasted_iota(jnp.int32, scores.shape, 1)
    key_pos = lax.broadcasted_iota(jnp.int32, scores.shape, 2)
    return jnp.where(key_pos <= query_pos, scores, MASKED_SCORE)


def shards(
    hidden_in,
    cotangent,
    group_ids,
    weight_table,
    table_index,
    qkv_weight,
    out_weight,
    up_weight,
    down_weight,
    norm1_gain,
    norm1_bias,
    norm2_gain,
    norm2_bias,
):
    local_rows = hidden_in.shape[0]
    total_tokens = local_rows * lax.axis_size("dp") * lax.axis_size("tensor")
    member = (group_ids[:, None] == jnp.arange(GROUPS, dtype=jnp.int32)[None, :]).astype(
        jnp.float32
    )
    group_counts = lax.psum(jnp.sum(member, 0), ("dp", "tensor"))
    gathered = (
        lax.all_gather(qkv_weight, "dp", axis=0, tiled=True),
        lax.all_gather(out_weight, "dp", axis=1, tiled=True),
        lax.all_gather(up_weight, "dp", axis=0, tiled=True),
        lax.all_gather(down_weight, "dp", axis=1, tiled=True),
        lax.all_gather(norm1_gain, "dp", axis=0, tiled=True),
        lax.all_gather(norm1_bias, "dp", axis=0, tiled=True),
        lax.all_gather(norm2_gain, "dp", axis=0, tiled=True),
        lax.all_gather(norm2_bias, "dp", axis=0, tiled=True),
    )
    qkv_full, out_full, up_full, down_full = (gathered[0], gathered[1], gathered[2], gathered[3])
    gain_first = gathered[4].astype(jnp.float32)
    bias_first = gathered[5].astype(jnp.float32)
    gain_second = gathered[6].astype(jnp.float32)
    bias_second = gathered[7].astype(jnp.float32)
    head_width = qkv_full.shape[2]
    local_heads = head_width // HEAD_DIM
    qkv_flat = qkv_full.reshape(D, 3 * head_width)
    factor = HEAD_DIM ** (-0.5)
    block_rows = min(512, LENGTH)
    block_count = LENGTH // block_rows
    all_blocks = SEQS * block_count
    seq_tokens = SEQS * LENGTH
    inputs = hidden_in.astype(jnp.float32)
    normed_one, hat_one, inv_one = norm_forward(inputs, gain_first, bias_first)
    normed_rows = lax.all_gather(normed_one.astype(jnp.bfloat16), "tensor", axis=0, tiled=True)
    projected = jnp.dot(normed_rows, qkv_flat, preferred_element_type=jnp.float32).astype(
        jnp.bfloat16
    )
    projected = projected.reshape(SEQS, LENGTH, 3, local_heads, HEAD_DIM)
    queries = projected[:, :, 0].reshape(all_blocks, block_rows, local_heads, HEAD_DIM)
    key_rows = projected[:, :, 1]
    value_rows = projected[:, :, 2]
    block_ids = jnp.arange(all_blocks, dtype=jnp.int32)

    def attend_block(packed):
        query_block, block_id = packed
        sequence = block_id // block_count
        first_row = block_id % block_count * block_rows
        keys_seq = lax.dynamic_index_in_dim(key_rows, sequence, 0, keepdims=False)
        values_seq = lax.dynamic_index_in_dim(value_rows, sequence, 0, keepdims=False)
        scores = causal_scores(query_block, keys_seq, first_row, factor)
        peak = jnp.max(scores, -1, keepdims=True)
        expon = jnp.exp(scores - peak)
        totals = jnp.sum(expon, -1, keepdims=True)
        probs = (expon / totals).astype(jnp.bfloat16)
        context = jnp.einsum("hqk,khd->qhd", probs, values_seq, preferred_element_type=jnp.float32)
        return (context.astype(jnp.bfloat16), (peak + jnp.log(totals))[..., 0])

    context, log_totals = lax.map(attend_block, (queries, block_ids))
    context_flat = context.reshape(seq_tokens, head_width)
    piece = context_flat
    middle = inputs + lax.psum_scatter(
        jnp.dot(piece, out_full, preferred_element_type=jnp.float32),
        "tensor",
        scatter_dimension=0,
        tiled=True,
    )
    normed_two, hat_two, inv_two = norm_forward(middle, gain_second, bias_second)
    normed_rows_two = lax.all_gather(normed_two.astype(jnp.bfloat16), "tensor", axis=0, tiled=True)
    pre_act = jnp.dot(normed_rows_two, up_full, preferred_element_type=jnp.float32)
    activ = gelu_tanh(pre_act).astype(jnp.bfloat16)
    piece = activ
    block_output = middle + lax.psum_scatter(
        jnp.dot(piece, down_full, preferred_element_type=jnp.float32).astype(jnp.bfloat16),
        "tensor",
        scatter_dimension=0,
        tiled=True,
    ).astype(jnp.float32)
    table_hits = table_index[:, None] == jnp.arange(TABLE, dtype=jnp.int32)[None, :]
    group_weight = jnp.sum(jnp.where(table_hits, weight_table[None, :], 0.0), 1)
    group_scale = group_weight * (total_tokens / GROUPS) / jnp.maximum(group_counts, 1.0)
    row_scale = jnp.sum(jnp.where(member > 0.5, group_scale[None, :], 0.0), 1)
    upstream = (cotangent.astype(jnp.float32) * row_scale[:, None]).astype(jnp.bfloat16)
    qkv_back, out_back, up_back, down_back = (qkv_flat, out_full, up_full, down_full)
    upstream_rows = lax.all_gather(upstream, "tensor", axis=0, tiled=True)
    d_activ = jnp.dot(upstream_rows, down_back.T, preferred_element_type=jnp.float32)
    gelu_pull = jax.vjp(gelu_tanh, pre_act)[1]
    d_pre = gelu_pull(d_activ)[0].astype(jnp.bfloat16)
    grad_down = jnp.dot(activ.T, upstream_rows, preferred_element_type=jnp.float32)
    grad_up = jnp.dot(normed_rows_two.T, d_pre, preferred_element_type=jnp.float32)
    piece = d_pre
    d_normed_two = lax.psum_scatter(
        jnp.dot(piece, up_back.T, preferred_element_type=jnp.float32),
        "tensor",
        scatter_dimension=0,
        tiled=True,
    )
    d_mid_norm, d_gain_two, d_bias_two = norm_backward(d_normed_two, hat_two, inv_two, gain_second)
    d_middle = upstream.astype(jnp.float32) + d_mid_norm
    middle_rows = lax.all_gather(d_middle.astype(jnp.bfloat16), "tensor", axis=0, tiled=True)
    grad_out = jnp.dot(context_flat.T, middle_rows, preferred_element_type=jnp.float32)
    d_context = jnp.dot(middle_rows, out_back.T, preferred_element_type=jnp.float32).astype(
        jnp.bfloat16
    )
    d_context = d_context.reshape(all_blocks, block_rows, local_heads, HEAD_DIM)

    def attend_back(packed):
        query_block, grad_block, log_block, block_id = packed
        sequence = block_id // block_count
        first_row = block_id % block_count * block_rows
        keys_seq = lax.dynamic_index_in_dim(key_rows, sequence, 0, keepdims=False)
        values_seq = lax.dynamic_index_in_dim(value_rows, sequence, 0, keepdims=False)
        scores = causal_scores(query_block, keys_seq, first_row, factor)
        probs = jnp.exp(scores - log_block[..., None])
        d_probs = jnp.einsum(
            "qhd,khd->hqk", grad_block, values_seq, preferred_element_type=jnp.float32
        )
        d_scores = (probs * (d_probs - jnp.sum(probs * d_probs, -1, keepdims=True))).astype(
            jnp.bfloat16
        )
        d_query = (
            jnp.einsum("hqk,khd->qhd", d_scores, keys_seq, preferred_element_type=jnp.float32)
            * factor
        )
        d_key = (
            jnp.einsum("hqk,qhd->khd", d_scores, query_block, preferred_element_type=jnp.float32)
            * factor
        )
        d_value = jnp.einsum(
            "hqk,qhd->khd",
            probs.astype(jnp.bfloat16),
            grad_block,
            preferred_element_type=jnp.float32,
        )
        return (d_query, d_key, d_value)

    d_query, d_key, d_value = lax.map(attend_back, (queries, d_context, log_totals, block_ids))
    d_query = d_query.reshape(SEQS, LENGTH, local_heads, HEAD_DIM)
    d_key = jnp.sum(d_key.reshape(SEQS, block_count, LENGTH, local_heads, HEAD_DIM), 1)
    d_value = jnp.sum(d_value.reshape(SEQS, block_count, LENGTH, local_heads, HEAD_DIM), 1)
    d_projected = (
        jnp.stack([d_query, d_key, d_value], 2)
        .astype(jnp.bfloat16)
        .reshape(seq_tokens, 3 * head_width)
    )
    grad_qkv = jnp.dot(normed_rows.T, d_projected, preferred_element_type=jnp.float32).reshape(
        D, 3, head_width
    )
    piece = d_projected
    d_normed_one = lax.psum_scatter(
        jnp.dot(piece, qkv_back.T, preferred_element_type=jnp.float32).astype(jnp.bfloat16),
        "tensor",
        scatter_dimension=0,
        tiled=True,
    ).astype(jnp.float32)
    d_in_norm, d_gain_one, d_bias_one = norm_backward(d_normed_one, hat_one, inv_one, gain_first)
    input_grad = d_middle + d_in_norm
    grad_qkv, grad_out, grad_up, grad_down = (
        lax.psum_scatter(grad_qkv, "dp", scatter_dimension=0, tiled=True),
        lax.psum_scatter(grad_out, "dp", scatter_dimension=1, tiled=True),
        lax.psum_scatter(grad_up, "dp", scatter_dimension=0, tiled=True),
        lax.psum_scatter(grad_down, "dp", scatter_dimension=1, tiled=True),
    )
    norm_parts = (
        lax.psum_scatter(d_gain_one, ("dp", "tensor"), scatter_dimension=0, tiled=True),
        lax.psum_scatter(d_bias_one, ("dp", "tensor"), scatter_dimension=0, tiled=True),
        lax.psum_scatter(d_gain_two, ("dp", "tensor"), scatter_dimension=0, tiled=True),
        lax.psum_scatter(d_bias_two, ("dp", "tensor"), scatter_dimension=0, tiled=True),
    )
    return (
        block_output,
        input_grad,
        grad_qkv,
        grad_out,
        grad_up,
        grad_down,
        norm_parts[0],
        norm_parts[1],
        norm_parts[2],
        norm_parts[3],
        group_counts,
    )


def solution(mesh):
    return jax.shard_map(
        shards,
        mesh=mesh,
        in_specs=(
            P(("dp", "tensor"), None),
            P(("dp", "tensor"), None),
            P(("dp", "tensor")),
            P(),
            P(),
            P("dp", None, "tensor"),
            P("tensor", "dp"),
            P("dp", "tensor"),
            P("tensor", "dp"),
            P("dp"),
            P("dp"),
            P("dp"),
            P("dp"),
        ),
        out_specs=(
            P(("dp", "tensor"), None),
            P(("dp", "tensor"), None),
            P("dp", None, "tensor"),
            P("tensor", "dp"),
            P("dp", "tensor"),
            P("tensor", "dp"),
            P(("dp", "tensor")),
            P(("dp", "tensor")),
            P(("dp", "tensor")),
            P(("dp", "tensor")),
            P(),
        ),
        check_vma=False,
    )
```

profile of v0, /device:TPU:0, one launch (start us, length us, event | category | flops | bytes accessed | tf_op | source)
XLA Modules:
  0.0 852.7 jit_solution(6379859181451184641)
XLA Ops:
  16.2 23.4 %all-reduce.9 = (bf16[768]{0:T(1024)(128)(2,1)S(1)}, bf16[768]{0:T(1024)(128)(2,1)S(1)}, bf16[768]{0:T(1024)(128)(2,1)S(1)}, bf16[768]{0:T(1024)(128)(2,1)S(1)}) all-reduce(bf16[768]{0:T(1024)(128)(2,1)S(1)} %dynamic-update-slice.1, bf16[768]{0:T(1024)(128)(2,1)S(1)} %dynamic-update-slice, ...), channel_id=1, replica_groups=mesh['dp'=8,'tensor'=4] {'dp'}, use_global_device_ids=true, to_apply=%add.1 | all-reduce | flops 3072 | bytes 12288
  42.9 35.2 %all_gather.39 = bf16[768,3,192]{2,1,0:T(4,128)(2,1)S(1)} all-gather(bf16[96,3,192]{2,1,0:T(4,128)(2,1)S(1)} %copy.62), channel_id=1, replica_groups=mesh['dp'=8,'tensor'=4] {'dp'}, dimensions={0}, use_global_device_ids=true | all-gather | bytes 995328 | tf_op jit(solution)/shard_map/all_gather | solution.py:71
  79.1 31.3 %all_gather.40 = bf16[192,768]{0,1:T(8,128)(2,1)S(1)} all-gather(bf16[192,96]{0,1:T(8,128)(2,1)S(1)} %copy.68), channel_id=1, replica_groups=mesh['dp'=8,'tensor'=4] {'dp'}, dimensions={1}, use_global_device_ids=true | all-gather | bytes 331776 | tf_op jit(solution)/shard_map/all_gather | solution.py:72
  127.6 41.7 %while.30 = (s32[]{:T(128)}, bf16[4,512,3,64]{1,3,2,0:T(8,128)(2,1)S(1)}, f32[4,3,512]{2,1,0:T(4,128)}, s32[4]{0:T(128)S(1)}, bf16[2,1024,3,64]{1,3,2,0:T(8,128)...) while((s32[]{:T(128)}, ...), condition=%wide.region_5.6_spmd, body=%wide.region_2.5_spmd.sunk | while | flops 426343456 | bytes 20117896 | solution.py:119
  177.0 39.4 %psum.7 = f32[16]{0:T(128)S(1)} all-reduce(f32[16]{0:T(128)S(1)} %convert_reduce_fusion.2), channel_id=1, replica_groups=mesh['dp'=8,'tensor'=4] {'dp','tensor'}, use_global_device_ids=true, to_apply=%region_12.13 | all-reduce | flops 16 | bytes 128 | tf_op jit(solution)/shard_map/psum | solution.py:69
  219.3 16.6 %reduce-scatter.11.cloned.1.call-done = f32[512,768]{1,0:T(8,128)} async-done(((f32[2048,768]{1,0:T(8,128)}), f32[512,768]{1,0:T(8,128)}) %reduce-scatter.11.cloned.1.call-update) | async-done | bytes 1572880 | tf_op jit(solution)/shard_map/reduce_scatter | solution.py:122
  239.2 13.2 %all-gather.15.cloned.1.call-done = bf16[2048,768]{1,0:T(8,128)(2,1)} async-done(((bf16[512,768]{1,0:T(8,128)(2,1)}), bf16[2048,768]{1,0:T(8,128)(2,1)}) %all-gather.15.cloned.1.call-update) | async-done | bytes 3145744 | tf_op jit(solution)/shard_map/all_gather | solution.py:145
  259.9 36.1 %all-gather.11.cloned.1.call-done = bf16[768,768]{1,0:T(8,128)(2,1)} async-done(((bf16[96,768]{1,0:T(8,128)(2,1)}), bf16[768,768]{1,0:T(8,128)(2,1)}) %all-gather.11.cloned.1.call-update) | async-done | bytes 1179664 | tf_op jit(solution)/shard_map/all_gather | solution.py:73
  295.9 29.1 %all-gather.9.cloned.1.call-done = bf16[2048,768]{1,0:T(8,128)(2,1)} async-done(((bf16[512,768]{1,0:T(8,128)(2,1)}), bf16[2048,768]{1,0:T(8,128)(2,1)}) %all-gather.9.cloned.1.call-update) | async-done | bytes 3145744 | tf_op jit(solution)/shard_map/all_gather | solution.py:129
  325.1 11.2 %fusion.54 = (bf16[2048,768]{1,0:T(8,128)(2,1)S(1)}, f32[2048,768]{1,0:T(8,128)}) fusion(f32[2048,768]{1,0:T(8,128)} %fusion.77, bf16[2048,768]{1,0:T(8,128)(2,1)} %all-gather.9.cloned.1.call-done, bf16[768,768]{1,0:T(8,128)(2,1)} %all-gather.11.cloned.1.call-done), kind=kOutput, calls=%fused_computation.66 | convolution fusion | flops 2447376384 | bytes 20054016 | tf_op jit(solution)/shard_map/dot_general | solution.py:130
  342.5 8.8 %convolution_convert_fusion = bf16[2048,768]{1,0:T(8,128)(2,1)} fusion(bf16[768,768]{0,1:T(8,128)(2,1)} %all-gather.13.cloned.1.call-done, f32[2048,768]{1,0:T(8,128)} %get-tuple-element.380), kind=kOutput, calls=%fused_computation.69 | convolution fusion | flops 2431647744 | bytes 10616832 | tf_op jit(solution)/shard_map/dot_general | solution.py:134
  351.3 49.4 %reduce-scatter.15.cloned.1.call-done = f32[512,768]{1,0:T(8,128)} async-done(((f32[2048,768]{1,0:T(8,128)}), f32[512,768]{1,0:T(8,128)}) %reduce-scatter.15.cloned.1.call-update) | async-done | bytes 1572880 | tf_op jit(solution)/shard_map/reduce_scatter | solution.py:152
  404.6 36.5 %reduce-scatter.13.cloned.1.call-done = bf16[512,768]{1,0:T(8,128)(2,1)} async-done(((bf16[2048,768]{1,0:T(8,128)(2,1)}), bf16[512,768]{1,0:T(8,128)(2,1)}) %reduce-scatter.13.cloned.1.call-update) | async-done | bytes 786448 | tf_op jit(solution)/shard_map/reduce_scatter | solution.py:133
  445.5 28.6 %all-gather.17.cloned.1.call-done = bf16[2048,768]{1,0:T(8,128)(2,1)} async-done(((bf16[512,768]{1,0:T(8,128)(2,1)}), bf16[2048,768]{1,0:T(8,128)(2,1)}) %all-gather.17.cloned.1.call-update) | async-done | bytes 3145744 | tf_op jit(solution)/shard_map/all_gather | solution.py:160
  483.3 90.8 %while.31 = (s32[]{:T(128)}, bf16[4,512,3,64]{1,0,3,2:T(4,128)(2,1)}, f32[4,1024,3,64]{1,3,2,0:T(8,128)}, f32[4,1024,3,64]{1,3,2,0:T(8,128)}, s32[4]{0:T(128)S(1...) while((s32[]{:T(128)}, ...), condition=%wide.region_19.20_spmd, body=%wide.region_17.19_spmd.sunk | while | flops 1022753792 | bytes 51747240 | solution.py:197
  498.1 8.0 dynamic_update_slice.47
  520.8 8.0 dynamic_update_slice.47
  543.5 8.0 dynamic_update_slice.47
  595.0 9.1 %fusion.72 = f32[768,768]{0,1:T(8,128)} fusion(bf16[2048,768]{1,0:T(8,128)(2,1)} %all-gather.15.cloned.1.call-done, f32[2048,768]{1,0:T(8,128)} %get-tuple-element.380), kind=kOutput, calls=%fused_computation.125 | convolution fusion | flops 2430074880 | bytes 11796480 | tf_op jit(solution)/shard_map/dot_general | solution.py:149
  612.4 13.4 %reduce-scatter.17.cloned.1.call-done = bf16[512,768]{1,0:T(8,128)(2,1)} async-done(((bf16[2048,768]{1,0:T(8,128)(2,1)}), bf16[512,768]{1,0:T(8,128)(2,1)}) %reduce-scatter.17.cloned.1.call-update) | async-done | bytes 786448 | tf_op jit(solution)/shard_map/reduce_scatter | solution.py:210
  627.9 41.4 %all-reduce.8 = (f32[768]{0:T(1024)S(1)}, f32[768]{0:T(1024)S(1)}, f32[768]{0:T(1024)S(1)}, f32[768]{0:T(1024)S(1)}) all-reduce(f32[768]{0:T(1024)S(1)} %get-tuple-element.320, f32[768]{0:T(1024)S(1)} %get-tuple-element.324, f32[768]{0:T(1024)S(1)} %copy-done.24, ...), channel_id=10, replica_groups=mesh['dp'=8,'tensor'=4] {'dp','tensor'}, use_global_device_ids=true, to_apply=%region_30.31.clone | all-reduce | flops 3072 | bytes 24576
  674.5 25.7 %reduce-scatter.21.cloned.1.call-done = f32[96,768]{1,0:T(8,128)} async-done(((f32[768,768]{1,0:T(8,128)}), f32[96,768]{1,0:T(8,128)}) %reduce-scatter.21.cloned.1.call-update) | async-done | bytes 294928 | tf_op jit(solution)/shard_map/reduce_scatter | solution.py:221
  700.1 72.7 %reduce-scatter.23.cloned.1.call-done = f32[768,96]{0,1:T(8,128)} async-done(((f32[768,768]{0,1:T(8,128)}), f32[768,96]{0,1:T(8,128)}) %reduce-scatter.23.cloned.1.call-update) | async-done | bytes 294928 | tf_op jit(solution)/shard_map/reduce_scatter | solution.py:222
  772.8 72.3 %reduce-scatter.19.cloned.1.call-done = f32[96,3,192]{2,0,1:T(8,128)} async-done(((f32[768,3,192]{2,0,1:T(8,128)}), f32[96,3,192]{2,0,1:T(8,128)}) %reduce-scatter.19.cloned.1.call-update) | async-done | bytes 221200 | tf_op jit(solution)/shard_map/reduce_scatter | solution.py:219
  (236 shorter events, 197.2 us)
Async XLA Ops:
  8.0 34.6 %copy-start.20 = (bf16[192,96]{1,0:T(8,128)(2,1)S(1)}, bf16[192,96]{1,0:T(8,128)(2,1)}, u32[]{:S(2)}) copy-start(bf16[192,96]{1,0:T(8,128)(2,1)} %param.23) | copy-start | bytes 110596
  8.0 34.8 %copy-start.15 = (bf16[96,3,192]{2,0,1:T(8,128)(2,1)S(1)}, bf16[96,3,192]{2,0,1:T(8,128)(2,1)}, u32[]{:S(2)}) copy-start(bf16[96,3,192]{2,0,1:T(8,128)(2,1)} %param.22) | copy-start | bytes 331780
  8.0 102.3 %all-gather.7.cloned.1.call-start = ((), (), s32[]{:S(2)}) async-start(), calls=%async_computation.8 | async-start | bytes 3932160 | tf_op jit(solution)/shard_map/all_gather | solution.py:95
  9.4 33.3 %copy-start.18 = (f32[512]{0:T(512)}, f32[512]{0:T(512)S(1)}, u32[]{:S(2)}) copy-start(f32[512]{0:T(512)S(1)} %broadcast_multiply_fusion.5) | copy-start | bytes 6148
  42.6 193.3 %reduce-scatter.11.cloned.1.call-start = ((), (), s32[]{:S(2)}) async-start(), calls=%async_computation.9 | async-start | bytes 7864320 | tf_op jit(solution)/shard_map/reduce_scatter | solution.py:122
  176.1 40.2 %copy-start.28 = (f32[8]{0:T(128)S(1)}, f32[8]{0:T(128)}, u32[]{:S(2)}) copy-start(f32[8]{0:T(128)} %param.20) | copy-start | bytes 100
  176.1 40.2 %copy-start.29 = (s32[16]{0:T(128)S(1)}, s32[16]{0:T(128)}, u32[]{:S(2)}) copy-start(s32[16]{0:T(128)} %param.21) | copy-start | bytes 196
  176.2 40.4 %copy-start.7 = (bf16[512,768]{1,0:T(8,128)(2,1)S(1)}, bf16[512,768]{1,0:T(8,128)(2,1)}, u32[]{:S(2)}) copy-start(bf16[512,768]{1,0:T(8,128)(2,1)} %param.18) | copy-start | bytes 2359300
  176.2 59.7 %copy-start = (bf16[512,768]{1,0:T(8,128)(2,1)S(1)}, bf16[512,768]{1,0:T(8,128)(2,1)}, u32[]{:S(2)}) copy-start(bf16[512,768]{1,0:T(8,128)(2,1)} %param.17) | copy-start | bytes 2359300
  176.2 63.0 %all-gather.13.cloned.1.call-start = ((), (), s32[]{:S(2)}) async-start(), calls=%async_computation.12 | async-start | bytes 1327104 | tf_op jit(solution)/shard_map/all_gather | solution.py:74
  176.8 75.5 %all-gather.15.cloned.1.call-start = ((), (), s32[]{:S(2)}) async-start(), calls=%async_computation.14 | async-start | bytes 3932160 | tf_op jit(solution)/shard_map/all_gather | solution.py:145
  217.6 78.3 %all-gather.11.cloned.1.call-start = ((), (), s32[]{:S(2)}) async-start(), calls=%async_computation.11 | async-start | bytes 1327104 | tf_op jit(solution)/shard_map/all_gather | solution.py:73
  218.2 106.9 %all-gather.9.cloned.1.call-start = ((), (), s32[]{:S(2)}) async-start(), calls=%async_computation.10 | async-start | bytes 3932160 | tf_op jit(solution)/shard_map/all_gather | solution.py:129
  239.1 161.7 %reduce-scatter.15.cloned.1.call-start = ((), (), s32[]{:S(2)}) async-start(), calls=%async_computation.15 | async-start | bytes 7864320 | tf_op jit(solution)/shard_map/reduce_scatter | solution.py:152
  342.4 98.7 %reduce-scatter.13.cloned.1.call-start = ((), (), s32[]{:S(2)}) async-start(), calls=%async_computation.13 | async-start | bytes 3932160 | tf_op jit(solution)/shard_map/reduce_scatter | solution.py:133
  351.2 89.9 %copy-start.8 = (bf16[512,768]{1,0:T(8,128)(2,1)S(1)}, bf16[512,768]{1,0:T(8,128)(2,1)}, u32[]{:S(2)}) copy-start(bf16[512,768]{1,0:T(8,128)(2,1)} %param.18) | copy-start | bytes 2359300
  351.3 122.9 %all-gather.17.cloned.1.call-start = ((), (), s32[]{:S(2)}) async-start(), calls=%async_computation.16 | async-start | bytes 3932160 | tf_op jit(solution)/shard_map/all_gather | solution.py:160
  445.5 165.2 %reduce-scatter.25.cloned.1.call-start = ((), (), s32[]{:S(2)}) async-start(), calls=%async_computation.21 | async-start | bytes 884736
  445.5 33.4 %copy-start.6 = (bf16[24,8,4,512]{3,1,2,0:T(8,128)(2,1)S(1)}, bf16[24,8,4,512]{3,1,2,0:T(8,128)(2,1)}, u32[]{:S(2)}) copy-start(bf16[24,8,4,512]{3,1,2,0:T(8,128)(2,1)} %copy-done.5) | copy-start | bytes 2359300
  483.1 142.8 %reduce-scatter.17.cloned.1.call-start = ((), (), s32[]{:S(2)}) async-start(), calls=%async_computation.17 | async-start | bytes 3932160 | tf_op jit(solution)/shard_map/reduce_scatter | solution.py:210
  587.9 112.2 %reduce-scatter.21.cloned.1.call-start = ((), (), s32[]{:S(2)}) async-start(), calls=%async_computation.19 | async-start | bytes 2654208 | tf_op jit(solution)/shard_map/reduce_scatter | solution.py:221
  595.0 177.9 %reduce-scatter.23.cloned.1.call-start = ((), (), s32[]{:S(2)}) async-start(), calls=%async_computation.20 | async-start | bytes 2654208 | tf_op jit(solution)/shard_map/reduce_scatter | solution.py:222
  604.2 241.0 %reduce-scatter.19.cloned.1.call-start = ((), (), s32[]{:S(2)}) async-start(), calls=%async_computation.18 | async-start | bytes 2654208 | tf_op jit(solution)/shard_map/reduce_scatter | solution.py:219
  610.6 61.0 %copy-start.4 = (f32[512,768]{1,0:T(8,128)S(1)}, f32[512,768]{1,0:T(8,128)}, u32[]{:S(2)}) copy-start(f32[512,768]{1,0:T(8,128)} %get-tuple-element.368) | copy-start | bytes 4718596
  (22 other events, 228.6 us)
Sparse Core Ops, SparseCore 0:
  42.7 25.7 all-gather.6
  176.3 59.5 reduce-scatter.10
  445.6 28.5 all-gather.16
Sparse Core Ops, SparseCore 1:
  178.9 42.0 all-gather.12
  222.9 29.4 all-gather.14
  254.4 41.5 all-gather.10
  298.2 26.8 all-gather.8
  342.5 58.2 reduce-scatter.14
  403.3 37.8 reduce-scatter.12
  483.2 62.5 reduce-scatter.24
  588.0 37.8 reduce-scatter.16
  630.2 69.8 reduce-scatter.20
  704.6 68.2 reduce-scatter.22
  777.2 67.9 reduce-scatter.18
where the time goes:
time: 859 us; the launch traced here: 853 us
  waiting for transfers between devices  395 us (46%)
  blocking collectives  171 us (20%)
  matrix products  134 us (16%)
  local copies, waits for them, and re-layouts  75.7 us (9%)
  other arithmetic  38.5 us (4%)
  loops' own time  21.1 us (2%)
  between operations  17 us (2%)
    reduce_scatter x1, waiting for transfers between devices, shards(): lax.psum_scatter(grad_down, 'dp', scatter_dimension=1, tiled=True)  72.7 us
    reduce_scatter x1, waiting for transfers between devices, shards(): lax.psum_scatter(grad_qkv, 'dp', scatter_dimension=0, tiled=True)  72.3 us
    unnamed x2, blocking collectives  64.8 us
    reduce_scatter x1, waiting for transfers between devices, shards(): lax.psum_scatter(jnp.dot(piece, up_back.T, preferred_element_type=jnp.flo...  49.4 us
    psum x1, blocking collectives, shards(): group_counts = lax.psum(jnp.sum(member, 0), ('dp', 'tensor'))  39.4 us
    reduce_scatter x1, waiting for transfers between devices, shards(): lax.psum_scatter(jnp.dot(piece, down_full, preferred_element_type=jnp.flo...  36.5 us
    all_gather x1, waiting for transfers between devices, shards(): lax.all_gather(up_weight, 'dp', axis=0, tiled=True)  36.1 us
    all_gather x1, blocking collectives, shards(): lax.all_gather(qkv_weight, 'dp', axis=0, tiled=True)  35.2 us
  transfers between devices with their start and end apart: 14, of which 11 were waited for; matrix products, arithmetic and copies ran while one was open for 18% of the time, Pallas kernels for 0%

commit v1 on v0

v1 whole, which is shorter than its diff:
```python
import functools

import jax
import jax.numpy as jnp
from jax import lax
from jax.experimental import pallas as pl
from jax.experimental.pallas import tpu as pltpu
from jax.sharding import PartitionSpec as P

D = 768
HEAD_DIM = 64
LENGTH = 1024
HALF = 512
GROUPS = 16
TABLE = 8
NB = 8
RB = D // NB
HEADROWS = 144
EPSILON = 1e-05
MASKED_SCORE = -1e30
GELU_C = 0.7978845608028654
GELU_A = 0.044715
MESH = pl.DeviceIdType.MESH
F32 = jnp.float32
BF16 = jnp.bfloat16
NT = (((1,), (1,)), ((), ()))
TN = (((0,), (0,)), ((), ()))
NN = (((1,), (0,)), ((), ()))
VMEM_LIMIT = 66_000_000


def mm(a, b, dims=NN):
    return lax.dot_general(a, b, dims, preferred_element_type=F32)


class Place:
    def __init__(self):
        self.d = lax.axis_index("dp")
        self.t = lax.axis_index("tensor")
        self.z = lax.div(self.d, 2)
        self.y = lax.rem(self.d, 2)
        self.x = lax.div(self.t, 2)
        self.c = lax.rem(self.t, 2)
        c = self.c
        self.sibling = (self.d, self.t + 1 - 2 * c)
        self.x1 = lax.rem(self.x + c, 2)
        self.y1 = lax.rem(self.y + 1 - c, 2)
        self.x2 = lax.rem(self.x + 1 - c, 2)
        self.y2 = lax.rem(self.y + c, 2)
        self.p1 = (2 * self.z + self.y1, 2 * self.x1 + c)
        self.p2 = (2 * self.z + self.y2, 2 * self.x2 + c)
        self.up = (self.d + 2, self.t)
        self.dn = (self.d - 2, self.t)
        self.has_up = self.z < 3
        self.has_dn = self.z > 0


def entry_barrier(pos, net):
    bar = pltpu.get_barrier_semaphore()
    pl.semaphore_signal(bar, inc=1, device_id=pos.sibling, device_id_type=MESH)
    if not net:
        pl.semaphore_wait(bar, 1)
        return
    pl.semaphore_signal(bar, inc=1, device_id=pos.p1, device_id_type=MESH)
    pl.semaphore_signal(bar, inc=1, device_id=pos.p2, device_id_type=MESH)

    @pl.when(pos.has_up)
    def _():
        pl.semaphore_signal(bar, inc=1, device_id=pos.up, device_id_type=MESH)

    @pl.when(pos.has_dn)
    def _():
        pl.semaphore_signal(bar, inc=1, device_id=pos.dn, device_id_type=MESH)

    pl.semaphore_wait(bar, 3 + jnp.where(pos.has_up, 1, 0) + jnp.where(pos.has_dn, 1, 0))


class Gather:
    def __init__(self, pos, g, own, full, ssem, rsem):
        self.pos, self.g, self.own, self.full = pos, g, own, full
        self.ssem, self.rsem = ssem, rsem

    def copy(self, b, dd, link, zz, dev, src=None):
        slot = self.full.at[b, dd]
        return pltpu.make_async_remote_copy(
            src_ref=slot if src is None else src,
            dst_ref=slot,
            send_sem=self.ssem.at[self.g, link, zz],
            recv_sem=self.rsem.at[self.g, b, dd],
            device_id=dev,
            device_id_type=MESH,
        )

    def wait(self, b, dd):
        self.copy(b, dd, 0, 0, self.pos.p1).wait_recv()

    def start(self):
        p = self.pos
        own = self.own
        self.copy(p.x, p.d, 2, p.z, p.p1, own).start()
        self.copy(p.x, p.d, 3, p.z, p.p2, own).start()

        @pl.when(p.has_up)
        def _():
            self.copy(p.x, p.d, 0, p.z, p.up, own).start()

        @pl.when(p.has_dn)
        def _():
            self.copy(p.x, p.d, 1, p.z, p.dn, own).start()

    def line(self, k):
        p = self.pos

        @pl.when(p.z - k >= 0)
        def _():
            zz = p.z - k
            self.wait(p.x, 2 * zz + p.y)

            @pl.when(p.has_up)
            def _():
                self.copy(p.x, 2 * zz + p.y, 0, zz, p.up).start()

            self.copy(p.x, 2 * zz + p.y, 2, zz, p.p1).start()
            self.copy(p.x, 2 * zz + p.y, 3, zz, p.p2).start()

        @pl.when(p.z + k <= 3)
        def _():
            zz = p.z + k
            self.wait(p.x, 2 * zz + p.y)

            @pl.when(p.has_dn)
            def _():
                self.copy(p.x, 2 * zz + p.y, 1, zz, p.dn).start()

            self.copy(p.x, 2 * zz + p.y, 2, zz, p.p1).start()
            self.copy(p.x, 2 * zz + p.y, 3, zz, p.p2).start()

    def side(self, k):
        p = self.pos

        def forward(zz):
            self.wait(p.x1, 2 * zz + p.y1)
            self.copy(p.x1, 2 * zz + p.y1, 4, zz, p.p2).start()

        if k == 0:
            forward(p.z)
            return

        @pl.when(p.z - k >= 0)
        def _():
            forward(p.z - k)

        @pl.when(p.z + k <= 3)
        def _():
            forward(p.z + k)

    def step(self, k):
        if k == 0:
            self.start()
        if 1 <= k <= 3:
            self.line(k)
        if k >= 1:
            self.side(k - 1)

    def finish(self):
        p = self.pos
        for zz in range(4):
            self.wait(p.x2, 2 * zz + p.y2)
            self.wait(1 - p.x, 2 * zz + 1 - p.y)

    def drain(self):
        p = self.pos
        for zz in range(4):
            dd = 2 * zz + p.y

            @pl.when(p.has_up & (zz <= p.z))
            def _():
                self.copy(p.x, dd, 0, zz, p.up).wait_send()

            @pl.when(p.has_dn & (zz >= p.z))
            def _():
                self.copy(p.x, dd, 1, zz, p.dn).wait_send()

            self.copy(p.x, dd, 2, zz, p.p1).wait_send()
            self.copy(p.x, dd, 3, zz, p.p2).wait_send()
            self.copy(p.x1, 2 * zz + p.y1, 4, zz, p.p2).wait_send()


class Reduce:
    def __init__(self, pos, g, part, r2, rz, ssem, rsem):
        self.pos, self.g, self.part, self.r2, self.rz = pos, g, part, r2, rz
        self.ssem, self.rsem = ssem, rsem

    def copy(self, src, dst, link, zz, dev):
        return pltpu.make_async_remote_copy(
            src_ref=src,
            dst_ref=dst,
            send_sem=self.ssem.at[self.g, link, zz],
            recv_sem=self.rsem.at[self.g, link, zz],
            device_id=dev,
            device_id_type=MESH,
        )

    def to_p2(self, which, zz):
        p = self.pos
        b, dd = (p.x2, 2 * zz + p.y2) if which == 0 else (1 - p.x, 2 * zz + 1 - p.y)
        return self.copy(self.part.at[b, dd], self.r2.at[which, zz], which, zz, p.p2)

    def to_p1(self, zz):
        p = self.pos
        return self.copy(self.part.at[p.x1, 2 * zz + p.y1], self.rz.at[0, zz], 2, zz, p.p1)

    def to_z(self, way, zz):
        p = self.pos
        return self.copy(
            self.part.at[p.x, 2 * zz + p.y], self.rz.at[1 + way, zz], 3 + way, zz, p.dn if way else p.up
        )

    def add(self, b, dd, other):
        total = self.part[b, dd].astype(F32) + other.astype(F32)
        self.part[b, dd] = total.astype(self.part.dtype)

    def start(self):
        for which in (1, 0):
            for zz in range(4):
                self.to_p2(which, zz).start()

    def middle(self):
        p = self.pos
        for zz in range(4):
            self.to_p2(1, zz).wait_recv()
            self.add(p.x1, 2 * zz + p.y1, self.r2[1, zz])
            self.to_p1(zz).start()
        for zz in range(4):
            self.to_p2(0, zz).wait_recv()
            self.add(p.x, 2 * zz + p.y, self.r2[0, zz])

    def line(self):
        p = self.pos
        for zz in range(4):
            self.to_p1(zz).wait_recv()
            self.add(p.x, 2 * zz + p.y, self.rz[0, zz])
        for zz in (3, 2, 1):

            @pl.when(zz > p.z)
            def _():
                @pl.when(p.has_dn)
                def _():
                    self.to_z(0, zz).wait_recv()
                    self.add(p.x, 2 * zz + p.y, self.rz[1, zz])

                self.to_z(0, zz).start()

            dz = 3 - zz

            @pl.when(dz < p.z)
            def _():
                @pl.when(p.has_up)
                def _():
                    self.to_z(1, dz).wait_recv()
                    self.add(p.x, 2 * dz + p.y, self.rz[2, dz])

                self.to_z(1, dz).start()

    def finish(self, out):
        p = self.pos
        out[...] = self.part[p.x, p.d].astype(F32)

        @pl.when(p.has_dn)
        def _():
            self.to_z(0, p.z).wait_recv()
            out[...] += self.rz[1, p.z].astype(F32)

        @pl.when(p.has_up)
        def _():
            self.to_z(1, p.z).wait_recv()
            out[...] += self.rz[2, p.z].astype(F32)

    def drain(self):
        p = self.pos
        for zz in range(4):
            self.to_p2(1, zz).wait_send()
            self.to_p2(0, zz).wait_send()
            self.to_p1(zz).wait_send()

            @pl.when(zz > p.z)
            def _():
                self.to_z(0, zz).wait_send()

            @pl.when(zz < p.z)
            def _():
                self.to_z(1, zz).wait_send()


def rows(start, size):
    return pl.ds(pl.multiple_of(start, size), size)


def swap(pos, src, dst, sems, i):
    return pltpu.make_async_remote_copy(
        src_ref=src,
        dst_ref=dst,
        send_sem=sems.at[0, i],
        recv_sem=sems.at[1, i],
        device_id=pos.sibling,
        device_id_type=MESH,
    )


def norm_stats(values):
    center = values - jnp.mean(values, -1, keepdims=True)
    inv = lax.rsqrt(jnp.mean(center * center, -1, keepdims=True) + EPSILON)
    return center * inv, inv


def lane_half(shape, which):
    lane = lax.broadcasted_iota(jnp.int32, shape, 1)
    return (lane < HEAD_DIM) if which == 0 else (lane >= HEAD_DIM)


def only(values, which):
    return jnp.where(lane_half(values.shape, which), values, jnp.zeros_like(values))


def roll_half(values):
    return pltpu.roll(values.astype(F32), HEAD_DIM, 1).astype(BF16)


def unpack_heads(raw, wh):
    @pl.loop(0, NB)
    def _(dd):
        at = pl.multiple_of(dd * RB, 16)
        for part in range(4):
            wh[part, 0, pl.ds(at, RB)] = raw[0, dd, part, 0:96]
            wh[part, 1, pl.ds(at, RB)] = raw[1, dd, part, 0:96]
            first, second = raw[0, dd, part, 96:144], raw[1, dd, part, 96:144]
            left = lane_half(first.shape, 0)
            wh[part, 2, pl.ds(at, 48)] = jnp.where(left, first, roll_half(second))
            wh[part, 2, pl.ds(at + 48, 48)] = jnp.where(left, roll_half(first), second)


def pack_heads(gh, raw):
    @pl.loop(0, NB)
    def _(dd):
        at = pl.multiple_of(dd * RB, 16)
        for part in range(4):
            raw[0, dd, part, 0:96] = gh[part, 0, pl.ds(at, RB)]
            raw[1, dd, part, 0:96] = gh[part, 1, pl.ds(at, RB)]
            top, bottom = gh[part, 2, pl.ds(at, 48)], gh[part, 2, pl.ds(at + 48, 48)]
            left = lane_half(top.shape, 0)
            raw[0, dd, part, 96:144] = jnp.where(left, top, roll_half(bottom))
            raw[1, dd, part, 96:144] = jnp.where(left, roll_half(top), bottom)


def cat_pairs(ref, parts, pick):
    return jnp.concatenate([pick(ref, part, pair) for part in parts for pair in range(3)], axis=1)


def transpose_rows(src, dst):
    @pl.loop(0, LENGTH // 128)
    def _(i):
        r = rows(i * 128, 128)
        dst[:, r] = src[r, :].T


def forward_kernel(net, scale_tokens, *refs):
    (hid, cot, ids, table, weights, small, own1, own2, own3) = refs[:9]
    (o_block, o_counts, o_param, o_mid, o_heads, o_up, o_down, o_nrmT, o_qkv, o_lse, o_ctx, o_n2T, o_act, o_slope, o_ups, o_upsT) = refs[9:25]
    (
        v_small, v_raw, v_up, v_down, v_heads, v_param, v_counts, v_cnt, v_nrm, v_nrmT, v_qkv, v_lse, v_ctx,
        v_mid, v_n2, v_n2T, v_act, v_slope, v_ups, v_upsT, v_send, v_recv, v_acc, v_block,
        ssem, rsem, swsem, osem,
    ) = refs[25:]
    pos = Place()
    c = pos.c
    mine = c * HALF
    theirs = HALF - mine
    entry_barrier(pos, net)
    lanes = lax.broadcasted_iota(jnp.int32, (HALF, 128), 1)
    member = ids[...] == lanes
    own_counts = jnp.sum(member.astype(F32), 0, keepdims=True)

    puts = []

    def put(src, dst):
        cp = pltpu.make_async_copy(src, dst, osem.at[len(puts)])
        cp.start()
        puts.append(cp)

    if net:
        v_cnt[2] = small[...]
        v_cnt[2, 4:5, :] = own_counts
        g0 = Gather(pos, 0, v_cnt.at[2], v_small, ssem, rsem)
        g1 = Gather(pos, 1, own1, v_raw, ssem, rsem)
        g2 = Gather(pos, 2, own2, v_up, ssem, rsem)
        g3 = Gather(pos, 3, own3, v_down, ssem, rsem)
        g0.step(0)
        g1.step(0)
        v_small[pos.x, pos.d] = v_cnt[2]
        v_raw[pos.x, pos.d] = own1[...]
        v_up[pos.x, pos.d] = own2[...]
        v_down[pos.x, pos.d] = own3[...]
        for k in (1, 2, 3, 4):
            g0.step(k)
            g1.step(k)
        g0.finish()
        g2.step(0)
        v_param[...] = jnp.zeros_like(v_param)
        total = jnp.zeros((8, 128), F32)
        for dd in range(NB):
            row = lax.broadcasted_iota(jnp.int32, (128, D), 0)
            col = lax.broadcasted_iota(jnp.int32, (128, D), 1)
            place = ((col == row + RB * dd) & (row < RB)).astype(BF16)
            block = v_small[pos.x, dd]
            v_param[...] += mm(block.astype(BF16), place)
            total += v_small[0, dd] + v_small[1, dd]
        v_cnt[0] = total
        swap(pos, v_cnt.at[0], v_cnt.at[1], swsem, 0).start()
    else:
        v_param[...] = small[...]
        v_cnt[0] = jnp.broadcast_to(own_counts, (8, 128))
        cps = [
            pltpu.make_async_copy(own1, v_raw, osem.at[16]),
            pltpu.make_async_copy(own2, v_up, osem.at[17]),
            pltpu.make_async_copy(own3, v_down, osem.at[18]),
        ]
        for cp in cps:
            cp.start()
        for cp in cps:
            cp.wait()

    @pl.loop(0, HALF // 64)
    def _(i):
        r = rows(i * 64, 64)
        hat, _inv = norm_stats(hid[r, :].astype(F32))
        normed = hat * v_param[0:1, :] + v_param[1:2, :]
        v_nrm[rows(mine + i * 64, 64), :] = normed.astype(BF16)

    swap_nrm = swap(pos, v_nrm.at[rows(mine, HALF)], v_nrm.at[rows(mine, HALF)], swsem, 1)
    swap_nrm.start()

    if net:
        swap(pos, v_cnt.at[0], v_cnt.at[1], swsem, 0).wait()
        counts = (v_cnt[0] + v_cnt[1])[4:5, :]
        v_counts[...] = jnp.broadcast_to(counts, (8, 128))
        index = table[0:1, :]
        weight = jnp.zeros((1, 128), F32)
        for r in range(TABLE):
            weight = weight + jnp.where(index == r, weights[r], 0.0)
        group_scale = weight * scale_tokens / jnp.maximum(counts, 1.0)
    else:
        v_counts[...] = table[...].astype(F32)
        group_scale = weights[0:1, :]

    row_scale = jnp.sum(jnp.where(member, group_scale, 0.0), 1, keepdims=True)
    v_ups[rows(mine, HALF), :] = (cot[...].astype(F32) * row_scale).astype(BF16)
    swap_ups = swap(pos, v_ups.at[rows(mine, HALF)], v_ups.at[rows(mine, HALF)], swsem, 2)
    swap_ups.start()

    if net:
        g1.finish()
    unpack_heads(v_raw, v_heads)
    put(v_heads, o_heads)
    put(v_param, o_param)
    put(v_counts, o_counts)

    if net:
        g2.step(1)
    for half, start in enumerate((mine, theirs)):
        if half == 1:
            swap(pos, v_nrm.at[rows(theirs, HALF)], v_nrm.at[rows(theirs, HALF)], swsem, 1).wait_recv()
        lhs = v_nrm[rows(start, HALF), :]
        for part in range(3):
            rhs = cat_pairs(v_heads, (part,), lambda ref, a, b: ref[a, b])
            res = mm(lhs, rhs).astype(BF16)
            if part == 0:
                res = (res.astype(F32) * HEAD_DIM**-0.5).astype(BF16)
            for pair in range(3):
                v_qkv[3 * part + pair, rows(start, HALF), :] = res[:, 128 * pair : 128 * pair + 128]
    put(v_qkv, o_qkv)
    if net:
        g2.step(2)

    @pl.loop(0, 3)
    def _(pair):
        if net:

            @pl.when(pair == 1)
            def _():
                g2.step(3)

            @pl.when(pair == 2)
            def _():
                g2.step(4)
                g3.step(0)

        for i in range(4):
            n = 256 * (i + 1)
            q = v_qkv[pair, 256 * i : n, :]
            out = jnp.zeros((256, 128), F32)
            for h in range(2):
                pieces = []
                peak = None
                for j in range(i + 1):
                    k = only(v_qkv[3 + pair, 256 * j : 256 * j + 256, :], h)
                    s = mm(k, q, NT)
                    if j == i:
                        key = lax.broadcasted_iota(jnp.int32, s.shape, 0)
                        query = lax.broadcasted_iota(jnp.int32, s.shape, 1)
                        s = jnp.where(key <= query, s, MASKED_SCORE)
                    top = jnp.max(s, 0, keepdims=True)
                    peak = top if peak is None else jnp.maximum(peak, top)
                    pieces.append(s)
                total = jnp.zeros((1, 256), F32)
                for j in range(i + 1):
                    e = jnp.exp(pieces[j] - peak)
                    total += jnp.sum(e, 0, keepdims=True)
                    pieces[j] = e
                inv = 1.0 / total
                for j in range(i + 1):
                    v = only(v_qkv[6 + pair, 256 * j : 256 * j + 256, :], h)
                    out += mm((pieces[j] * inv).astype(BF16), v, TN)
                v_lse[pair, h : h + 1, 256 * i : n] = peak + jnp.log(total)
            v_ctx[pair, 256 * i : n, :] = out.astype(BF16)

    put(v_lse, o_lse)
    put(v_ctx, o_ctx)
    if net:
        g3.step(1)

    w_out = cat_pairs(v_heads, (3,), lambda ref, a, b: ref[a, b])
    for half, start in enumerate((theirs, mine)):
        lhs = jnp.concatenate([v_ctx[pair, rows(start, HALF), :] for pair in range(3)], axis=1)
        res = mm(lhs, w_out, NT)
        if half == 0:
            v_send[0] = res.astype(BF16)
            swap(pos, v_send.at[0], v_recv.at[0], swsem, 3).start()
        else:
            v_acc[...] = res
    if net:
        g3.step(2)
    transpose_rows(v_nrm, v_nrmT)
    put(v_nrmT, o_nrmT)
    swap(pos, v_send.at[0], v_recv.at[0], swsem, 3).wait()

    @pl.loop(0, HALF // 64)
    def _(i):
        r = rows(i * 64, 64)
        middle = hid[r, :].astype(F32) + v_acc[r, :] + v_recv[0, r, :].astype(F32)
        v_mid[r, :] = middle
        hat, _inv = norm_stats(middle)
        v_n2[rows(mine + i * 64, 64), :] = (hat * v_param[2:3, :] + v_param[3:4, :]).astype(BF16)

    swap(pos, v_n2.at[rows(mine, HALF)], v_n2.at[rows(mine, HALF)], swsem, 4).start()
    put(v_mid, o_mid)
    if net:
        g2.finish()
        g3.step(3)
    put(v_up, o_up)

    for half, start in enumerate((mine, theirs)):
        if half == 1:
            swap(pos, v_n2.at[rows(theirs, HALF)], v_n2.at[rows(theirs, HALF)], swsem, 4).wait_recv()

        @pl.loop(0, 6)
        def _(tile):
            b = lax.div(tile, 3)
            cols = pl.ds(pl.multiple_of(lax.rem(tile, 3) * 256, 256), 256)
            pre = mm(v_n2[rows(start, HALF), :], v_up[b, :, :, cols].reshape(D, 256))
            square = pre * pre
            bend = jnp.tanh(GELU_C * pre * (1.0 + GELU_A * square))
            v_act[b, rows(start, HALF), cols] = (0.5 * pre * (1.0 + bend)).astype(BF16)
            slope = 0.5 * (1.0 + bend) + 0.5 * pre * (1.0 - bend * bend) * (GELU_C * (1.0 + 3.0 * GELU_A * square))
            v_slope[b, rows(start, HALF), cols] = slope.astype(BF16)

        if net and half == 0:
            g3.step(4)

    put(v_act, o_act)
    put(v_slope, o_slope)
    transpose_rows(v_n2, v_n2T)
    put(v_n2T, o_n2T)
    swap(pos, v_ups.at[rows(theirs, HALF)], v_ups.at[rows(theirs, HALF)], swsem, 2).wait_recv()
    put(v_ups, o_ups)
    transpose_rows(v_ups, v_upsT)
    put(v_upsT, o_upsT)
    if net:
        g3.finish()
    put(v_down, o_down)
    for half, start in enumerate((theirs, mine)):
        res = mm(v_act[0, rows(start, HALF), :], v_down[0].reshape(D, D), NT)
        res += mm(v_act[1, rows(start, HALF), :], v_down[1].reshape(D, D), NT)
        if half == 0:
            v_send[1] = res.astype(BF16)
            swap(pos, v_send.at[1], v_recv.at[1], swsem, 5).start()
        else:
            v_acc[...] = res
    swap(pos, v_send.at[1], v_recv.at[1], swsem, 5).wait()
    v_block[...] = v_mid[...] + v_acc[...] + v_recv[1].astype(F32)
    put(v_block, o_block)
    for i, ref in ((1, v_nrm), (2, v_ups), (4, v_n2)):
        swap(pos, ref.at[rows(mine, HALF)], ref.at[rows(mine, HALF)], swsem, i).wait_send()
    if net:
        for g in (g0, g1, g2, g3):
            g.drain()
    for cp in puts:
        cp.wait()


def backward_kernel(net, *refs):
    (hid, param, h_mid, h_heads, h_up, h_down, h_nrmT, h_qkv, h_lse, h_ctx, h_n2T, h_act, h_slope, h_ups, h_upsT) = refs[:15]
    nout = 5
    o_in, o_small, o1, o2, o3 = refs[15 : 15 + nout]
    (
        v_mid, v_heads, v_up, v_down, v_nrmT, v_qkv, v_lse, v_ctx, v_n2T, v_act, v_slope, v_ups, v_upsT,
        v_low, v_dmid, v_dctx, v_dqkv, v_dk, v_dv, v_acc, v_send, v_recv, v_gh, v_p0, v_p1, v_p2, v_p3,
        v_sums, v_swap, *nets,
    ) = refs[15 + nout : 15 + nout + 29] + tuple(refs[15 + nout + 29 :])
    swsem, lsem = nets[-2:]
    pos = Place()
    c = pos.c
    mine = c * HALF
    theirs = HALF - mine
    loads = {}
    for i, (src, dst) in enumerate(
        ((h_upsT, v_upsT), (h_act, v_act), (h_ups, v_ups), (h_down, v_down), (h_slope, v_slope), (h_n2T, v_n2T), (h_up, v_up),
         (h_mid, v_mid), (h_heads, v_heads), (h_ctx, v_ctx), (h_qkv, v_qkv), (h_lse, v_lse), (h_nrmT, v_nrmT))
    ):
        cp = pltpu.make_async_copy(src, dst, lsem.at[i])
        cp.start()
        loads[id(dst)] = cp
    loaded = lambda *which: [loads[id(w)].wait() for w in which]
    entry_barrier(pos, net)
    if net:
        r2_0, rz_0, r2_1, rz_1, r2_2, rz_2, r2_3, rz_3, ssem, rsem = nets[:-2]
        s0 = Reduce(pos, 0, v_p0, r2_0, rz_0, ssem, rsem)
        s1 = Reduce(pos, 1, v_p1, r2_1, rz_1, ssem, rsem)
        s2 = Reduce(pos, 2, v_p2, r2_2, rz_2, ssem, rsem)
        s3 = Reduce(pos, 3, v_p3, r2_3, rz_3, ssem, rsem)

    def tile_of(tile):
        return lax.div(tile, 3), pl.ds(pl.multiple_of(lax.rem(tile, 3) * 256, 256), 256)

    loaded(v_upsT, v_act)

    @pl.loop(0, 6)
    def _(tile):
        b, cols = tile_of(tile)
        res = mm(v_upsT[...], v_act[b, :, cols])
        v_p3[b, :, :, cols] = res.astype(BF16).reshape(NB, RB, 256)

    if net:
        s3.start()
    loaded(v_ups, v_down, v_slope, v_n2T)

    @pl.loop(0, 6)
    def _(tile):
        b, cols = tile_of(tile)
        res = mm(v_ups[...], v_down[b, :, :, cols].reshape(D, 256))
        pre = (res * v_slope[b, :, cols].astype(F32)).astype(BF16)
        v_slope[b, :, cols] = pre
        res = mm(v_n2T[...], pre)
        v_p2[b, :, :, cols] = res.astype(BF16).reshape(NB, RB, 256)

    if net:
        s3.middle()
        s2.start()
    loaded(v_up, v_mid)
    for half, start in enumerate((theirs, mine)):
        res = mm(v_slope[0, rows(start, HALF), :], v_up[0].reshape(D, D), NT)
        res += mm(v_slope[1, rows(start, HALF), :], v_up[1].reshape(D, D), NT)
        if half == 0:
            v_send[0] = res.astype(BF16)
            swap(pos, v_send.at[0], v_recv.at[0], swsem, 0).start()
        else:
            v_acc[...] = res
    swap(pos, v_send.at[0], v_recv.at[0], swsem, 0).wait()
    v_sums[...] = jnp.zeros_like(v_sums)

    def norm_back(upper, values, gain, at):
        hat, inv = norm_stats(values)
        scaled = upper * gain
        first = jnp.mean(scaled, -1, keepdims=True)
        second = jnp.mean(scaled * hat, -1, keepdims=True)
        v_sums[at : at + 1, :] += jnp.sum(upper * hat, 0, keepdims=True)
        v_sums[at + 1 : at + 2, :] += jnp.sum(upper, 0, keepdims=True)
        return inv * (scaled - first - hat * second)

    @pl.loop(0, HALF // 64)
    def _(i):
        r = rows(i * 64, 64)
        upper = v_acc[r, :] + v_recv[0, r, :].astype(F32)
        wide = rows(mine + i * 64, 64)
        d_mid = v_ups[wide, :].astype(F32) + norm_back(upper, v_mid[r, :], param[2:3, :], 2)
        v_dmid[r, :] = d_mid
        v_low[wide, :] = d_mid.astype(BF16)

    swap(pos, v_low.at[rows(mine, HALF)], v_low.at[rows(mine, HALF)], swsem, 1).start()
    if net:
        s3.line()
    loaded(v_heads, v_ctx)
    w_out = cat_pairs(v_heads, (3,), lambda ref, a, b: ref[a, b])
    for half, start in enumerate((mine, theirs)):
        if half == 1:
            swap(pos, v_low.at[rows(theirs, HALF)], v_low.at[rows(theirs, HALF)], swsem, 1).wait_recv()
        res = mm(v_low[rows(start, HALF), :], w_out).astype(BF16)
        for pair in range(3):
            v_dctx[pair, rows(start, HALF), :] = res[:, 128 * pair : 128 * pair + 128]
    transpose_rows(v_low, v_upsT)
    res = mm(v_upsT[...], jnp.concatenate([v_ctx[pair] for pair in range(3)], axis=1)).astype(BF16)
    for pair in range(3):
        v_gh[3, pair] = res[:, 128 * pair : 128 * pair + 128]
    if net:
        s3.finish(o3)
        s2.middle()
    loaded(v_qkv, v_lse, v_nrmT)

    @pl.loop(0, 3)
    def _(pair):
        if net:

            @pl.when(pair == 1)
            def _():
                s2.line()

            @pl.when(pair == 2)
            def _():
                s2.finish(o2)

        v_dk[...] = jnp.zeros_like(v_dk)
        v_dv[...] = jnp.zeros_like(v_dv)
        for i in range(4):
            n = 256 * (i + 1)
            q = v_qkv[pair, 256 * i : n, :]
            up = v_dctx[pair, 256 * i : n, :]
            qs = [only(q, h) for h in range(2)]
            ups = [only(up, h) for h in range(2)]
            dq = jnp.zeros((256, 128), F32)
            probs = [[], []]
            grads = [[], []]
            for h in range(2):
                lse = v_lse[pair, h : h + 1, 256 * i : n]
                delta = jnp.zeros((1, 256), F32)
                for j in range(i + 1):
                    at = slice(256 * j, 256 * j + 256)
                    s = mm(v_qkv[3 + pair, at, :], qs[h], NT)
                    p = jnp.exp(s - lse)
                    if j == i:
                        key = lax.broadcasted_iota(jnp.int32, s.shape, 0)
                        query = lax.broadcasted_iota(jnp.int32, s.shape, 1)
                        p = jnp.where(key <= query, p, 0.0)
                    dp = mm(v_qkv[6 + pair, at, :], ups[h], NT)
                    delta += jnp.sum(p * dp, 0, keepdims=True)
                    probs[h].append(p)
                    grads[h].append(dp)
                for j in range(i + 1):
                    grads[h][j] = (probs[h][j] * (grads[h][j] - delta)).astype(BF16)
                    probs[h][j] = probs[h][j].astype(BF16)
            for j in range(i + 1):
                at = slice(256 * j, 256 * j + 256)
                for h in range(2):
                    k = only(v_qkv[3 + pair, at, :], h)
                    dq += mm(grads[h][j], k, TN)
                v_dv[at, :] += mm(
                    jnp.concatenate([probs[0][j], probs[1][j]], axis=1), jnp.concatenate(ups, axis=0)
                )
                v_dk[at, :] += mm(
                    jnp.concatenate([grads[0][j], grads[1][j]], axis=1), jnp.concatenate(qs, axis=0)
                )
            v_dqkv[pair, 256 * i : n, :] = (dq * HEAD_DIM**-0.5).astype(BF16)
        v_dqkv[3 + pair] = v_dk[...].astype(BF16)
        v_dqkv[6 + pair] = v_dv[...].astype(BF16)

    for part in range(3):
        res = mm(v_nrmT[...], jnp.concatenate([v_dqkv[3 * part + pair] for pair in range(3)], axis=1)).astype(BF16)
        for pair in range(3):
            v_gh[part, pair] = res[:, 128 * pair : 128 * pair + 128]
    pack_heads(v_gh, v_p1)
    if net:
        s1.start()
    w_qkv = cat_pairs(v_heads, (0, 1, 2), lambda ref, a, b: ref[a, b])
    for half, start in enumerate((theirs, mine)):
        lhs = jnp.concatenate([v_dqkv[j, rows(start, HALF), :] for j in range(9)], axis=1)
        res = mm(lhs, w_qkv, NT)
        if half == 0:
            v_send[1] = res.astype(BF16)
            swap(pos, v_send.at[1], v_recv.at[1], swsem, 2).start()
        else:
            v_acc[...] = res
    swap(pos, v_send.at[1], v_recv.at[1], swsem, 2).wait()

    @pl.loop(0, HALF // 64)
    def _(i):
        r = rows(i * 64, 64)
        upper = v_acc[r, :] + v_recv[1, r, :].astype(F32)
        o_in[r, :] = v_dmid[r, :] + norm_back(upper, hid[r, :].astype(F32), param[0:1, :], 0)

    v_swap[0] = v_sums[...]
    swap(pos, v_swap.at[0], v_swap.at[1], swsem, 3).start()
    if net:
        s1.middle()
    swap(pos, v_swap.at[0], v_swap.at[1], swsem, 3).wait()
    both = v_swap[0] + v_swap[1]
    if net:
        for dd in range(NB):
            piece = jnp.concatenate([both[:, RB * dd : RB * dd + RB], jnp.zeros((8, 128 - RB), F32)], axis=1)
            v_p0[0, dd] = piece
            v_p0[1, dd] = piece
        s0.start()
        s0.middle()
        s1.line()
        s0.line()
        s1.finish(o1)
        s0.finish(o_small)
        for s in (s0, s1, s2, s3):
            s.drain()
    else:
        o_small[...] = both
        o1[...] = v_p1[...]
        o2[...] = v_p2[...]
        o3[...] = v_p3[...]
    swap(pos, v_low.at[rows(mine, HALF)], v_low.at[rows(mine, HALF)], swsem, 1).wait_send()


def pack_rows(block):
    third = block[:, :, 128:].reshape(4, 2, 48, 64).transpose(0, 2, 1, 3).reshape(4, 48, 128)
    return jnp.concatenate([block[:, :, :128], third], axis=1)


def unpack_rows(packed):
    third = packed[:, 96:].reshape(4, 48, 2, 64).transpose(0, 2, 1, 3).reshape(4, 96, 64)
    return jnp.concatenate([packed[:, :96], third], axis=2)


def shards(
    hidden_in, cotangent, group_ids, weight_table, table_index, qkv_weight, out_weight, up_weight, down_weight,
    norm1_gain, norm1_bias, norm2_gain, norm2_bias,
):
    n_dp, n_t = lax.axis_size("dp"), lax.axis_size("tensor")
    net = n_dp == NB and n_t == 4
    t = lax.axis_index("tensor")
    core = lax.rem(t, 2)
    tokens = hidden_in.shape[0] * n_dp * n_t
    scale_tokens = tokens / GROUPS
    heads = jnp.concatenate([qkv_weight.transpose(1, 0, 2), out_weight.T[None]], axis=0)
    vectors = jnp.stack([norm1_gain, norm1_bias, norm2_gain, norm2_bias]).astype(F32)
    ids = group_ids.reshape(HALF, 1)
    down = down_weight.T
    if net:
        own = (pack_rows(heads), up_weight, down)
        small = jnp.pad(vectors, ((0, 4), (0, 128 - RB)))
        table = jnp.pad(table_index[None, :], ((0, 7), (0, 128 - GROUPS)), constant_values=-1)
        weights = weight_table
        weight_spec = pl.BlockSpec(memory_space=pltpu.SMEM)
        own_spec = pl.BlockSpec(memory_space=pltpu.VMEM)
    else:

        def whole(block, axis):
            full = lax.all_gather(block, "dp", axis=axis, tiled=True)
            every = lax.all_gather(full, "tensor", axis=0)
            pair = lax.dynamic_index_in_dim(every.reshape((n_t // 2, 2) + full.shape), core, 1, keepdims=False)
            return pair

        heads_all = whole(heads, 1).reshape(2, 4, NB, RB, 192).transpose(0, 2, 1, 3, 4)
        own = (
            jax.vmap(jax.vmap(pack_rows))(heads_all),
            whole(up_weight, 0).reshape(2, NB, RB, D),
            whole(down, 0).reshape(2, NB, RB, D),
        )
        small = jnp.pad(lax.all_gather(vectors, "dp", axis=1, tiled=True), ((0, 4), (0, 0)))
        member = (group_ids[:, None] == jnp.arange(GROUPS, dtype=jnp.int32)[None, :]).astype(F32)
        counts = lax.psum(jnp.sum(member, 0), ("dp", "tensor"))
        hits = table_index[:, None] == jnp.arange(TABLE, dtype=jnp.int32)[None, :]
        scale = jnp.sum(jnp.where(hits, weight_table[None, :], 0.0), 1) * scale_tokens / jnp.maximum(counts, 1.0)
        weights = jnp.pad(scale[None, :], ((0, 7), (0, 128 - GROUPS)))
        table = jnp.pad(counts.astype(jnp.int32)[None, :], ((0, 7), (0, 128 - GROUPS)))
        weight_spec = pl.BlockSpec(memory_space=pltpu.VMEM)
        own_spec = pl.BlockSpec(memory_space=pl.ANY)

    def sds(shape, dtype=BF16):
        return jax.ShapeDtypeStruct(shape, dtype)

    vspec = pl.BlockSpec(memory_space=pltpu.VMEM)
    aspec = pl.BlockSpec(memory_space=pl.ANY)
    saved = [
        sds((HALF, D), F32), sds((8, 128), F32), sds((8, D), F32), sds((HALF, D), F32), sds((4, 3, D, 128)),
        sds((2, NB, RB, D)), sds((2, NB, RB, D)), sds((D, LENGTH)), sds((9, LENGTH, 128)), sds((3, 8, LENGTH), F32),
        sds((3, LENGTH, 128)), sds((D, LENGTH)), sds((2, LENGTH, D)), sds((2, LENGTH, D)), sds((LENGTH, D)), sds((D, LENGTH)),
    ]
    vm = pltpu.VMEM
    dma = pltpu.SemaphoreType.DMA
    outs = pl.pallas_call(
        functools.partial(forward_kernel, net, scale_tokens),
        out_shape=saved,
        in_specs=[vspec, vspec, vspec, vspec, weight_spec, vspec, own_spec, own_spec, own_spec],
        out_specs=[aspec] * len(saved),
        scratch_shapes=[
            vm((2, NB, 8, 128), F32), vm((2, NB, 4, HEADROWS, 128), BF16), vm((2, NB, RB, D), BF16), vm((2, NB, RB, D), BF16),
            vm((4, 3, D, 128), BF16), vm((8, D), F32), vm((8, 128), F32), vm((3, 8, 128), F32),
            vm((LENGTH, D), BF16), vm((D, LENGTH), BF16), vm((9, LENGTH, 128), BF16), vm((3, 8, LENGTH), F32), vm((3, LENGTH, 128), BF16),
            vm((HALF, D), F32), vm((LENGTH, D), BF16), vm((D, LENGTH), BF16), vm((2, LENGTH, D), BF16), vm((2, LENGTH, D), BF16),
            vm((LENGTH, D), BF16), vm((D, LENGTH), BF16), vm((2, HALF, D), BF16), vm((2, HALF, D), BF16), vm((HALF, D), F32), vm((HALF, D), F32),
            dma((4, 5, 4)), dma((4, 2, NB)), dma((2, 6)), dma((19,)),
        ],
        compiler_params=pltpu.CompilerParams(collective_id=0, has_side_effects=True, vmem_limit_bytes=VMEM_LIMIT),
        name="block_forward",
    )(hidden_in, cotangent, ids, table, weights, small, *own)
    (block_output, counts_out, param, mid, heads_w, up_w, down_w, nrmT, qkv, lse, ctx, n2T, act, slope, ups, upsT) = outs

    slot = [(8, 128), (4, HEADROWS, 128), (RB, D), (RB, D)]
    kind = [F32, BF16, BF16, BF16]
    net_scratch = []
    if net:
        for s, k in zip(slot, kind):
            net_scratch += [vm((2, 4) + s, k), vm((3, 4) + s, k)]
        net_scratch += [dma((4, 5, 4)), dma((4, 5, 4))]
        grad_shapes = [sds(s, F32) for s in slot]
    else:
        grad_shapes = [sds((8, D), F32)] + [sds((2, NB) + s) for s in slot[1:]]
    out2 = pl.pallas_call(
        functools.partial(backward_kernel, net),
        out_shape=[sds((HALF, D), F32)] + grad_shapes,
        in_specs=[vspec, vspec] + [aspec] * 13,
        out_specs=[vspec] * 5,
        scratch_shapes=[
            vm((HALF, D), F32), vm((4, 3, D, 128), BF16), vm((2, NB, RB, D), BF16), vm((2, NB, RB, D), BF16), vm((D, LENGTH), BF16),
            vm((9, LENGTH, 128), BF16), vm((3, 8, LENGTH), F32), vm((3, LENGTH, 128), BF16), vm((D, LENGTH), BF16),
            vm((2, LENGTH, D), BF16), vm((2, LENGTH, D), BF16), vm((LENGTH, D), BF16), vm((D, LENGTH), BF16),
            vm((LENGTH, D), BF16), vm((HALF, D), F32), vm((3, LENGTH, 128), BF16), vm((9, LENGTH, 128), BF16),
            vm((LENGTH, 128), F32), vm((LENGTH, 128), F32), vm((HALF, D), F32), vm((2, HALF, D), BF16), vm((2, HALF, D), BF16),
            vm((4, 3, D, 128), BF16), vm((2, NB, 8, 128), F32), vm((2, NB, 4, HEADROWS, 128), BF16), vm((2, NB, RB, D), BF16), vm((2, NB, RB, D), BF16),
            vm((8, D), F32), vm((2, 8, D), F32),
            *net_scratch, dma((2, 4)), dma((13,)),
        ],
        compiler_params=pltpu.CompilerParams(collective_id=1, has_side_effects=True, vmem_limit_bytes=VMEM_LIMIT),
        name="block_backward",
    )(hidden_in, param, mid, heads_w, up_w, down_w, nrmT, qkv, lse, ctx, n2T, act, slope, ups, upsT)
    input_grad, sums, g1, g2, g3 = out2
    if net:
        piece = lax.dynamic_slice_in_dim(sums[:4], t * 24, 24, 1)
        norms = [piece[0], piece[1], piece[2], piece[3]]
        grad_heads, grad_up, grad_down = unpack_rows(g1), g2, g3
    else:

        def owned(part):
            base = jnp.zeros((n_t // 2, 2) + part.shape[1:], F32)
            base = lax.dynamic_update_index_in_dim(base, part.astype(F32), core, 1)
            flat = base.reshape((n_t,) + part.shape[1:])
            mine = lax.psum_scatter(flat, "tensor", scatter_dimension=0, tiled=False)
            return lax.psum_scatter(mine, "dp", scatter_dimension=0, tiled=True)

        gh = jax.vmap(jax.vmap(unpack_rows))(g1)
        gh = gh.transpose(0, 1, 3, 2, 4).reshape(2, D, 4, 192)
        grad_heads = owned(gh).transpose(1, 0, 2)
        grad_up, grad_down = owned(g2.reshape(2, D, D)), owned(g3.reshape(2, D, D))
        half_sums = jnp.where(core == 0, sums, 0.0)
        norms = [
            lax.psum_scatter(half_sums[i], ("dp", "tensor"), scatter_dimension=0, tiled=True) for i in range(4)
        ]
    return (
        block_output,
        input_grad,
        grad_heads[:3].transpose(1, 0, 2),
        grad_heads[3].T,
        grad_up,
        grad_down.T,
        norms[0],
        norms[1],
        norms[2],
        norms[3],
        counts_out[0, :GROUPS],
    )


def solution(mesh):
    both = ("dp", "tensor")
    return jax.shard_map(
        shards,
        mesh=mesh,
        in_specs=(
            P(both, None), P(both, None), P(both), P(), P(), P("dp", None, "tensor"), P("tensor", "dp"), P("dp", "tensor"),
            P("tensor", "dp"), P("dp"), P("dp"), P("dp"), P("dp"),
        ),
        out_specs=(
            P(both, None), P(both, None), P("dp", None, "tensor"), P("tensor", "dp"), P("dp", "tensor"), P("tensor", "dp"),
            P(both), P(both), P(both), P(both), P(),
        ),
        check_vma=False,
    )
```

time: 859 us -> 234 us (0.27)
  waiting for transfers between devices: 395 us -> 0 us
  Pallas kernels: 0 us -> 214 us
  blocking collectives: 171 us -> 0 us
  matrix products: 134 us -> 0 us
  local copies, waits for them, and re-layouts: 75.7 us -> 13.8 us
  other arithmetic: 38.5 us -> 4.54 us
  loops' own time: 21.1 us -> 0 us
  between operations: 17 us -> 0.73 us
    reduce_scatter x7 -> x0, waiting for transfers between devices: 287 us -> none  [the longest x1 72.7 us: shards(): lax.psum_scatter(grad_down, 'dp', scatter_dimension=1, tiled=True)]
    pallas_call x0 -> x2, Pallas kernels: none -> 214 us  [the longest x1 135 us: shards(): pl.pallas_call(functools.partial(backward_kernel, net), out_shape=[sds((H...]
    dot_general x39 -> x0, matrix products: 129 us -> none  [the longest x8 16.2 us: causal_scores(): jnp.einsum('qhd,khd->hqk', query_block, key_block, preferred_element_type...]
    all_gather x6 -> x0, waiting for transfers between devices: 107 us -> none  [the longest x1 36.1 us: shards(): lax.all_gather(up_weight, 'dp', axis=0, tiled=True)]
    all_gather x2 -> x0, blocking collectives: 66.5 us -> none  [the longest x1 35.2 us: shards(): lax.all_gather(qkv_weight, 'dp', axis=0, tiled=True)]
    unnamed x2 -> x0, blocking collectives: 64.8 us -> none
    psum x1 -> x0, blocking collectives: 39.4 us -> none  [shards(): group_counts = lax.psum(jnp.sum(member, 0), ('dp', 'tensor'))]
    dynamic_update_slice x8 -> x0, local copies, waits for them, and re-layouts: 33.2 us -> none  [shards(): lax.map(attend_back, (queries, d_context, log_totals, block_ids))]
  transfers between devices with their start and end apart: 14 -> 0, of which waited for: 11 -> 0; matrix products, arithmetic and copies ran while one was open for 18% -> 0% of each run, Pallas kernels for 0% -> 0%
where the time goes in v1:
time: 234 us; the launch traced here: 233 us
  Pallas kernels  214 us (91%)
  local copies, waits for them, and re-layouts  13.8 us (6%)
  other arithmetic  4.54 us (2%)
    pallas_call x1, Pallas kernels, shards(): pl.pallas_call(functools.partial(backward_kernel, net), out_shape=[sds((H...  135 us
    pallas_call x1, Pallas kernels, shards(): pl.pallas_call(functools.partial(forward_kernel, net, scale_tokens), out_...  78.7 us
    unnamed x14, local copies, waits for them, and re-layouts  6.18 us

profile of v1, /device:TPU:0, one launch (start us, length us, event | category | flops | bytes accessed | tf_op | source)
XLA Modules:
  0.0 233.2 jit_solution(877355561038522781)
XLA Ops:
  0.6 1.3 pad.10.refs_3_
  1.9 1.3 fusion.13.refs_5_
  3.2 0.9 copy.28
  4.1 0.9 pad_maximum_fusion.2
  5.0 0.1 copy.34
  5.1 0.1 reshape.39
  5.2 0.9 fusion.2
  6.1 0.7 pad_maximum_fusion.refs_6_
  6.8 1.5 copy.30.refs_2_
  8.3 78.7 %block_forward.1 = (f32[512,768]{1,0:T(8,128)}, f32[8,128]{1,0:T(8,128)}, f32[8,768]{1,0:T(8,128)}, f32[512,768]{1,0:T(8,128)}, bf16[4,3,768,128]{3,2,1,0:T(8,12...) custom-call(bf16[512,768]{1,0:T(8,128)(2,1)} %refs_0_.3, ...), custom_call_target="tpu_custom_call" | custom-call | tf_op jit(solution)/shard_map/block_forward/pallas_call | solution.py:892
  87.1 1.2 slice_bitcast_fusion
  88.2 135.5 %block_backward.1 = (f32[512,768]{1,0:T(8,128)}, f32[8,128]{1,0:T(8,128)}, f32[4,144,128]{2,1,0:T(8,128)}, f32[96,768]{1,0:T(8,128)}, f32[96,768]{1,0:T(8,128)}) custom-call(bf16[512,768]{1,0:T(8,128)(2,1)} %refs_0_.3, f32[8,768]{1,0:T(8,128)} %get-tuple-element.33.refs_1_, f32[512,768]{1,0:T(8,128)} %get-tuple-element.34.refs_2_, ...), custom_call_target="tpu_custom_call" | custom-call | tf_op jit(solution)/shard_map/block_backward/pallas_call | solution.py:920
  223.7 0.8 slice.42
  224.6 0.5 slice_bitcast_fusion.1
  225.1 0.9 slice.39
  226.0 0.9 slice.38
  227.0 0.2 reshape.40
  227.2 0.7 fusion.1
  227.9 0.7 copy.32
  228.7 1.1 copy.39
  229.8 0.8 copy-done.1
  230.6 1.1 copy.40
  231.8 0.7 copy.41
  232.5 0.7 copy.42
  (10 shorter events, 0.1 us)
Async XLA Ops:
  223.7 4.9 %copy-start = (f32[512,768]{1,0:T(8,128)S(1)}, f32[512,768]{1,0:T(8,128)}, u32[]{:S(2)}) copy-start(f32[512,768]{1,0:T(8,128)} %get-tuple-element.90) | copy-start | bytes 4718596
  228.7 2.0 copy-start.1
  230.6 1.1 copy-start.3
  230.6 1.9 copy-start.2

commit v2 on v1

--- a/solution.py
+++ b/solution.py
@@ -225,21 +225,27 @@
             for zz in range(4):
                 self.to_p2(which, zz).start()
 
-    def middle(self):
+    def mid1(self):
         p = self.pos
         for zz in range(4):
             self.to_p2(1, zz).wait_recv()
             self.add(p.x1, 2 * zz + p.y1, self.r2[1, zz])
             self.to_p1(zz).start()
+
+    def mid0(self):
+        p = self.pos
         for zz in range(4):
             self.to_p2(0, zz).wait_recv()
             self.add(p.x, 2 * zz + p.y, self.r2[0, zz])
 
-    def line(self):
+    def join(self):
         p = self.pos
         for zz in range(4):
             self.to_p1(zz).wait_recv()
             self.add(p.x, 2 * zz + p.y, self.rz[0, zz])
+
+    def chain(self):
+        p = self.pos
         for zz in (3, 2, 1):
 
             @pl.when(zz > p.z)
@@ -363,21 +369,22 @@
         dst[:, r] = src[r, :].T
 
 
-def forward_kernel(net, scale_tokens, *refs):
-    (hid, cot, ids, table, weights, small, own1, own2, own3) = refs[:9]
+def forward_kernel(net, scale_tokens, nin, *refs):
+    hid, cot, ids, table, weights, *given = refs[:nin]
+    refs = refs[nin - 9 :]
     (o_block, o_counts, o_param, o_mid, o_heads, o_up, o_down, o_nrmT, o_qkv, o_lse, o_ctx, o_n2T, o_act, o_slope, o_ups, o_upsT) = refs[9:25]
     (
         v_small, v_raw, v_up, v_down, v_heads, v_param, v_counts, v_cnt, v_nrm, v_nrmT, v_qkv, v_lse, v_ctx,
-        v_mid, v_n2, v_n2T, v_act, v_slope, v_ups, v_upsT, v_send, v_recv, v_acc, v_block,
+        v_mid, v_n2, v_n2T, v_act, v_slope, v_ups, v_upsT, v_send, v_recv, v_acc, v_block, own1,
         ssem, rsem, swsem, osem,
     ) = refs[25:]
     pos = Place()
     c = pos.c
     mine = c * HALF
     theirs = HALF - mine
-    entry_barrier(pos, net)
     lanes = lax.broadcasted_iota(jnp.int32, (HALF, 128), 1)
-    member = ids[...] == lanes
+    row_ids = jnp.broadcast_to(ids[...].astype(F32), (128, HALF)).T
+    member = row_ids == lanes.astype(F32)
     own_counts = jnp.sum(member.astype(F32), 0, keepdims=True)
 
     puts = []
@@ -388,8 +395,16 @@
         puts.append(cp)
 
     if net:
-        v_cnt[2] = small[...]
+        qkv_w, out_w, own2, own3, *vectors = given
+        v_cnt[2] = jnp.zeros((8, 128), F32)
+        for i in range(4):
+            v_cnt[2, i : i + 1, 0:RB] = vectors[i][...].astype(F32)
         v_cnt[2, 4:5, :] = own_counts
+        for part in range(4):
+            block = qkv_w[part] if part < 3 else out_w[...].T
+            own1[part, 0:RB] = block[:, 0:128]
+            own1[part, RB:HEADROWS] = jnp.concatenate([block[0:48, 128:192], block[48:96, 128:192]], axis=1)
+        entry_barrier(pos, net)
         g0 = Gather(pos, 0, v_cnt.at[2], v_small, ssem, rsem)
         g1 = Gather(pos, 1, own1, v_raw, ssem, rsem)
         g2 = Gather(pos, 2, own2, v_up, ssem, rsem)
@@ -400,11 +415,13 @@
         v_raw[pos.x, pos.d] = own1[...]
         v_up[pos.x, pos.d] = own2[...]
         v_down[pos.x, pos.d] = own3[...]
-        for k in (1, 2, 3, 4):
+        for k in (1, 2, 3):
             g0.step(k)
             g1.step(k)
+        g2.step(0)
+        g0.step(4)
+        g1.step(4)
         g0.finish()
-        g2.step(0)
         v_param[...] = jnp.zeros_like(v_param)
         total = jnp.zeros((8, 128), F32)
         for dd in range(NB):
@@ -417,12 +434,13 @@
         v_cnt[0] = total
         swap(pos, v_cnt.at[0], v_cnt.at[1], swsem, 0).start()
     else:
+        small, in1, in2, in3 = given
+        entry_barrier(pos, net)
         v_param[...] = small[...]
-        v_cnt[0] = jnp.broadcast_to(own_counts, (8, 128))
         cps = [
-            pltpu.make_async_copy(own1, v_raw, osem.at[16]),
-            pltpu.make_async_copy(own2, v_up, osem.at[17]),
-            pltpu.make_async_copy(own3, v_down, osem.at[18]),
+            pltpu.make_async_copy(in1, v_raw, osem.at[16]),
+            pltpu.make_async_copy(in2, v_up, osem.at[17]),
+            pltpu.make_async_copy(in3, v_down, osem.at[18]),
         ]
         for cp in cps:
             cp.start()
@@ -442,14 +460,16 @@
     if net:
         swap(pos, v_cnt.at[0], v_cnt.at[1], swsem, 0).wait()
         counts = (v_cnt[0] + v_cnt[1])[4:5, :]
-        v_counts[...] = jnp.broadcast_to(counts, (8, 128))
-        index = table[0:1, :]
+        v_counts[...] = jnp.full(v_counts.shape, -1, jnp.int32)
+        v_counts[0:1, 0:GROUPS] = table[...]
+        index = v_counts[0:1, :]
         weight = jnp.zeros((1, 128), F32)
         for r in range(TABLE):
             weight = weight + jnp.where(index == r, weights[r], 0.0)
         group_scale = weight * scale_tokens / jnp.maximum(counts, 1.0)
+        o_counts[...] = counts[:, 0:GROUPS]
     else:
-        v_counts[...] = table[...].astype(F32)
+        o_counts[...] = table[...]
         group_scale = weights[0:1, :]
 
     row_scale = jnp.sum(jnp.where(member, group_scale, 0.0), 1, keepdims=True)
@@ -458,14 +478,13 @@
     swap_ups.start()
 
     if net:
+        g2.step(1)
+        g2.step(2)
         g1.finish()
     unpack_heads(v_raw, v_heads)
     put(v_heads, o_heads)
     put(v_param, o_param)
-    put(v_counts, o_counts)
-
-    if net:
-        g2.step(1)
+
     for half, start in enumerate((mine, theirs)):
         if half == 1:
             swap(pos, v_nrm.at[rows(theirs, HALF)], v_nrm.at[rows(theirs, HALF)], swsem, 1).wait_recv()
@@ -479,7 +498,8 @@
                 v_qkv[3 * part + pair, rows(start, HALF), :] = res[:, 128 * pair : 128 * pair + 128]
     put(v_qkv, o_qkv)
     if net:
-        g2.step(2)
+        g2.step(3)
+        g3.step(0)
 
     @pl.loop(0, 3)
     def _(pair):
@@ -487,12 +507,12 @@
 
             @pl.when(pair == 1)
             def _():
-                g2.step(3)
+                g2.step(4)
+                g3.step(1)
 
             @pl.when(pair == 2)
             def _():
-                g2.step(4)
-                g3.step(0)
+                g3.step(2)
 
         for i in range(4):
             n = 256 * (i + 1)
@@ -526,7 +546,7 @@
     put(v_lse, o_lse)
     put(v_ctx, o_ctx)
     if net:
-        g3.step(1)
+        g3.step(3)
 
     w_out = cat_pairs(v_heads, (3,), lambda ref, a, b: ref[a, b])
     for half, start in enumerate((theirs, mine)):
@@ -537,8 +557,6 @@
             swap(pos, v_send.at[0], v_recv.at[0], swsem, 3).start()
         else:
             v_acc[...] = res
-    if net:
-        g3.step(2)
     transpose_rows(v_nrm, v_nrmT)
     put(v_nrmT, o_nrmT)
     swap(pos, v_send.at[0], v_recv.at[0], swsem, 3).wait()
@@ -554,8 +572,8 @@
     swap(pos, v_n2.at[rows(mine, HALF)], v_n2.at[rows(mine, HALF)], swsem, 4).start()
     put(v_mid, o_mid)
     if net:
+        g3.step(4)
         g2.finish()
-        g3.step(3)
     put(v_up, o_up)
 
     for half, start in enumerate((mine, theirs)):
@@ -572,9 +590,6 @@
             v_act[b, rows(start, HALF), cols] = (0.5 * pre * (1.0 + bend)).astype(BF16)
             slope = 0.5 * (1.0 + bend) + 0.5 * pre * (1.0 - bend * bend) * (GELU_C * (1.0 + 3.0 * GELU_A * square))
             v_slope[b, rows(start, HALF), cols] = slope.astype(BF16)
-
-        if net and half == 0:
-            g3.step(4)
 
     put(v_act, o_act)
     put(v_slope, o_slope)
@@ -609,13 +624,13 @@
 
 def backward_kernel(net, *refs):
     (hid, param, h_mid, h_heads, h_up, h_down, h_nrmT, h_qkv, h_lse, h_ctx, h_n2T, h_act, h_slope, h_ups, h_upsT) = refs[:15]
-    nout = 5
-    o_in, o_small, o1, o2, o3 = refs[15 : 15 + nout]
+    nout = 6
+    o_in, o_small, o1, o_out, o2, o3 = refs[15 : 15 + nout]
     (
         v_mid, v_heads, v_up, v_down, v_nrmT, v_qkv, v_lse, v_ctx, v_n2T, v_act, v_slope, v_ups, v_upsT,
         v_low, v_dmid, v_dctx, v_dqkv, v_dk, v_dv, v_acc, v_send, v_recv, v_gh, v_p0, v_p1, v_p2, v_p3,
-        v_sums, v_swap, *nets,
-    ) = refs[15 + nout : 15 + nout + 29] + tuple(refs[15 + nout + 29 :])
+        v_sums, v_swap, v_own, *nets,
+    ) = refs[15 + nout :]
     swsem, lsem = nets[-2:]
     pos = Place()
     c = pos.c
@@ -663,7 +678,6 @@
         v_p2[b, :, :, cols] = res.astype(BF16).reshape(NB, RB, 256)
 
     if net:
-        s3.middle()
         s2.start()
     loaded(v_up, v_mid)
     for half, start in enumerate((theirs, mine)):
@@ -674,6 +688,8 @@
             swap(pos, v_send.at[0], v_recv.at[0], swsem, 0).start()
         else:
             v_acc[...] = res
+    if net:
+        s3.mid1()
     swap(pos, v_send.at[0], v_recv.at[0], swsem, 0).wait()
     v_sums[...] = jnp.zeros_like(v_sums)
 
@@ -696,8 +712,6 @@
         v_low[wide, :] = d_mid.astype(BF16)
 
     swap(pos, v_low.at[rows(mine, HALF)], v_low.at[rows(mine, HALF)], swsem, 1).start()
-    if net:
-        s3.line()
     loaded(v_heads, v_ctx)
     w_out = cat_pairs(v_heads, (3,), lambda ref, a, b: ref[a, b])
     for half, start in enumerate((mine, theirs)):
@@ -711,21 +725,17 @@
     for pair in range(3):
         v_gh[3, pair] = res[:, 128 * pair : 128 * pair + 128]
     if net:
-        s3.finish(o3)
-        s2.middle()
+        s3.mid0()
     loaded(v_qkv, v_lse, v_nrmT)
 
     @pl.loop(0, 3)
     def _(pair):
         if net:
 
-            @pl.when(pair == 1)
-            def _():
-                s2.line()
-
             @pl.when(pair == 2)
             def _():
-                s2.finish(o2)
+                s3.join()
+                s2.mid1()
 
         v_dk[...] = jnp.zeros_like(v_dk)
         v_dv[...] = jnp.zeros_like(v_dv)
@@ -787,6 +797,9 @@
             swap(pos, v_send.at[1], v_recv.at[1], swsem, 2).start()
         else:
             v_acc[...] = res
+    if net:
+        s3.chain()
+        s2.mid0()
     swap(pos, v_send.at[1], v_recv.at[1], swsem, 2).wait()
 
     @pl.loop(0, HALF // 64)
@@ -797,8 +810,6 @@
 
     v_swap[0] = v_sums[...]
     swap(pos, v_swap.at[0], v_swap.at[1], swsem, 3).start()
-    if net:
-        s1.middle()
     swap(pos, v_swap.at[0], v_swap.at[1], swsem, 3).wait()
     both = v_swap[0] + v_swap[1]
     if net:
@@ -807,15 +818,34 @@
             v_p0[0, dd] = piece
             v_p0[1, dd] = piece
         s0.start()
-        s0.middle()
-        s1.line()
-        s0.line()
-        s1.finish(o1)
-        s0.finish(o_small)
+        s1.mid1()
+        s2.join()
+        s2.chain()
+        s3.finish(o3)
+        s1.mid0()
+        s0.mid1()
+        s0.mid0()
+        s1.join()
+        s1.chain()
+        s0.join()
+        s0.chain()
+        s2.finish(o2)
+        s1.finish(v_own)
+        s0.finish(v_swap.at[0, :, 0:128])
+        for part in range(4):
+            tail = v_own[part, RB:HEADROWS]
+            block = jnp.concatenate([tail[:, 0:64], tail[:, 64:128]], axis=0)
+            whole_rows = jnp.concatenate([v_own[part, 0:RB], block], axis=1)
+            if part < 3:
+                o1[part] = whole_rows
+            else:
+                o_out[...] = whole_rows.T
+        o_small[...] = pltpu.roll(v_swap[0, :, 0:128], lax.rem(128 - 24 * pos.t, 128), 1)[:, 0:24]
         for s in (s0, s1, s2, s3):
             s.drain()
     else:
         o_small[...] = both
+        o_out[...] = jnp.zeros_like(o_out)
         o1[...] = v_p1[...]
         o2[...] = v_p2[...]
         o3[...] = v_p3[...]
@@ -842,17 +872,16 @@
     core = lax.rem(t, 2)
     tokens = hidden_in.shape[0] * n_dp * n_t
     scale_tokens = tokens / GROUPS
-    heads = jnp.concatenate([qkv_weight.transpose(1, 0, 2), out_weight.T[None]], axis=0)
-    vectors = jnp.stack([norm1_gain, norm1_bias, norm2_gain, norm2_bias]).astype(F32)
-    ids = group_ids.reshape(HALF, 1)
+    ids = group_ids.reshape(1, HALF)
     down = down_weight.T
-    if net:
-        own = (pack_rows(heads), up_weight, down)
-        small = jnp.pad(vectors, ((0, 4), (0, 128 - RB)))
-        table = jnp.pad(table_index[None, :], ((0, 7), (0, 128 - GROUPS)), constant_values=-1)
-        weights = weight_table
+    vspec = pl.BlockSpec(memory_space=pltpu.VMEM)
+    aspec = pl.BlockSpec(memory_space=pl.ANY)
+    if net:
+        vectors = [v.reshape(1, RB) for v in (norm1_gain, norm1_bias, norm2_gain, norm2_bias)]
+        table, weights = table_index.reshape(1, GROUPS), weight_table
+        given = [qkv_weight.transpose(1, 0, 2), out_weight, up_weight, down, *vectors]
         weight_spec = pl.BlockSpec(memory_space=pltpu.SMEM)
-        own_spec = pl.BlockSpec(memory_space=pltpu.VMEM)
+        given_specs = [vspec] * len(given)
     else:
 
         def whole(block, axis):
@@ -861,50 +890,50 @@
             pair = lax.dynamic_index_in_dim(every.reshape((n_t // 2, 2) + full.shape), core, 1, keepdims=False)
             return pair
 
+        heads = jnp.concatenate([qkv_weight.transpose(1, 0, 2), out_weight.T[None]], axis=0)
+        vectors = jnp.stack([norm1_gain, norm1_bias, norm2_gain, norm2_bias]).astype(F32)
         heads_all = whole(heads, 1).reshape(2, 4, NB, RB, 192).transpose(0, 2, 1, 3, 4)
-        own = (
+        given = [
+            jnp.pad(lax.all_gather(vectors, "dp", axis=1, tiled=True), ((0, 4), (0, 0))),
             jax.vmap(jax.vmap(pack_rows))(heads_all),
             whole(up_weight, 0).reshape(2, NB, RB, D),
             whole(down, 0).reshape(2, NB, RB, D),
-        )
-        small = jnp.pad(lax.all_gather(vectors, "dp", axis=1, tiled=True), ((0, 4), (0, 0)))
+        ]
         member = (group_ids[:, None] == jnp.arange(GROUPS, dtype=jnp.int32)[None, :]).astype(F32)
         counts = lax.psum(jnp.sum(member, 0), ("dp", "tensor"))
         hits = table_index[:, None] == jnp.arange(TABLE, dtype=jnp.int32)[None, :]
         scale = jnp.sum(jnp.where(hits, weight_table[None, :], 0.0), 1) * scale_tokens / jnp.maximum(counts, 1.0)
         weights = jnp.pad(scale[None, :], ((0, 7), (0, 128 - GROUPS)))
-        table = jnp.pad(counts.astype(jnp.int32)[None, :], ((0, 7), (0, 128 - GROUPS)))
-        weight_spec = pl.BlockSpec(memory_space=pltpu.VMEM)
-        own_spec = pl.BlockSpec(memory_space=pl.ANY)
+        table = counts.reshape(1, GROUPS)
+        weight_spec = vspec
+        given_specs = [vspec, aspec, aspec, aspec]
 
     def sds(shape, dtype=BF16):
         return jax.ShapeDtypeStruct(shape, dtype)
 
-    vspec = pl.BlockSpec(memory_space=pltpu.VMEM)
-    aspec = pl.BlockSpec(memory_space=pl.ANY)
     saved = [
-        sds((HALF, D), F32), sds((8, 128), F32), sds((8, D), F32), sds((HALF, D), F32), sds((4, 3, D, 128)),
+        sds((HALF, D), F32), sds((1, GROUPS), F32), sds((8, D), F32), sds((HALF, D), F32), sds((4, 3, D, 128)),
         sds((2, NB, RB, D)), sds((2, NB, RB, D)), sds((D, LENGTH)), sds((9, LENGTH, 128)), sds((3, 8, LENGTH), F32),
         sds((3, LENGTH, 128)), sds((D, LENGTH)), sds((2, LENGTH, D)), sds((2, LENGTH, D)), sds((LENGTH, D)), sds((D, LENGTH)),
     ]
     vm = pltpu.VMEM
     dma = pltpu.SemaphoreType.DMA
     outs = pl.pallas_call(
-        functools.partial(forward_kernel, net, scale_tokens),
+        functools.partial(forward_kernel, net, scale_tokens, 5 + len(given)),
         out_shape=saved,
-        in_specs=[vspec, vspec, vspec, vspec, weight_spec, vspec, own_spec, own_spec, own_spec],
-        out_specs=[aspec] * len(saved),
+        in_specs=[vspec, vspec, vspec, vspec, weight_spec, *given_specs],
+        out_specs=[aspec, vspec] + [aspec] * (len(saved) - 2),
         scratch_shapes=[
             vm((2, NB, 8, 128), F32), vm((2, NB, 4, HEADROWS, 128), BF16), vm((2, NB, RB, D), BF16), vm((2, NB, RB, D), BF16),
-            vm((4, 3, D, 128), BF16), vm((8, D), F32), vm((8, 128), F32), vm((3, 8, 128), F32),
+            vm((4, 3, D, 128), BF16), vm((8, D), F32), vm((8, 128), jnp.int32), vm((3, 8, 128), F32),
             vm((LENGTH, D), BF16), vm((D, LENGTH), BF16), vm((9, LENGTH, 128), BF16), vm((3, 8, LENGTH), F32), vm((3, LENGTH, 128), BF16),
             vm((HALF, D), F32), vm((LENGTH, D), BF16), vm((D, LENGTH), BF16), vm((2, LENGTH, D), BF16), vm((2, LENGTH, D), BF16),
-            vm((LENGTH, D), BF16), vm((D, LENGTH), BF16), vm((2, HALF, D), BF16), vm((2, HALF, D), BF16), vm((HALF, D), F32), vm((HALF, D), F32),
+            vm((LENGTH, D), BF16), vm((D, LENGTH), BF16), vm((2, HALF, D), BF16), vm((2, HALF, D), BF16), vm((HALF, D), F32), vm((HALF, D), F32), vm((4, HEADROWS, 128), BF16),
             dma((4, 5, 4)), dma((4, 2, NB)), dma((2, 6)), dma((19,)),
         ],
         compiler_params=pltpu.CompilerParams(collective_id=0, has_side_effects=True, vmem_limit_bytes=VMEM_LIMIT),
         name="block_forward",
-    )(hidden_in, cotangent, ids, table, weights, small, *own)
+    )(hidden_in, cotangent, ids, table, weights, *given)
     (block_output, counts_out, param, mid, heads_w, up_w, down_w, nrmT, qkv, lse, ctx, n2T, act, slope, ups, upsT) = outs
 
     slot = [(8, 128), (4, HEADROWS, 128), (RB, D), (RB, D)]
@@ -914,14 +943,15 @@
         for s, k in zip(slot, kind):
             net_scratch += [vm((2, 4) + s, k), vm((3, 4) + s, k)]
         net_scratch += [dma((4, 5, 4)), dma((4, 5, 4))]
-        grad_shapes = [sds(s, F32) for s in slot]
+        grad_shapes = [sds((8, 24), F32), sds((3, RB, 192), F32), sds((192, RB), F32), sds((RB, D), F32), sds((RB, D), F32)]
     else:
-        grad_shapes = [sds((8, D), F32)] + [sds((2, NB) + s) for s in slot[1:]]
+        slots = [sds((2, NB) + s) for s in slot[1:]]
+        grad_shapes = [sds((8, D), F32), slots[0], sds((8, 128), F32), slots[1], slots[2]]
     out2 = pl.pallas_call(
         functools.partial(backward_kernel, net),
         out_shape=[sds((HALF, D), F32)] + grad_shapes,
         in_specs=[vspec, vspec] + [aspec] * 13,
-        out_specs=[vspec] * 5,
+        out_specs=[vspec] * 6,
         scratch_shapes=[
             vm((HALF, D), F32), vm((4, 3, D, 128), BF16), vm((2, NB, RB, D), BF16), vm((2, NB, RB, D), BF16), vm((D, LENGTH), BF16),
             vm((9, LENGTH, 128), BF16), vm((3, 8, LENGTH), F32), vm((3, LENGTH, 128), BF16), vm((D, LENGTH), BF16),
@@ -929,17 +959,16 @@
             vm((LENGTH, D), BF16), vm((HALF, D), F32), vm((3, LENGTH, 128), BF16), vm((9, LENGTH, 128), BF16),
             vm((LENGTH, 128), F32), vm((LENGTH, 128), F32), vm((HALF, D), F32), vm((2, HALF, D), BF16), vm((2, HALF, D), BF16),
             vm((4, 3, D, 128), BF16), vm((2, NB, 8, 128), F32), vm((2, NB, 4, HEADROWS, 128), BF16), vm((2, NB, RB, D), BF16), vm((2, NB, RB, D), BF16),
-            vm((8, D), F32), vm((2, 8, D), F32),
+            vm((8, D), F32), vm((2, 8, D), F32), vm((4, HEADROWS, 128), F32),
             *net_scratch, dma((2, 4)), dma((13,)),
         ],
         compiler_params=pltpu.CompilerParams(collective_id=1, has_side_effects=True, vmem_limit_bytes=VMEM_LIMIT),
         name="block_backward",
     )(hidden_in, param, mid, heads_w, up_w, down_w, nrmT, qkv, lse, ctx, n2T, act, slope, ups, upsT)
-    input_grad, sums, g1, g2, g3 = out2
-    if net:
-        piece = lax.dynamic_slice_in_dim(sums[:4], t * 24, 24, 1)
-        norms = [piece[0], piece[1], piece[2], piece[3]]
-        grad_heads, grad_up, grad_down = unpack_rows(g1), g2, g3
+    input_grad, sums, g1, grad_out, g2, g3 = out2
+    if net:
+        norms = [sums[i] for i in range(4)]
+        grad_qkv, grad_up, grad_down = g1, g2, g3
     else:
 
         def owned(part):
@@ -952,6 +981,7 @@
         gh = jax.vmap(jax.vmap(unpack_rows))(g1)
         gh = gh.transpose(0, 1, 3, 2, 4).reshape(2, D, 4, 192)
         grad_heads = owned(gh).transpose(1, 0, 2)
+        grad_qkv, grad_out = grad_heads[:3], grad_heads[3].T
         grad_up, grad_down = owned(g2.reshape(2, D, D)), owned(g3.reshape(2, D, D))
         half_sums = jnp.where(core == 0, sums, 0.0)
         norms = [
@@ -960,15 +990,15 @@
     return (
         block_output,
         input_grad,
-        grad_heads[:3].transpose(1, 0, 2),
-        grad_heads[3].T,
+        grad_qkv.transpose(1, 0, 2),
+        grad_out,
         grad_up,
         grad_down.T,
         norms[0],
         norms[1],
         norms[2],
         norms[3],
-        counts_out[0, :GROUPS],
+        counts_out.reshape(GROUPS),
     )
 
 

time: 234 us -> 193 us (0.82)
  Pallas kernels: 214 us -> 183 us
  local copies, waits for them, and re-layouts: 13.8 us -> 8.59 us
  other arithmetic: 4.54 us -> 0 us
    pallas_call x1, Pallas kernels: 135 us -> 103 us  [shards(): pl.pallas_call(functools.partial(backward_kernel, net), out_shape=[sds((H...]
    slice x3 -> x0, local copies, waits for them, and re-layouts: 2.64 us -> none  [the longest x1 0.94 us: unpack_rows(): return jnp.concatenate([packed[:, :96], third], axis=2)]
    concatenate x3 -> x0, other arithmetic: 2.48 us -> none  [the longest x2 1.81 us: shards(): jnp.concatenate([qkv_weight.transpose(1, 0, 2), out_weight.T[None]], axis=0)]
    unnamed x14 -> x19, local copies, waits for them, and re-layouts: 6.18 us -> 7.23 us
where the time goes in v2:
time: 193 us
  Pallas kernels  183 us (95%)
  local copies, waits for them, and re-layouts  8.59 us (4%)
    pallas_call x1, Pallas kernels, shards(): pl.pallas_call(functools.partial(backward_kernel, net), out_shape=[sds((H...  103 us
    pallas_call x1, Pallas kernels, shards(): pl.pallas_call(functools.partial(forward_kernel, net, scale_tokens, 5 + l...  80.3 us
    unnamed x19, local copies, waits for them, and re-layouts  7.23 us

profile of v2, /device:TPU:0, one launch (start us, length us, event | category | flops | bytes accessed | tf_op | source)
XLA Modules:
  0.0 192.7 jit_solution(6968879063793239835)
XLA Ops:
  0.6 80.3 %block_forward.1 = (f32[512,768]{1,0:T(8,128)}, f32[1,16]{1,0:T(1,128)}, f32[8,768]{1,0:T(8,128)}, f32[512,768]{1,0:T(8,128)}, bf16[4,3,768,128]{3,2,1,0:T(8,128...) custom-call(bf16[512,768]{1,0:T(8,128)(2,1)} %refs_0_.3, ...), custom_call_target="tpu_custom_call" | custom-call | tf_op jit(solution)/shard_map/block_forward/pallas_call | solution.py:921
  81.0 103.2 %block_backward.1 = (f32[512,768]{1,0:T(8,128)}, f32[8,24]{1,0:T(8,128)}, f32[3,96,192]{2,1,0:T(8,128)}, f32[192,96]{1,0:T(8,128)}, f32[96,768]{1,0:T(8,128)}, /*index=5*/f32[96,768]{1,0:T(8,128)}) custom-call(bf16[512,768]{1,0:T(8,128)(2,1)} %refs_0_.3, f32[8,768]{1,0:T(8,128)} %get-tuple-element.34.refs_1_, f32[512,768]{1,0:T(8,128)} %get-tuple-element.35.refs_2_, ...), custom_call_target="tpu_custom_call" | custom-call | tf_op jit(solution)/shard_map/block_backward/pallas_call | solution.py:950
  184.1 1.4 slice_bitcast_fusion
  185.5 0.0 copy-start
  185.5 2.8 %copy.31 = f32[512,768]{1,0:T(8,128)} copy(f32[512,768]{1,0:T(8,128)} %get-tuple-element.70) | data formatting | bytes 3145728
  188.3 0.0 copy-done
  188.3 0.0 copy-start.3
  188.3 0.0 copy-start.4
  188.3 0.0 copy-start.2
  188.3 0.0 copy-start.1
  188.3 1.1 copy.32
  189.4 0.0 copy-done.3
  189.4 0.0 copy-start.5
  189.4 0.7 copy.33
  190.2 0.0 copy-done.4
  190.2 0.6 copy.34
  190.8 0.0 copy-done.2
  190.8 0.7 copy.35
  191.5 0.0 copy-done.1
  191.5 0.7 copy.36
  192.2 0.0 copy-done.5
  192.2 0.5 copy.37
Async XLA Ops:
  185.5 2.8 %copy-start = (f32[512,768]{1,0:T(8,128)S(1)}, f32[512,768]{1,0:T(8,128)}, u32[]{:S(2)}) copy-start(f32[512,768]{1,0:T(8,128)} %get-tuple-element.71) | copy-start | bytes 4718596
  188.3 1.2 copy-start.3
  188.3 1.9 copy-start.4
  188.3 2.5 %copy-start.2 = (f32[96,768]{1,0:T(8,128)S(1)}, f32[96,768]{1,0:T(8,128)}, u32[]{:S(2)}) copy-start(f32[96,768]{1,0:T(8,128)} %get-tuple-element.74) | copy-start | bytes 884740
  188.3 3.2 %copy-start.1 = (f32[96,768]{1,0:T(8,128)S(1)}, f32[96,768]{1,0:T(8,128)}, u32[]{:S(2)}) copy-start(f32[96,768]{1,0:T(8,128)} %get-tuple-element.52) | copy-start | bytes 884740
  189.4 2.8 %copy-start.5 = (f32[1,16]{1,0:T(1,128)S(1)}, f32[1,16]{1,0:T(1,128)}, u32[]{:S(2)}) copy-start(f32[1,16]{1,0:T(1,128)} %get-tuple-element.54) | copy-start | bytes 196

commit v3 on v2

v3 whole, which is shorter than its diff:
```python
import functools

import jax
import jax.numpy as jnp
from jax import lax
from jax.experimental import pallas as pl
from jax.experimental.pallas import tpu as pltpu
from jax.sharding import PartitionSpec as P

D = 768
HEAD_DIM = 64
LENGTH = 1024
HALF = 512
GROUPS = 16
TABLE = 8
NB = 8
RB = D // NB
ORDER = (0, 3, 1, 2)
EPSILON = 1e-05
MASKED_SCORE = -1e30
GELU_C = 0.7978845608028654
GELU_A = 0.044715
MESH = pl.DeviceIdType.MESH
F32 = jnp.float32
BF16 = jnp.bfloat16
NT = (((1,), (1,)), ((), ()))
TN = (((0,), (0,)), ((), ()))
NN = (((1,), (0,)), ((), ()))
VMEM_LIMIT = 66_000_000


def mm(a, b, dims=NN):
    return lax.dot_general(a, b, dims, preferred_element_type=F32)


class Place:
    def __init__(self):
        self.d = lax.axis_index("dp")
        self.t = lax.axis_index("tensor")
        self.z = lax.div(self.d, 2)
        self.y = lax.rem(self.d, 2)
        self.x = lax.div(self.t, 2)
        self.c = lax.rem(self.t, 2)
        c = self.c
        self.sibling = (self.d, self.t + 1 - 2 * c)
        self.x1 = lax.rem(self.x + c, 2)
        self.y1 = lax.rem(self.y + 1 - c, 2)
        self.x2 = lax.rem(self.x + 1 - c, 2)
        self.y2 = lax.rem(self.y + c, 2)
        self.p1 = (2 * self.z + self.y1, 2 * self.x1 + c)
        self.p2 = (2 * self.z + self.y2, 2 * self.x2 + c)
        self.up = (self.d + 2, self.t)
        self.dn = (self.d - 2, self.t)
        self.has_up = self.z < 3
        self.has_dn = self.z > 0


def entry_barrier(pos, net):
    bar = pltpu.get_barrier_semaphore()
    pl.semaphore_signal(bar, inc=1, device_id=pos.sibling, device_id_type=MESH)
    if not net:
        pl.semaphore_wait(bar, 1)
        return
    pl.semaphore_signal(bar, inc=1, device_id=pos.p1, device_id_type=MESH)
    pl.semaphore_signal(bar, inc=1, device_id=pos.p2, device_id_type=MESH)

    @pl.when(pos.has_up)
    def _():
        pl.semaphore_signal(bar, inc=1, device_id=pos.up, device_id_type=MESH)

    @pl.when(pos.has_dn)
    def _():
        pl.semaphore_signal(bar, inc=1, device_id=pos.dn, device_id_type=MESH)

    pl.semaphore_wait(bar, 3 + jnp.where(pos.has_up, 1, 0) + jnp.where(pos.has_dn, 1, 0))


class Gather:
    def __init__(self, pos, g, own, full, ssem, rsem):
        self.pos, self.g, self.own, self.full = pos, g, own, full
        self.ssem, self.rsem = ssem, rsem

    def copy(self, b, dd, link, zz, dev, src=None):
        slot = self.full.at[b, dd]
        return pltpu.make_async_remote_copy(
            src_ref=slot if src is None else src,
            dst_ref=slot,
            send_sem=self.ssem.at[self.g, link, zz],
            recv_sem=self.rsem.at[self.g, b, dd],
            device_id=dev,
            device_id_type=MESH,
        )

    def wait(self, b, dd):
        self.copy(b, dd, 0, 0, self.pos.p1).wait_recv()

    def start(self):
        p = self.pos
        own = self.own
        self.copy(p.x, p.d, 2, p.z, p.p1, own).start()
        self.copy(p.x, p.d, 3, p.z, p.p2, own).start()

        @pl.when(p.has_up)
        def _():
            self.copy(p.x, p.d, 0, p.z, p.up, own).start()

        @pl.when(p.has_dn)
        def _():
            self.copy(p.x, p.d, 1, p.z, p.dn, own).start()

    def line(self, k):
        p = self.pos

        @pl.when(p.z - k >= 0)
        def _():
            zz = p.z - k
            self.wait(p.x, 2 * zz + p.y)

            @pl.when(p.has_up)
            def _():
                self.copy(p.x, 2 * zz + p.y, 0, zz, p.up).start()

            self.copy(p.x, 2 * zz + p.y, 2, zz, p.p1).start()
            self.copy(p.x, 2 * zz + p.y, 3, zz, p.p2).start()

        @pl.when(p.z + k <= 3)
        def _():
            zz = p.z + k
            self.wait(p.x, 2 * zz + p.y)

            @pl.when(p.has_dn)
            def _():
                self.copy(p.x, 2 * zz + p.y, 1, zz, p.dn).start()

            self.copy(p.x, 2 * zz + p.y, 2, zz, p.p1).start()
            self.copy(p.x, 2 * zz + p.y, 3, zz, p.p2).start()

    def side(self, k):
        p = self.pos

        def forward(zz):
            self.wait(p.x1, 2 * zz + p.y1)
            self.copy(p.x1, 2 * zz + p.y1, 4, zz, p.p2).start()

        if k == 0:
            forward(p.z)
            return

        @pl.when(p.z - k >= 0)
        def _():
            forward(p.z - k)

        @pl.when(p.z + k <= 3)
        def _():
            forward(p.z + k)

    def step(self, k):
        if k == 0:
            self.start()
        if 1 <= k <= 3:
            self.line(k)
        if k >= 1:
            self.side(k - 1)

    def finish(self):
        p = self.pos
        for zz in range(4):
            self.wait(p.x2, 2 * zz + p.y2)
            self.wait(1 - p.x, 2 * zz + 1 - p.y)

    def drain(self):
        p = self.pos
        for zz in range(4):
            dd = 2 * zz + p.y

            @pl.when(p.has_up & (zz <= p.z))
            def _():
                self.copy(p.x, dd, 0, zz, p.up).wait_send()

            @pl.when(p.has_dn & (zz >= p.z))
            def _():
                self.copy(p.x, dd, 1, zz, p.dn).wait_send()

            self.copy(p.x, dd, 2, zz, p.p1).wait_send()
            self.copy(p.x, dd, 3, zz, p.p2).wait_send()
            self.copy(p.x1, 2 * zz + p.y1, 4, zz, p.p2).wait_send()


class Reduce:
    def __init__(self, pos, g, slot, r2, rz, ssem, rsem):
        self.pos, self.g, self.slot, self.r2, self.rz = pos, g, slot, r2, rz
        self.ssem, self.rsem = ssem, rsem

    def copy(self, src, dst, link, zz, dev):
        return pltpu.make_async_remote_copy(
            src_ref=src,
            dst_ref=dst,
            send_sem=self.ssem.at[self.g, link, zz],
            recv_sem=self.rsem.at[self.g, link, zz],
            device_id=dev,
            device_id_type=MESH,
        )

    def to_p2(self, which, zz):
        p = self.pos
        b, dd = (p.x2, 2 * zz + p.y2) if which == 0 else (1 - p.x, 2 * zz + 1 - p.y)
        return self.copy(self.slot(b, dd), self.r2.at[which, zz], which, zz, p.p2)

    def to_p1(self, zz):
        p = self.pos
        return self.copy(self.slot(p.x1, 2 * zz + p.y1), self.rz.at[zz], 2, zz, p.p1)

    def to_z(self, way, zz):
        p = self.pos
        place = self.rz.at[4 + zz if way else 5 + zz]
        return self.copy(self.slot(p.x, 2 * zz + p.y), place, 3 + way, zz, p.dn if way else p.up)

    def add(self, b, dd, other):
        ref = self.slot(b, dd)
        ref[...] = (ref[...].astype(F32) + other.astype(F32)).astype(ref.dtype)

    def start(self):
        for which in (1, 0):
            for zz in ORDER:
                self.to_p2(which, zz).start()

    def mid1(self):
        p = self.pos
        for zz in ORDER:
            self.to_p2(1, zz).wait_recv()
            self.add(p.x1, 2 * zz + p.y1, self.r2[1, zz])
            self.to_p1(zz).start()

    def mid0(self):
        p = self.pos
        for zz in ORDER:
            self.to_p2(0, zz).wait_recv()
            self.add(p.x, 2 * zz + p.y, self.r2[0, zz])

    def join(self):
        p = self.pos
        for zz in ORDER:
            self.to_p1(zz).wait_recv()
            self.add(p.x, 2 * zz + p.y, self.rz[zz])

    def hop(self, h):
        p = self.pos
        for zz in range(3, h, -1):

            @pl.when(p.z == h)
            def _():
                if h > 0:
                    self.to_z(0, zz).wait_recv()
                    self.add(p.x, 2 * zz + p.y, self.rz[5 + zz])
                self.to_z(0, zz).start()

            dz = 3 - zz

            @pl.when(p.z == 3 - h)
            def _():
                if h > 0:
                    self.to_z(1, dz).wait_recv()
                    self.add(p.x, 2 * dz + p.y, self.rz[4 + dz])
                self.to_z(1, dz).start()

    def finish(self, out):
        p = self.pos
        out[...] = self.slot(p.x, p.d)[...].astype(F32)

        @pl.when(p.has_dn)
        def _():
            self.to_z(0, p.z).wait_recv()
            out[...] += self.rz[5 + p.z].astype(F32)

        @pl.when(p.has_up)
        def _():
            self.to_z(1, p.z).wait_recv()
            out[...] += self.rz[4 + p.z].astype(F32)

    def drain(self):
        p = self.pos
        for zz in range(4):
            self.to_p2(1, zz).wait_send()
            self.to_p2(0, zz).wait_send()
            self.to_p1(zz).wait_send()

            @pl.when(zz > p.z)
            def _():
                self.to_z(0, zz).wait_send()

            @pl.when(zz < p.z)
            def _():
                self.to_z(1, zz).wait_send()


def rows(start, size):
    return pl.ds(pl.multiple_of(start, size), size)


def swap(pos, src, dst, sems, i):
    return pltpu.make_async_remote_copy(
        src_ref=src,
        dst_ref=dst,
        send_sem=sems.at[0, i],
        recv_sem=sems.at[1, i],
        device_id=pos.sibling,
        device_id_type=MESH,
    )


def norm_stats(values):
    center = values - jnp.mean(values, -1, keepdims=True)
    inv = lax.rsqrt(jnp.mean(center * center, -1, keepdims=True) + EPSILON)
    return center * inv, inv


def lane_half(shape, which):
    lane = lax.broadcasted_iota(jnp.int32, shape, 1)
    return (lane < HEAD_DIM) if which == 0 else (lane >= HEAD_DIM)


def only(values, which):
    return jnp.where(lane_half(values.shape, which), values, jnp.zeros_like(values))


def roll_half(values):
    return pltpu.roll(values.astype(F32), HEAD_DIM, 1).astype(BF16)


def unpack_heads(raw, first, count, wh):
    @pl.loop(0, NB)
    def _(dd):
        at = pl.multiple_of(dd * RB, 16)
        for i in range(count):
            one, two = raw[0, dd, first + i], raw[1, dd, first + i]
            left = lane_half(one.shape, 0)
            wh[first + i, pl.ds(at, 48)] = jnp.where(left, one, roll_half(two))
            wh[first + i, pl.ds(at + 48, 48)] = jnp.where(left, roll_half(one), two)


def pack_head(grad, raw, i):
    left = lane_half((48, 128), 0)
    for dd in range(NB):
        top, bottom = grad[RB * dd : RB * dd + 48], grad[RB * dd + 48 : RB * dd + 96]
        raw[0, dd, i] = jnp.where(left, top, roll_half(bottom))
        raw[1, dd, i] = jnp.where(left, roll_half(top), bottom)


def fold(block):
    return jnp.concatenate([block[0:48], block[48:96]], axis=1)


def unfold(block):
    return jnp.concatenate([block[:, 0:64], block[:, 64:128]], axis=0)


def transpose_rows(src, dst):
    @pl.loop(0, LENGTH // 128)
    def _(i):
        r = rows(i * 128, 128)
        dst[:, r] = src[r, :].T


def cat(pieces):
    return jnp.concatenate(pieces, axis=1)


def block_kernel(net, scale_tokens, nin, *refs):
    hid, cot, ids, table, weights, *given = refs[:nin]
    o_block, o_counts, o_in, o_small, o_qkv, o_out, o_up, o_down = refs[nin : nin + 8]
    (
        v_small, v_cnt, v_param, v_index, own_q, own_o, v_rq, v_ro, v_up, v_down, v_wh, v_wo,
        v_nrm, v_nrmT, v_n2, v_n2T, v_ups, v_upsT, v_qkv, v_lse, v_ctx, v_dctx, v_mid, v_act, v_slope,
        v_send, v_recv, v_acc, v_dk, v_dv, v_p2, v_p3, v_sums, v_swap, swsem, lsem, *nets,
    ) = refs[nin + 8 :]
    v_low, v_lowT = v_nrm, v_upsT
    pos = Place()
    mine = pos.c * HALF
    theirs = HALF - mine

    def exchange(i, src, dst):
        return swap(pos, src, dst, swsem, i)

    def exchange_rows(i, ref):
        return swap(pos, ref.at[rows(mine, HALF)], ref.at[rows(mine, HALF)], swsem, i)

    row_ids = jnp.broadcast_to(ids[...].astype(F32), (128, HALF)).T
    member = row_ids == lax.broadcasted_iota(jnp.int32, (HALF, 128), 1).astype(F32)
    own_counts = jnp.sum(member.astype(F32), 0, keepdims=True)

    if net:
        qkv_w, out_w, own_up, own_down, *vectors = given
        v_p0, r2_0, rz_0, r2_q, rz_q, r2_o, rz_o, r2_2, rz_2, r2_3, rz_3, f_q, f_o, gssem, grsem, rssem, rrsem = nets
        v_cnt[2] = jnp.zeros((8, 128), F32)
        for i in range(4):
            v_cnt[2, i : i + 1, 0:RB] = vectors[i][...].astype(F32)
        v_cnt[2, 4:5, :] = own_counts
        out_rows = out_w[...].T
        for j in range(3):
            for part in range(3):
                own_q[3 * j + part] = fold(qkv_w[part][:, 64 * j : 64 * j + 64])
            own_o[j] = fold(out_rows[:, 64 * j : 64 * j + 64])
        entry_barrier(pos, net)
        g0 = Gather(pos, 0, v_cnt.at[2], v_small, gssem, grsem)
        gq = Gather(pos, 1, own_q, v_rq, gssem, grsem)
        go = Gather(pos, 2, own_o, v_ro, gssem, grsem)
        g2 = Gather(pos, 3, own_up, v_up, gssem, grsem)
        g3 = Gather(pos, 4, own_down, v_down, gssem, grsem)
        s0 = Reduce(pos, 0, lambda b, dd: v_p0.at[b, dd], r2_0, rz_0, rssem, rrsem)
        so = Reduce(pos, 1, lambda b, dd: v_ro.at[b, dd], r2_o, rz_o, rssem, rrsem)
        s2 = Reduce(pos, 2, lambda b, dd: v_p2.at[b, dd], r2_2, rz_2, rssem, rrsem)
        s3 = Reduce(pos, 3, lambda b, dd: v_p3.at[b, dd], r2_3, rz_3, rssem, rrsem)

        def sq(j):
            return Reduce(
                pos, 4 + j, lambda b, dd: v_rq.at[b, dd, pl.ds(3 * j, 3)], r2_q.at[j], rz_q.at[j], rssem, rrsem
            )

        g0.step(0)
        gq.step(0)
        v_small[pos.x, pos.d] = v_cnt[2]
        v_rq[pos.x, pos.d] = own_q[...]
        v_ro[pos.x, pos.d] = own_o[...]
        v_up[pos.x, pos.d] = own_up[...]
        v_down[pos.x, pos.d] = own_down[...]
        for k in (1, 2, 3):
            g0.step(k)
            gq.step(k)
        go.step(0)
        g2.step(0)
        g0.step(4)
        gq.step(4)
        g0.finish()
        v_param[...] = jnp.zeros_like(v_param)
        total = jnp.zeros((8, 128), F32)
        for dd in range(NB):
            row = lax.broadcasted_iota(jnp.int32, (128, D), 0)
            col = lax.broadcasted_iota(jnp.int32, (128, D), 1)
            place = ((col == row + RB * dd) & (row < RB)).astype(BF16)
            block = v_small[pos.x, dd]
            v_param[...] += mm(block.astype(BF16), place)
            total += v_small[0, dd] + v_small[1, dd]
        v_cnt[0] = total
        exchange(0, v_cnt.at[0], v_cnt.at[1]).start()
    else:
        vectors, *wide = given
        entry_barrier(pos, net)
        v_param[...] = vectors[...]
        cps = [pltpu.make_async_copy(a, b, lsem.at[i]) for i, (a, b) in enumerate(zip(wide, (v_rq, v_ro, v_up, v_down)))]
        for cp in cps:
            cp.start()
        for cp in cps:
            cp.wait()

    @pl.loop(0, HALF // 64)
    def _(i):
        r = rows(i * 64, 64)
        hat, _inv = norm_stats(hid[r, :].astype(F32))
        v_nrm[rows(mine + i * 64, 64), :] = (hat * v_param[0:1, :] + v_param[1:2, :]).astype(BF16)

    exchange_rows(1, v_nrm).start()

    if net:
        exchange(0, v_cnt.at[0], v_cnt.at[1]).wait()
        counts = (v_cnt[0] + v_cnt[1])[4:5, :]
        v_index[...] = jnp.full(v_index.shape, -1, jnp.int32)
        v_index[0:1, 0:GROUPS] = table[...]
        index = v_index[0:1, :]
        weight = jnp.zeros((1, 128), F32)
        for r in range(TABLE):
            weight = weight + jnp.where(index == r, weights[r], 0.0)
        group_scale = weight * scale_tokens / jnp.maximum(counts, 1.0)
        o_counts[...] = counts[:, 0:GROUPS]
    else:
        o_counts[...] = table[...]
        group_scale = weights[0:1, :]
    row_scale = jnp.sum(jnp.where(member, group_scale, 0.0), 1, keepdims=True)
    v_ups[rows(mine, HALF), :] = (cot[...].astype(F32) * row_scale).astype(BF16)
    exchange_rows(2, v_ups).start()

    if net:
        go.step(1)
        g2.step(1)
        go.step(2)
        g2.step(2)
        gq.finish()
    unpack_heads(v_rq, 0, 9, v_wh)
    if net:
        go.step(3)
        g2.step(3)
        go.step(4)
        g3.step(0)

    for half, start in enumerate((mine, theirs)):
        if half == 1:
            exchange_rows(1, v_nrm).wait_send()
            swap(pos, v_nrm.at[rows(theirs, HALF)], v_nrm.at[rows(theirs, HALF)], swsem, 1).wait_recv()
        lhs = v_nrm[rows(start, HALF), :]
        for part in range(3):
            res = mm(lhs, cat([v_wh[3 * j + part] for j in range(3)])).astype(BF16)
            if part == 0:
                res = (res.astype(F32) * HEAD_DIM**-0.5).astype(BF16)
            for j in range(3):
                v_qkv[3 * part + j, rows(start, HALF), :] = res[:, 128 * j : 128 * j + 128]

    @pl.loop(0, 3)
    def _(pair):
        if net:

            @pl.when(pair == 1)
            def _():
                g2.step(4)
                g3.step(1)

            @pl.when(pair == 2)
            def _():
                g3.step(2)

        for i in range(4):
            n = 256 * (i + 1)
            q = v_qkv[pair, 256 * i : n, :]
            out = jnp.zeros((256, 128), F32)
            for h in range(2):
                pieces = []
                peak = None
                for j in range(i + 1):
                    k = only(v_qkv[3 + pair, 256 * j : 256 * j + 256, :], h)
                    s = mm(k, q, NT)
                    if j == i:
                        key = lax.broadcasted_iota(jnp.int32, s.shape, 0)
                        query = lax.broadcasted_iota(jnp.int32, s.shape, 1)
                        s = jnp.where(key <= query, s, MASKED_SCORE)
                    top = jnp.max(s, 0, keepdims=True)
                    peak = top if peak is None else jnp.maximum(peak, top)
                    pieces.append(s)
                total = jnp.zeros((1, 256), F32)
                for j in range(i + 1):
                    e = jnp.exp(pieces[j] - peak)
                    total += jnp.sum(e, 0, keepdims=True)
                    pieces[j] = e
                inv = 1.0 / total
                for j in range(i + 1):
                    v = only(v_qkv[6 + pair, 256 * j : 256 * j + 256, :], h)
                    out += mm((pieces[j] * inv).astype(BF16), v, TN)
                v_lse[pair, h : h + 1, 256 * i : n] = peak + jnp.log(total)
            v_ctx[pair, 256 * i : n, :] = out.astype(BF16)

    if net:
        g3.step(3)
        go.finish()
    unpack_heads(v_ro, 0, 3, v_wo)

    w_out = cat([v_wo[j] for j in range(3)])
    for half, start in enumerate((theirs, mine)):
        lhs = cat([v_ctx[j, rows(start, HALF), :] for j in range(3)])
        res = mm(lhs, w_out, NT)
        if half == 0:
            v_send[0] = res.astype(BF16)
            exchange(3, v_send.at[0], v_recv.at[0]).start()
        else:
            v_acc[...] = res
    if net:
        g3.step(4)
    transpose_rows(v_nrm, v_nrmT)
    exchange(3, v_send.at[0], v_recv.at[0]).wait()

    @pl.loop(0, HALF // 64)
    def _(i):
        r = rows(i * 64, 64)
        middle = hid[r, :].astype(F32) + v_acc[r, :] + v_recv[0, r, :].astype(F32)
        v_mid[r, :] = middle
        hat, _inv = norm_stats(middle)
        v_n2[rows(mine + i * 64, 64), :] = (hat * v_param[2:3, :] + v_param[3:4, :]).astype(BF16)

    exchange_rows(4, v_n2).start()
    exchange_rows(2, v_ups).wait_send()
    swap(pos, v_ups.at[rows(theirs, HALF)], v_ups.at[rows(theirs, HALF)], swsem, 2).wait_recv()
    transpose_rows(v_ups, v_upsT)
    if net:
        g2.finish()

    for half, start in enumerate((mine, theirs)):
        if half == 1:
            swap(pos, v_n2.at[rows(theirs, HALF)], v_n2.at[rows(theirs, HALF)], swsem, 4).wait_recv()

        @pl.loop(0, 6)
        def _(tile):
            b = lax.div(tile, 3)
            cols = pl.ds(pl.multiple_of(lax.rem(tile, 3) * 256, 256), 256)
            pre = mm(v_n2[rows(start, HALF), :], v_up[b, :, :, cols].reshape(D, 256))
            square = pre * pre
            bend = jnp.tanh(GELU_C * pre * (1.0 + GELU_A * square))
            v_act[b, rows(start, HALF), cols] = (0.5 * pre * (1.0 + bend)).astype(BF16)
            slope = 0.5 * (1.0 + bend) + 0.5 * pre * (1.0 - bend * bend) * (GELU_C * (1.0 + 3.0 * GELU_A * square))
            v_slope[b, rows(start, HALF), cols] = slope.astype(BF16)

    exchange_rows(4, v_n2).wait_send()
    transpose_rows(v_n2, v_n2T)

    def tile_of(tile):
        return lax.div(tile, 3), pl.ds(pl.multiple_of(lax.rem(tile, 3) * 256, 256), 256)

    @pl.loop(0, 6)
    def _(tile):
        b, cols = tile_of(tile)
        res = mm(v_upsT[...], v_act[b, :, cols])
        v_p3[b, :, :, cols] = res.astype(BF16).reshape(NB, RB, 256)

    if net:
        s3.start()
        g3.finish()
        gq.drain()
        go.drain()

    @pl.loop(0, 6)
    def _(tile):
        b, cols = tile_of(tile)
        res = mm(v_ups[...], v_down[b, :, :, cols].reshape(D, 256))
        pre = (res * v_slope[b, :, cols].astype(F32)).astype(BF16)
        v_slope[b, :, cols] = pre
        res = mm(v_n2T[...], pre)
        v_p2[b, :, :, cols] = res.astype(BF16).reshape(NB, RB, 256)

    if net:
        s2.start()
    for half, start in enumerate((theirs, mine)):
        res = mm(v_slope[0, rows(start, HALF), :], v_up[0].reshape(D, D), NT)
        res += mm(v_slope[1, rows(start, HALF), :], v_up[1].reshape(D, D), NT)
        if half == 0:
            v_send[0] = res.astype(BF16)
            exchange(5, v_send.at[0], v_recv.at[0]).start()
        else:
            v_acc[...] = res
    if net:
        s3.mid1()
    exchange(5, v_send.at[0], v_recv.at[0]).wait()
    v_sums[...] = jnp.zeros_like(v_sums)

    def norm_back(upper, values, gain, at):
        hat, inv = norm_stats(values)
        scaled = upper * gain
        first = jnp.mean(scaled, -1, keepdims=True)
        second = jnp.mean(scaled * hat, -1, keepdims=True)
        v_sums[at : at + 1, :] += jnp.sum(upper * hat, 0, keepdims=True)
        v_sums[at + 1 : at + 2, :] += jnp.sum(upper, 0, keepdims=True)
        return inv * (scaled - first - hat * second)

    @pl.loop(0, HALF // 64)
    def _(i):
        r = rows(i * 64, 64)
        wide = rows(mine + i * 64, 64)
        upper = v_acc[r, :] + v_recv[0, r, :].astype(F32)
        d_mid = v_ups[wide, :].astype(F32) + norm_back(upper, v_mid[r, :], v_param[2:3, :], 2)
        o_in[r, :] = d_mid
        v_low[wide, :] = d_mid.astype(BF16)

    exchange_rows(6, v_low).start()
    for half, start in enumerate((mine, theirs)):
        if half == 1:
            swap(pos, v_low.at[rows(theirs, HALF)], v_low.at[rows(theirs, HALF)], swsem, 6).wait_recv()
        res = mm(v_low[rows(start, HALF), :], w_out).astype(BF16)
        for j in range(3):
            v_dctx[j, rows(start, HALF), :] = res[:, 128 * j : 128 * j + 128]
    transpose_rows(v_low, v_lowT)
    res = mm(v_lowT[...], cat([v_ctx[j] for j in range(3)])).astype(BF16)
    for j in range(3):
        pack_head(res[:, 128 * j : 128 * j + 128], v_ro, j)
    if net:
        so.start()
        s3.mid0()

    @pl.loop(0, 3)
    def _(pair):
        if net:

            @pl.when(pair == 1)
            def _():
                s3.join()
                s3.hop(0)

            @pl.when(pair == 2)
            def _():
                s2.mid1()
                s3.hop(1)

        v_dk[...] = jnp.zeros_like(v_dk)
        v_dv[...] = jnp.zeros_like(v_dv)
        for i in range(4):
            n = 256 * (i + 1)
            q = v_qkv[pair, 256 * i : n, :]
            up = v_dctx[pair, 256 * i : n, :]
            qs = [only(q, h) for h in range(2)]
            ups = [only(up, h) for h in range(2)]
            dq = jnp.zeros((256, 128), F32)
            probs = [[], []]
            grads = [[], []]
            for h in range(2):
                lse = v_lse[pair, h : h + 1, 256 * i : n]
                delta = jnp.zeros((1, 256), F32)
                for j in range(i + 1):
                    at = slice(256 * j, 256 * j + 256)
                    s = mm(v_qkv[3 + pair, at, :], qs[h], NT)
                    p = jnp.exp(s - lse)
                    if j == i:
                        key = lax.broadcasted_iota(jnp.int32, s.shape, 0)
                        query = lax.broadcasted_iota(jnp.int32, s.shape, 1)
                        p = jnp.where(key <= query, p, 0.0)
                    dp = mm(v_qkv[6 + pair, at, :], ups[h], NT)
                    delta += jnp.sum(p * dp, 0, keepdims=True)
                    probs[h].append(p)
                    grads[h].append(dp)
                for j in range(i + 1):
                    grads[h][j] = (probs[h][j] * (grads[h][j] - delta)).astype(BF16)
                    probs[h][j] = probs[h][j].astype(BF16)
            for j in range(i + 1):
                at = slice(256 * j, 256 * j + 256)
                for h in range(2):
                    k = only(v_qkv[3 + pair, at, :], h)
                    dq += mm(grads[h][j], k, TN)
                v_dv[at, :] += mm(cat([probs[0][j], probs[1][j]]), jnp.concatenate(ups, axis=0))
                v_dk[at, :] += mm(cat([grads[0][j], grads[1][j]]), jnp.concatenate(qs, axis=0))
            v_qkv[pair, 256 * i : n, :] = (dq * HEAD_DIM**-0.5).astype(BF16)
        v_qkv[3 + pair] = v_dk[...].astype(BF16)
        v_qkv[6 + pair] = v_dv[...].astype(BF16)
        res = mm(v_nrmT[...], cat([v_qkv[3 * part + pair] for part in range(3)])).astype(BF16)
        for part in range(3):
            pack_head(res[:, 128 * part : 128 * part + 128], v_rq, 3 * pair + part)
        if net:
            sq(pair).start()

    w_qkv = cat([v_wh[3 * j + part] for part in range(3) for j in range(3)])
    for half, start in enumerate((theirs, mine)):
        lhs = cat([v_qkv[i, rows(start, HALF), :] for i in range(9)])
        res = mm(lhs, w_qkv, NT)
        if half == 0:
            v_send[1] = res.astype(BF16)
            exchange(7, v_send.at[1], v_recv.at[1]).start()
        else:
            v_acc[...] = res
    if net:
        q0, q1, q2 = sq(0), sq(1), sq(2)
        s2.mid0()
        s3.hop(2)
        so.mid1()
        so.mid0()
    exchange(7, v_send.at[1], v_recv.at[1]).wait()

    @pl.loop(0, HALF // 64)
    def _(i):
        r = rows(i * 64, 64)
        upper = v_acc[r, :] + v_recv[1, r, :].astype(F32)
        o_in[r, :] = o_in[r, :] + norm_back(upper, hid[r, :].astype(F32), v_param[0:1, :], 0)

    v_swap[0] = v_sums[...]
    exchange(8, v_swap.at[0], v_swap.at[1]).start()
    if net:
        s2.join()
        s2.hop(0)
        q0.mid1()
        q0.mid0()
        so.join()
        so.hop(0)
        s2.hop(1)
    exchange(8, v_swap.at[0], v_swap.at[1]).wait()
    both = v_swap[0] + v_swap[1]
    if net:
        for dd in range(NB):
            piece = cat([both[:, RB * dd : RB * dd + RB], jnp.zeros((8, 128 - RB), F32)])
            v_p0[0, dd] = piece
            v_p0[1, dd] = piece
        s0.start()
        q1.mid1()
        q1.mid0()

    for half, start in enumerate((theirs, mine)):
        res = mm(v_act[0, rows(start, HALF), :], v_down[0].reshape(D, D), NT)
        res += mm(v_act[1, rows(start, HALF), :], v_down[1].reshape(D, D), NT)
        if half == 0:
            v_send[0] = res.astype(BF16)
            exchange(9, v_send.at[0], v_recv.at[0]).start()
            if net:
                s2.hop(2)
                q0.join()
                q0.hop(0)
                so.hop(1)
                q2.mid1()
                q2.mid0()
        else:
            o_block[...] = v_mid[...] + res
    if net:
        q1.join()
        q1.hop(0)
        so.hop(2)
        q0.hop(1)
        s0.mid1()
        s0.mid0()
        q2.join()
        q2.hop(0)
        q1.hop(1)
        q0.hop(2)
        s0.join()
        s0.hop(0)
        q2.hop(1)
        q1.hop(2)
        s0.hop(1)
        q2.hop(2)
        s0.hop(2)
    exchange(9, v_send.at[0], v_recv.at[0]).wait()
    o_block[...] += v_recv[0].astype(F32)
    if net:
        s3.finish(o_down)
        s2.finish(o_up)
        so.finish(f_o)
        o_out[...] = cat([unfold(f_o[j]) for j in range(3)]).T
        q0.finish(f_q.at[0])
        q1.finish(f_q.at[1])
        q2.finish(f_q.at[2])
        for part in range(3):
            o_qkv[part] = cat([unfold(f_q[j, part]) for j in range(3)])
        s0.finish(v_swap.at[0, :, 0:128])
        o_small[...] = pltpu.roll(v_swap[0, :, 0:128], lax.rem(128 - 24 * pos.t, 128), 1)[:, 0:24]
        for g in (g0, g2, g3, s0, so, s2, s3, q0, q1, q2):
            g.drain()
    else:
        o_small[...] = both
        o_qkv[...] = v_rq[...]
        o_out[...] = v_ro[...]
        o_up[...] = v_p2[...]
        o_down[...] = v_p3[...]
    exchange_rows(6, v_low).wait_send()


def fold_rows(block):
    return block.reshape(2, 48, 3, 64).transpose(2, 1, 0, 3).reshape(3, 48, 128)


def unfold_rows(packed):
    return packed.reshape(3, 48, 2, 64).transpose(2, 1, 0, 3).reshape(RB, 192)


def shards(
    hidden_in, cotangent, group_ids, weight_table, table_index, qkv_weight, out_weight, up_weight, down_weight,
    norm1_gain, norm1_bias, norm2_gain, norm2_bias,
):
    n_dp, n_t = lax.axis_size("dp"), lax.axis_size("tensor")
    net = n_dp == NB and n_t == 4
    core = lax.rem(lax.axis_index("tensor"), 2)
    scale_tokens = hidden_in.shape[0] * n_dp * n_t / GROUPS
    ids = group_ids.reshape(1, HALF)
    down = down_weight.T
    vm, dma = pltpu.VMEM, pltpu.SemaphoreType.DMA
    vspec = pl.BlockSpec(memory_space=pltpu.VMEM)
    aspec = pl.BlockSpec(memory_space=pl.ANY)
    norm_vectors = (norm1_gain, norm1_bias, norm2_gain, norm2_bias)
    s_q, s_o, s_w = (3, 48, 128), (3, 48, 128), (RB, D)
    if net:
        vectors = [v.reshape(1, RB) for v in norm_vectors]
        table, weights = table_index.reshape(1, GROUPS), weight_table
        given = [qkv_weight.transpose(1, 0, 2), out_weight, up_weight, down, *vectors]
        weight_spec = pl.BlockSpec(memory_space=pltpu.SMEM)
        given_specs = [vspec] * len(given)
        grads = [((8, 24), F32), ((3, RB, 192), F32), ((192, RB), F32), (s_w, F32), (s_w, F32)]
        nets = [vm((2, NB, 8, 128), F32), vm((2, 4, 8, 128), F32), vm((9, 8, 128), F32)]
        nets += [vm((3, 2, 4) + s_q, BF16), vm((3, 9) + s_q, BF16)]
        for s in (s_o, s_w, s_w):
            nets += [vm((2, 4) + s, BF16), vm((9,) + s, BF16)]
        nets += [vm((3,) + s_q, F32), vm(s_o, F32)]
        nets += [dma((5, 5, 4)), dma((5, 2, NB)), dma((7, 5, 4)), dma((7, 5, 4))]
    else:

        def whole(block, axis):
            full = lax.all_gather(block, "dp", axis=axis, tiled=True)
            every = lax.all_gather(full, "tensor", axis=0)
            return lax.dynamic_index_in_dim(every.reshape((n_t // 2, 2) + full.shape), core, 1, keepdims=False)

        heads = jnp.concatenate([qkv_weight.transpose(1, 0, 2), out_weight.T[None]], axis=0)
        heads = whole(heads, 1).reshape(2, 4, NB, RB, 192).transpose(0, 2, 1, 3, 4)
        folded = jax.vmap(jax.vmap(jax.vmap(fold_rows)))(heads)
        given = [
            jnp.pad(lax.all_gather(jnp.stack(norm_vectors).astype(F32), "dp", axis=1, tiled=True), ((0, 4), (0, 0))),
            folded[:, :, :3].transpose(0, 1, 3, 2, 4, 5).reshape(2, NB, 9, 48, 128),
            folded[:, :, 3],
            whole(up_weight, 0).reshape(2, NB, RB, D),
            whole(down, 0).reshape(2, NB, RB, D),
        ]
        member = (group_ids[:, None] == jnp.arange(GROUPS, dtype=jnp.int32)[None, :]).astype(F32)
        counts = lax.psum(jnp.sum(member, 0), ("dp", "tensor"))
        hits = table_index[:, None] == jnp.arange(TABLE, dtype=jnp.int32)[None, :]
        scale = jnp.sum(jnp.where(hits, weight_table[None, :], 0.0), 1) * scale_tokens / jnp.maximum(counts, 1.0)
        weights = jnp.pad(scale[None, :], ((0, 7), (0, 128 - GROUPS)))
        table = counts.reshape(1, GROUPS)
        weight_spec = vspec
        given_specs = [vspec, aspec, aspec, aspec, aspec]
        grads = [((8, D), F32), ((2, NB, 9, 48, 128), BF16), ((2, NB, 3, 48, 128), BF16)]
        grads += [((2, NB) + s_w, BF16), ((2, NB) + s_w, BF16)]
        nets = []
    shapes = [((HALF, D), F32), ((1, GROUPS), F32), ((HALF, D), F32), *grads]
    outs = pl.pallas_call(
        functools.partial(block_kernel, net, scale_tokens, 5 + len(given)),
        out_shape=[jax.ShapeDtypeStruct(*s) for s in shapes],
        in_specs=[vspec, vspec, vspec, vspec, weight_spec, *given_specs],
        out_specs=[vspec] * len(shapes),
        scratch_shapes=[
            vm((2, NB, 8, 128), F32), vm((3, 8, 128), F32), vm((8, D), F32), vm((8, 128), jnp.int32), vm((9, 48, 128), BF16),
            vm((3, 48, 128), BF16), vm((2, NB, 9, 48, 128), BF16), vm((2, NB, 3, 48, 128), BF16), vm((2, NB, RB, D), BF16),
            vm((2, NB, RB, D), BF16), vm((9, D, 128), BF16), vm((3, D, 128), BF16),
            vm((LENGTH, D), BF16), vm((D, LENGTH), BF16), vm((LENGTH, D), BF16), vm((D, LENGTH), BF16), vm((LENGTH, D), BF16),
            vm((D, LENGTH), BF16), vm((9, LENGTH, 128), BF16), vm((3, 8, LENGTH), F32), vm((3, LENGTH, 128), BF16),
            vm((3, LENGTH, 128), BF16), vm((HALF, D), F32), vm((2, LENGTH, D), BF16), vm((2, LENGTH, D), BF16),
            vm((2, HALF, D), BF16), vm((2, HALF, D), BF16), vm((HALF, D), F32), vm((LENGTH, 128), F32), vm((LENGTH, 128), F32),
            vm((2, NB, RB, D), BF16), vm((2, NB, RB, D), BF16), vm((8, D), F32), vm((2, 8, D), F32),
            dma((2, 10)), dma((4,)), *nets,
        ],
        compiler_params=pltpu.CompilerParams(collective_id=0, has_side_effects=True, vmem_limit_bytes=VMEM_LIMIT),
        name="block",
    )(hidden_in, cotangent, ids, table, weights, *given)
    block_output, counts, input_grad, sums, grad_qkv, grad_out, grad_up, grad_down = outs
    if net:
        norms = [sums[i] for i in range(4)]
        grad_qkv = grad_qkv.transpose(1, 0, 2)
    else:

        def owned(part):
            base = jnp.zeros((n_t // 2, 2) + part.shape[1:], F32)
            base = lax.dynamic_update_index_in_dim(base, part.astype(F32), core, 1)
            flat = base.reshape((n_t,) + part.shape[1:])
            mine = lax.psum_scatter(flat, "tensor", scatter_dimension=0, tiled=False)
            return lax.psum_scatter(mine, "dp", scatter_dimension=0, tiled=True)

        parts = grad_qkv.reshape(2, NB, 3, 3, 48, 128).transpose(0, 1, 3, 2, 4, 5)
        parts = jax.vmap(jax.vmap(jax.vmap(unfold_rows)))(parts)
        grad_qkv = owned(parts.transpose(0, 1, 3, 2, 4).reshape(2, D, 3, 192))
        grad_out = owned(jax.vmap(jax.vmap(unfold_rows))(grad_out).reshape(2, D, 192)).T
        grad_up, grad_down = owned(grad_up.reshape(2, D, D)), owned(grad_down.reshape(2, D, D))
        half_sums = jnp.where(core == 0, sums, 0.0)
        norms = [lax.psum_scatter(half_sums[i], ("dp", "tensor"), scatter_dimension=0, tiled=True) for i in range(4)]
    return (
        block_output,
        input_grad,
        grad_qkv,
        grad_out,
        grad_up,
        grad_down.T,
        norms[0],
        norms[1],
        norms[2],
        norms[3],
        counts.reshape(GROUPS),
    )


def solution(mesh):
    both = ("dp", "tensor")
    return jax.shard_map(
        shards,
        mesh=mesh,
        in_specs=(
            P(both, None), P(both, None), P(both), P(), P(), P("dp", None, "tensor"), P("tensor", "dp"), P("dp", "tensor"),
            P("tensor", "dp"), P("dp"), P("dp"), P("dp"), P("dp"),
        ),
        out_specs=(
            P(both, None), P(both, None), P("dp", None, "tensor"), P("tensor", "dp"), P("dp", "tensor"), P("tensor", "dp"),
            P(both), P(both), P(both), P(both), P(),
        ),
        check_vma=False,
    )
```

time: 193 us -> 170 us (0.88)
  Pallas kernels: 183 us -> 160 us
    pallas_call x2 -> x1, Pallas kernels: 183 us -> 160 us  [shards(): pl.pallas_call(functools.partial(block_kernel, net, scale_tokens, 5 + len...]
where the time goes in v3:
time: 170 us; the launch traced here: 169 us
  Pallas kernels  160 us (94%)
  local copies, waits for them, and re-layouts  8.58 us (5%)
    pallas_call x1, Pallas kernels, shards(): pl.pallas_call(functools.partial(block_kernel, net, scale_tokens, 5 + len...  160 us
    unnamed x19, local copies, waits for them, and re-layouts  7.23 us

profile of v3, /device:TPU:0, one launch (start us, length us, event | category | flops | bytes accessed | tf_op | source)
XLA Modules:
  0.0 169.3 jit_solution(5871685967961168978)
XLA Ops:
  0.6 160.0 %block.1 = (f32[512,768]{1,0:T(8,128)}, f32[1,16]{1,0:T(1,128)}, f32[512,768]{1,0:T(8,128)}, f32[8,24]{1,0:T(8,128)}, f32[3,96,192]{2,1,0:T(8,128)}, /*index=5*/...) custom-call(bf16[512,768]{1,0:T(8,128)(2,1)} %refs_0_.1, bf16[512,768]{1,0:T(8,128)(2,1)} %refs_1_.1, ...), custom_call_target="tpu_custom_call" | custom-call | tf_op jit(solution)/shard_map/block/pallas_call | solution.py:898
  160.7 1.4 slice_bitcast_fusion
  162.0 0.0 copy-start
  162.0 2.8 %copy.31 = f32[512,768]{1,0:T(8,128)} copy(f32[512,768]{1,0:T(8,128)} %get-tuple-element.42) | data formatting | bytes 3145728
  164.8 0.0 copy-done
  164.8 0.0 copy-start.3
  164.8 0.0 copy-start.4
  164.8 0.0 copy-start.2
  164.8 0.0 copy-start.1
  164.8 1.1 copy.32
  166.0 0.0 copy-done.3
  166.0 0.0 copy-start.5
  166.0 0.7 copy.33
  166.7 0.0 copy-done.4
  166.7 0.6 copy.34
  167.3 0.0 copy-done.2
  167.3 0.7 copy.35
  168.1 0.0 copy-done.1
  168.1 0.7 copy.36
  168.8 0.0 copy-done.5
  168.8 0.5 copy.37
Async XLA Ops:
  162.0 2.8 %copy-start = (f32[512,768]{1,0:T(8,128)S(1)}, f32[512,768]{1,0:T(8,128)}, u32[]{:S(2)}) copy-start(f32[512,768]{1,0:T(8,128)} %get-tuple-element.43) | copy-start | bytes 4718596
  164.8 1.2 copy-start.3
  164.8 1.9 %copy-start.4 = (f32[192,96]{1,0:T(8,128)S(1)}, f32[192,96]{1,0:T(8,128)}, u32[]{:S(2)}) copy-start(f32[192,96]{1,0:T(8,128)} %get-tuple-element.45) | copy-start | bytes 221188
  164.8 2.5 %copy-start.2 = (f32[96,768]{1,0:T(8,128)S(1)}, f32[96,768]{1,0:T(8,128)}, u32[]{:S(2)}) copy-start(f32[96,768]{1,0:T(8,128)} %get-tuple-element.46) | copy-start | bytes 884740
  164.8 3.2 %copy-start.1 = (f32[96,768]{1,0:T(8,128)S(1)}, f32[96,768]{1,0:T(8,128)}, u32[]{:S(2)}) copy-start(f32[96,768]{1,0:T(8,128)} %get-tuple-element.24) | copy-start | bytes 884740
  166.0 2.8 %copy-start.5 = (f32[1,16]{1,0:T(1,128)S(1)}, f32[1,16]{1,0:T(1,128)}, u32[]{:S(2)}) copy-start(f32[1,16]{1,0:T(1,128)} %get-tuple-element.26) | copy-start | bytes 196

commit v4 on v3

--- a/solution.py
+++ b/solution.py
@@ -15,7 +15,7 @@
 TABLE = 8
 NB = 8
 RB = D // NB
-ORDER = (0, 3, 1, 2)
+CUT = 512
 EPSILON = 1e-05
 MASKED_SCORE = -1e30
 GELU_C = 0.7978845608028654
@@ -49,10 +49,11 @@
         self.y2 = lax.rem(self.y + c, 2)
         self.p1 = (2 * self.z + self.y1, 2 * self.x1 + c)
         self.p2 = (2 * self.z + self.y2, 2 * self.x2 + c)
-        self.up = (self.d + 2, self.t)
-        self.dn = (self.d - 2, self.t)
-        self.has_up = self.z < 3
-        self.has_dn = self.z > 0
+        self.others = [lax.rem(self.z + k, 4) for k in (1, 2, 3)]
+        self.sources = [lax.rem(self.z + k, 4) for k in (3, 2, 1)]
+
+    def at_z(self, zz):
+        return (2 * zz + self.y, self.t)
 
 
 def entry_barrier(pos, net):
@@ -61,31 +62,22 @@
     if not net:
         pl.semaphore_wait(bar, 1)
         return
-    pl.semaphore_signal(bar, inc=1, device_id=pos.p1, device_id_type=MESH)
-    pl.semaphore_signal(bar, inc=1, device_id=pos.p2, device_id_type=MESH)
-
-    @pl.when(pos.has_up)
-    def _():
-        pl.semaphore_signal(bar, inc=1, device_id=pos.up, device_id_type=MESH)
-
-    @pl.when(pos.has_dn)
-    def _():
-        pl.semaphore_signal(bar, inc=1, device_id=pos.dn, device_id_type=MESH)
-
-    pl.semaphore_wait(bar, 3 + jnp.where(pos.has_up, 1, 0) + jnp.where(pos.has_dn, 1, 0))
+    for peer in (pos.p1, pos.p2, *[pos.at_z(zz) for zz in pos.others]):
+        pl.semaphore_signal(bar, inc=1, device_id=peer, device_id_type=MESH)
+    pl.semaphore_wait(bar, 6)
 
 
 class Gather:
-    def __init__(self, pos, g, own, full, ssem, rsem):
-        self.pos, self.g, self.own, self.full = pos, g, own, full
+    def __init__(self, pos, g, own, slot, ssem, rsem):
+        self.pos, self.g, self.own, self.slot = pos, g, own, slot
         self.ssem, self.rsem = ssem, rsem
 
-    def copy(self, b, dd, link, zz, dev, src=None):
-        slot = self.full.at[b, dd]
+    def copy(self, b, dd, link, i, dev, src=None):
+        slot = self.slot(b, dd)
         return pltpu.make_async_remote_copy(
             src_ref=slot if src is None else src,
             dst_ref=slot,
-            send_sem=self.ssem.at[self.g, link, zz],
+            send_sem=self.ssem.at[self.g, link, i],
             recv_sem=self.rsem.at[self.g, b, dd],
             device_id=dev,
             device_id_type=MESH,
@@ -94,73 +86,32 @@
     def wait(self, b, dd):
         self.copy(b, dd, 0, 0, self.pos.p1).wait_recv()
 
-    def start(self):
-        p = self.pos
-        own = self.own
-        self.copy(p.x, p.d, 2, p.z, p.p1, own).start()
-        self.copy(p.x, p.d, 3, p.z, p.p2, own).start()
-
-        @pl.when(p.has_up)
-        def _():
-            self.copy(p.x, p.d, 0, p.z, p.up, own).start()
-
-        @pl.when(p.has_dn)
-        def _():
-            self.copy(p.x, p.d, 1, p.z, p.dn, own).start()
-
-    def line(self, k):
-        p = self.pos
-
-        @pl.when(p.z - k >= 0)
-        def _():
-            zz = p.z - k
-            self.wait(p.x, 2 * zz + p.y)
-
-            @pl.when(p.has_up)
-            def _():
-                self.copy(p.x, 2 * zz + p.y, 0, zz, p.up).start()
-
-            self.copy(p.x, 2 * zz + p.y, 2, zz, p.p1).start()
-            self.copy(p.x, 2 * zz + p.y, 3, zz, p.p2).start()
-
-        @pl.when(p.z + k <= 3)
-        def _():
-            zz = p.z + k
-            self.wait(p.x, 2 * zz + p.y)
-
-            @pl.when(p.has_dn)
-            def _():
-                self.copy(p.x, 2 * zz + p.y, 1, zz, p.dn).start()
-
-            self.copy(p.x, 2 * zz + p.y, 2, zz, p.p1).start()
-            self.copy(p.x, 2 * zz + p.y, 3, zz, p.p2).start()
-
-    def side(self, k):
-        p = self.pos
-
-        def forward(zz):
-            self.wait(p.x1, 2 * zz + p.y1)
-            self.copy(p.x1, 2 * zz + p.y1, 4, zz, p.p2).start()
-
-        if k == 0:
-            forward(p.z)
-            return
-
-        @pl.when(p.z - k >= 0)
-        def _():
-            forward(p.z - k)
-
-        @pl.when(p.z + k <= 3)
-        def _():
-            forward(p.z + k)
-
-    def step(self, k):
-        if k == 0:
-            self.start()
-        if 1 <= k <= 3:
-            self.line(k)
-        if k >= 1:
-            self.side(k - 1)
+    def own_z(self):
+        p = self.pos
+        for zz in p.others:
+            self.copy(p.x, p.d, 0, zz, p.at_z(zz), self.own).start()
+
+    def own_xy(self):
+        p = self.pos
+        self.copy(p.x, p.d, 1, p.z, p.p1, self.own).start()
+        self.copy(p.x, p.d, 2, p.z, p.p2, self.own).start()
+
+    def line(self, *ks):
+        p = self.pos
+        for k in ks:
+            zz = p.sources[k]
+            dd = 2 * zz + p.y
+            self.wait(p.x, dd)
+            self.copy(p.x, dd, 1, zz, p.p1).start()
+            self.copy(p.x, dd, 2, zz, p.p2).start()
+
+    def side(self, *ks):
+        p = self.pos
+        for k in ks:
+            zz = p.z if k == 0 else p.sources[k - 1]
+            dd = 2 * zz + p.y1
+            self.wait(p.x1, dd)
+            self.copy(p.x1, dd, 3, zz, p.p2).start()
 
     def finish(self):
         p = self.pos
@@ -170,20 +121,69 @@
 
     def drain(self):
         p = self.pos
+        for zz in p.others:
+            self.copy(p.x, p.d, 0, zz, p.at_z(zz), self.own).wait_send()
         for zz in range(4):
-            dd = 2 * zz + p.y
-
-            @pl.when(p.has_up & (zz <= p.z))
-            def _():
-                self.copy(p.x, dd, 0, zz, p.up).wait_send()
-
-            @pl.when(p.has_dn & (zz >= p.z))
-            def _():
-                self.copy(p.x, dd, 1, zz, p.dn).wait_send()
-
-            self.copy(p.x, dd, 2, zz, p.p1).wait_send()
-            self.copy(p.x, dd, 3, zz, p.p2).wait_send()
-            self.copy(p.x1, 2 * zz + p.y1, 4, zz, p.p2).wait_send()
+            self.copy(p.x, 2 * zz + p.y, 1, zz, p.p1).wait_send()
+            self.copy(p.x, 2 * zz + p.y, 2, zz, p.p2).wait_send()
+            self.copy(p.x1, 2 * zz + p.y1, 3, zz, p.p2).wait_send()
+
+
+class GatherZ(Gather):
+    def __init__(self, pos, g, own, slot, ssem, rsem, zsem):
+        super().__init__(pos, g, own, slot, zsem, rsem)
+
+    def copy(self, b, dd, link, i, dev, src=None):
+        slot = self.slot(b, dd)
+        return pltpu.make_async_remote_copy(
+            src_ref=slot if src is None else src,
+            dst_ref=slot,
+            send_sem=self.ssem.at[link, i],
+            recv_sem=self.rsem.at[self.g, b, dd],
+            device_id=dev,
+            device_id_type=MESH,
+        )
+
+    def column(self, col, zz):
+        p = self.pos
+        x, y = ((p.x, p.y), (p.x1, p.y1), (p.x2, p.y2), (1 - p.x, 1 - p.y))[col]
+        return x, 2 * zz + y
+
+    def own_xy(self):
+        p = self.pos
+        self.copy(p.x, p.d, 4, 0, p.p1, self.own).start()
+        self.copy(p.x, p.d, 4, 1, p.p2, self.own).start()
+
+    def side(self):
+        p = self.pos
+        b, dd = self.column(1, p.z)
+        self.wait(b, dd)
+        self.copy(b, dd, 4, 2, p.p2).start()
+
+    def spread(self, *cols):
+        p = self.pos
+        for col in cols:
+            b, dd = self.column(col, p.z)
+            if col >= 2:
+                self.wait(b, dd)
+            for zz in p.others:
+                self.copy(b, dd, col, zz, p.at_z(zz), self.own if col == 0 else None).start()
+
+    def finish(self):
+        for zz in self.pos.others:
+            for col in range(4):
+                self.wait(*self.column(col, zz))
+
+    def drain(self):
+        p = self.pos
+        self.copy(p.x, p.d, 4, 0, p.p1, self.own).wait_send()
+        self.copy(p.x, p.d, 4, 1, p.p2, self.own).wait_send()
+        b, dd = self.column(1, p.z)
+        self.copy(b, dd, 4, 2, p.p2).wait_send()
+        for col in range(4):
+            b, dd = self.column(col, p.z)
+            for zz in p.others:
+                self.copy(b, dd, col, zz, p.at_z(zz)).wait_send()
 
 
 class Reduce:
@@ -191,12 +191,12 @@
         self.pos, self.g, self.slot, self.r2, self.rz = pos, g, slot, r2, rz
         self.ssem, self.rsem = ssem, rsem
 
-    def copy(self, src, dst, link, zz, dev):
+    def copy(self, src, dst, link, i, dev, j=None):
         return pltpu.make_async_remote_copy(
             src_ref=src,
             dst_ref=dst,
-            send_sem=self.ssem.at[self.g, link, zz],
-            recv_sem=self.rsem.at[self.g, link, zz],
+            send_sem=self.ssem.at[self.g, link, i],
+            recv_sem=self.rsem.at[self.g, link, i if j is None else j],
             device_id=dev,
             device_id_type=MESH,
         )
@@ -210,10 +210,13 @@
         p = self.pos
         return self.copy(self.slot(p.x1, 2 * zz + p.y1), self.rz.at[zz], 2, zz, p.p1)
 
-    def to_z(self, way, zz):
-        p = self.pos
-        place = self.rz.at[4 + zz if way else 5 + zz]
-        return self.copy(self.slot(p.x, 2 * zz + p.y), place, 3 + way, zz, p.dn if way else p.up)
+    def to_z(self, zz):
+        p = self.pos
+        return self.copy(self.slot(p.x, 2 * zz + p.y), self.rz.at[4 + p.z], 3, zz, p.at_z(zz), p.z)
+
+    def from_z(self, zz):
+        p = self.pos
+        return self.copy(self.slot(p.x, p.d), self.rz.at[4 + zz], 3, zz, p.at_z(zz))
 
     def add(self, b, dd, other):
         ref = self.slot(b, dd)
@@ -221,76 +224,163 @@
 
     def start(self):
         for which in (1, 0):
-            for zz in ORDER:
+            for zz in range(4):
                 self.to_p2(which, zz).start()
 
     def mid1(self):
         p = self.pos
-        for zz in ORDER:
+        for zz in range(4):
             self.to_p2(1, zz).wait_recv()
             self.add(p.x1, 2 * zz + p.y1, self.r2[1, zz])
             self.to_p1(zz).start()
 
     def mid0(self):
         p = self.pos
-        for zz in ORDER:
+        for zz in range(4):
             self.to_p2(0, zz).wait_recv()
             self.add(p.x, 2 * zz + p.y, self.r2[0, zz])
 
     def join(self):
         p = self.pos
-        for zz in ORDER:
+        for zz in range(4):
             self.to_p1(zz).wait_recv()
             self.add(p.x, 2 * zz + p.y, self.rz[zz])
-
-    def hop(self, h):
-        p = self.pos
-        for zz in range(3, h, -1):
-
-            @pl.when(p.z == h)
-            def _():
-                if h > 0:
-                    self.to_z(0, zz).wait_recv()
-                    self.add(p.x, 2 * zz + p.y, self.rz[5 + zz])
-                self.to_z(0, zz).start()
-
-            dz = 3 - zz
-
-            @pl.when(p.z == 3 - h)
-            def _():
-                if h > 0:
-                    self.to_z(1, dz).wait_recv()
-                    self.add(p.x, 2 * dz + p.y, self.rz[4 + dz])
-                self.to_z(1, dz).start()
+        for zz in p.others:
+            self.to_z(zz).start()
 
     def finish(self, out):
         p = self.pos
-        out[...] = self.slot(p.x, p.d)[...].astype(F32)
-
-        @pl.when(p.has_dn)
-        def _():
-            self.to_z(0, p.z).wait_recv()
-            out[...] += self.rz[5 + p.z].astype(F32)
-
-        @pl.when(p.has_up)
-        def _():
-            self.to_z(1, p.z).wait_recv()
-            out[...] += self.rz[4 + p.z].astype(F32)
+        total = self.slot(p.x, p.d)[...].astype(F32)
+        for zz in p.others:
+            self.from_z(zz).wait_recv()
+            total += self.rz[4 + zz].astype(F32)
+        out[...] = total
 
     def drain(self):
-        p = self.pos
         for zz in range(4):
             self.to_p2(1, zz).wait_send()
             self.to_p2(0, zz).wait_send()
             self.to_p1(zz).wait_send()
-
-            @pl.when(zz > p.z)
+        for zz in self.pos.others:
+            self.to_z(zz).wait_send()
+
+
+class ReduceZ:
+    def __init__(self, pos, slot, rl, rx, ssem, rsem):
+        self.pos, self.slot, self.rl, self.rx = pos, slot, rl, rx
+        self.ssem, self.rsem = ssem, rsem
+
+    def column(self, col, zz):
+        p = self.pos
+        x, y = ((p.x, p.y), (p.x1, p.y1), (p.x2, p.y2), (1 - p.x, 1 - p.y))[col]
+        return self.slot(x, 2 * zz + y)
+
+    def copy(self, src, dst, link, i, dev, j=None):
+        return pltpu.make_async_remote_copy(
+            src_ref=src,
+            dst_ref=dst,
+            send_sem=self.ssem.at[link, i],
+            recv_sem=self.rsem.at[link, i if j is None else j],
+            device_id=dev,
+            device_id_type=MESH,
+        )
+
+    def to_z(self, col, zz):
+        p = self.pos
+        return self.copy(self.column(col, zz), self.rl.at[col, p.z], col, zz, p.at_z(zz), p.z)
+
+    def from_z(self, col, zz):
+        p = self.pos
+        return self.copy(self.column(col, p.z), self.rl.at[col, zz], col, zz, p.at_z(zz))
+
+    def to_p2(self, which):
+        return self.copy(self.column(2 + which, self.pos.z), self.rx.at[which], 4, which, self.pos.p2)
+
+    def to_p1(self):
+        return self.copy(self.column(1, self.pos.z), self.rx.at[2], 4, 2, self.pos.p1)
+
+    def start(self):
+        for col in (3, 2, 1, 0):
+            for zz in self.pos.others:
+                self.to_z(col, zz).start()
+
+    def settle(self, col):
+        p = self.pos
+        ref = self.column(col, p.z)
+        total = ref[...].astype(F32)
+        for zz in p.others:
+            self.from_z(col, zz).wait_recv()
+            total += self.rl[col, zz].astype(F32)
+        ref[...] = total.astype(ref.dtype)
+
+    def cross2(self):
+        for which in (1, 0):
+            self.settle(2 + which)
+            self.to_p2(which).start()
+        self.settle(1)
+        self.settle(0)
+
+    def add(self, col, i):
+        ref = self.column(col, self.pos.z)
+        ref[...] = (ref[...].astype(F32) + self.rx[i].astype(F32)).astype(ref.dtype)
+
+    def cross1(self):
+        self.to_p2(1).wait_recv()
+        self.add(1, 1)
+        self.to_p1().start()
+        self.to_p2(0).wait_recv()
+        self.add(0, 0)
+
+    def finish(self, out):
+        self.to_p1().wait_recv()
+        out[...] = self.column(0, self.pos.z)[...].astype(F32) + self.rx[2].astype(F32)
+
+    def drain(self):
+        self.to_p2(0).wait_send()
+        self.to_p2(1).wait_send()
+        self.to_p1().wait_send()
+        for col in range(4):
+            for zz in self.pos.others:
+                self.to_z(col, zz).wait_send()
+
+
+class Scatter:
+    def __init__(self, pos, part, land, ssem, rsem):
+        self.pos, self.part, self.land, self.ssem, self.rsem = pos, part, land, ssem, rsem
+        self.me = 2 * pos.d + pos.x
+
+    def copy(self, i, place):
+        b, dd = i % 2, i // 2
+        return pltpu.make_async_remote_copy(
+            src_ref=self.part.at[b, dd],
+            dst_ref=self.land.at[place],
+            send_sem=self.ssem.at[i],
+            recv_sem=self.rsem.at[place],
+            device_id=(dd, 2 * b + self.pos.c),
+            device_id_type=MESH,
+        )
+
+    def each(self, do):
+        for i in range(2 * NB):
+
+            @pl.when(i != self.me)
             def _():
-                self.to_z(0, zz).wait_send()
-
-            @pl.when(zz < p.z)
-            def _():
-                self.to_z(1, zz).wait_send()
+                do(i)
+
+    def start(self):
+        self.each(lambda i: self.copy(i, self.me).start())
+
+    def finish(self, out):
+        out[...] = self.part[self.pos.x, self.pos.d]
+
+        def take(i):
+            self.copy(i, i).wait_recv()
+            out[...] += self.land[i]
+
+        self.each(take)
+
+    def drain(self):
+        self.each(lambda i: self.copy(i, self.me).wait_send())
 
 
 def rows(start, size):
@@ -390,7 +480,10 @@
 
     if net:
         qkv_w, out_w, own_up, own_down, *vectors = given
-        v_p0, r2_0, rz_0, r2_q, rz_q, r2_o, rz_o, r2_2, rz_2, r2_3, rz_3, f_q, f_o, gssem, grsem, rssem, rrsem = nets
+        (
+            v_p0, land_0, ssem_0, rsem_0, r2_q, rz_q, r2_o, rz_o, r2_2, rz_2, r2_3, rz_3, rl_3, rx_3, f_q, f_o,
+            gssem, grsem, gzsem, rssem, rrsem, rzssem, rzrsem,
+        ) = nets
         v_cnt[2] = jnp.zeros((8, 128), F32)
         for i in range(4):
             v_cnt[2, i : i + 1, 0:RB] = vectors[i][...].astype(F32)
@@ -401,35 +494,42 @@
                 own_q[3 * j + part] = fold(qkv_w[part][:, 64 * j : 64 * j + 64])
             own_o[j] = fold(out_rows[:, 64 * j : 64 * j + 64])
         entry_barrier(pos, net)
-        g0 = Gather(pos, 0, v_cnt.at[2], v_small, gssem, grsem)
-        gq = Gather(pos, 1, own_q, v_rq, gssem, grsem)
-        go = Gather(pos, 2, own_o, v_ro, gssem, grsem)
-        g2 = Gather(pos, 3, own_up, v_up, gssem, grsem)
-        g3 = Gather(pos, 4, own_down, v_down, gssem, grsem)
-        s0 = Reduce(pos, 0, lambda b, dd: v_p0.at[b, dd], r2_0, rz_0, rssem, rrsem)
+        left, right = slice(0, CUT), slice(CUT, D)
+        g0 = Gather(pos, 0, v_cnt.at[2], lambda b, dd: v_small.at[b, dd], gssem, grsem)
+        go = Gather(pos, 1, own_o, lambda b, dd: v_ro.at[b, dd], gssem, grsem)
+        g2 = Gather(pos, 2, own_up, lambda b, dd: v_up.at[b, dd], gssem, grsem)
+        g3 = Gather(pos, 3, own_down.at[:, left], lambda b, dd: v_down.at[b, dd, :, left], gssem, grsem)
+        gz = GatherZ(pos, 7, own_down.at[:, right], lambda b, dd: v_down.at[b, dd, :, right], gssem, grsem, gzsem)
+        s0 = Scatter(pos, v_p0, land_0, ssem_0, rsem_0)
         so = Reduce(pos, 1, lambda b, dd: v_ro.at[b, dd], r2_o, rz_o, rssem, rrsem)
         s2 = Reduce(pos, 2, lambda b, dd: v_p2.at[b, dd], r2_2, rz_2, rssem, rrsem)
-        s3 = Reduce(pos, 3, lambda b, dd: v_p3.at[b, dd], r2_3, rz_3, rssem, rrsem)
+        s3 = Reduce(pos, 3, lambda b, dd: v_p3.at[b, dd, :, left], r2_3, rz_3, rssem, rrsem)
+        sz = ReduceZ(pos, lambda b, dd: v_p3.at[b, dd, :, right], rl_3, rx_3, rzssem, rzrsem)
+
+        def gq(j):
+            at = pl.ds(3 * j, 3)
+            return Gather(pos, 4 + j, own_q.at[at], lambda b, dd: v_rq.at[b, dd, at], gssem, grsem)
 
         def sq(j):
-            return Reduce(
-                pos, 4 + j, lambda b, dd: v_rq.at[b, dd, pl.ds(3 * j, 3)], r2_q.at[j], rz_q.at[j], rssem, rrsem
-            )
-
-        g0.step(0)
-        gq.step(0)
+            at = pl.ds(3 * j, 3)
+            return Reduce(pos, 4 + j, lambda b, dd: v_rq.at[b, dd, at], r2_q.at[j], rz_q.at[j], rssem, rrsem)
+
+        q0, q1, q2 = gq(0), gq(1), gq(2)
+        for g in (g0, q0, q1, q2, go, g2):
+            g.own_z()
+        for g in (g0, q0, q1, q2, go):
+            g.own_xy()
         v_small[pos.x, pos.d] = v_cnt[2]
         v_rq[pos.x, pos.d] = own_q[...]
         v_ro[pos.x, pos.d] = own_o[...]
         v_up[pos.x, pos.d] = own_up[...]
         v_down[pos.x, pos.d] = own_down[...]
-        for k in (1, 2, 3):
-            g0.step(k)
-            gq.step(k)
-        go.step(0)
-        g2.step(0)
-        g0.step(4)
-        gq.step(4)
+        for k in range(3):
+            g0.line(k)
+            q0.line(k)
+        g0.side(0, 1, 2, 3)
+        q0.side(0, 1, 2, 3)
+        q1.line(0, 1, 2)
         g0.finish()
         v_param[...] = jnp.zeros_like(v_param)
         total = jnp.zeros((8, 128), F32)
@@ -477,76 +577,78 @@
     row_scale = jnp.sum(jnp.where(member, group_scale, 0.0), 1, keepdims=True)
     v_ups[rows(mine, HALF), :] = (cot[...].astype(F32) * row_scale).astype(BF16)
     exchange_rows(2, v_ups).start()
-
-    if net:
-        go.step(1)
-        g2.step(1)
-        go.step(2)
-        g2.step(2)
-        gq.finish()
-    unpack_heads(v_rq, 0, 9, v_wh)
-    if net:
-        go.step(3)
-        g2.step(3)
-        go.step(4)
-        g3.step(0)
-
-    for half, start in enumerate((mine, theirs)):
-        if half == 1:
-            exchange_rows(1, v_nrm).wait_send()
-            swap(pos, v_nrm.at[rows(theirs, HALF)], v_nrm.at[rows(theirs, HALF)], swsem, 1).wait_recv()
-        lhs = v_nrm[rows(start, HALF), :]
-        for part in range(3):
-            res = mm(lhs, cat([v_wh[3 * j + part] for j in range(3)])).astype(BF16)
-            if part == 0:
-                res = (res.astype(F32) * HEAD_DIM**-0.5).astype(BF16)
-            for j in range(3):
-                v_qkv[3 * part + j, rows(start, HALF), :] = res[:, 128 * j : 128 * j + 128]
+    for i, ref, turned in ((1, v_nrm, v_nrmT), (2, v_ups, v_upsT)):
+        exchange_rows(i, ref).wait_send()
+        swap(pos, ref.at[rows(theirs, HALF)], ref.at[rows(theirs, HALF)], swsem, i).wait_recv()
+        transpose_rows(ref, turned)
+
+    def on(pair, k, *steps):
+        @pl.when(pair == k)
+        def _():
+            for step in steps:
+                step()
 
     @pl.loop(0, 3)
     def _(pair):
         if net:
-
-            @pl.when(pair == 1)
-            def _():
-                g2.step(4)
-                g3.step(1)
-
-            @pl.when(pair == 2)
-            def _():
-                g3.step(2)
-
-        for i in range(4):
-            n = 256 * (i + 1)
-            q = v_qkv[pair, 256 * i : n, :]
-            out = jnp.zeros((256, 128), F32)
-            for h in range(2):
-                pieces = []
-                peak = None
-                for j in range(i + 1):
-                    k = only(v_qkv[3 + pair, 256 * j : 256 * j + 256, :], h)
-                    s = mm(k, q, NT)
-                    if j == i:
-                        key = lax.broadcasted_iota(jnp.int32, s.shape, 0)
-                        query = lax.broadcasted_iota(jnp.int32, s.shape, 1)
-                        s = jnp.where(key <= query, s, MASKED_SCORE)
-                    top = jnp.max(s, 0, keepdims=True)
-                    peak = top if peak is None else jnp.maximum(peak, top)
-                    pieces.append(s)
-                total = jnp.zeros((1, 256), F32)
-                for j in range(i + 1):
-                    e = jnp.exp(pieces[j] - peak)
-                    total += jnp.sum(e, 0, keepdims=True)
-                    pieces[j] = e
-                inv = 1.0 / total
-                for j in range(i + 1):
-                    v = only(v_qkv[6 + pair, 256 * j : 256 * j + 256, :], h)
-                    out += mm((pieces[j] * inv).astype(BF16), v, TN)
-                v_lse[pair, h : h + 1, 256 * i : n] = peak + jnp.log(total)
-            v_ctx[pair, 256 * i : n, :] = out.astype(BF16)
-
-    if net:
-        g3.step(3)
+            on(pair, 0, lambda: q1.side(0, 1, 2, 3), lambda: q2.line(0, 1, 2), g3.own_z)
+            on(pair, 1, lambda: go.side(0, 1, 2, 3), lambda: g2.line(0))
+            on(pair, 2, lambda: g2.line(2), lambda: g2.side(0), gz.side, lambda: gz.spread(0, 1))
+            gq(pair).finish()
+        unpack_heads(v_rq, 3 * pair, 3, v_wh)
+        for half, start in enumerate((mine, theirs)):
+            res = mm(v_nrm[rows(start, HALF), :], cat([v_wh[3 * pair + part] for part in range(3)])).astype(BF16)
+            for part in range(3):
+                piece = res[:, 128 * part : 128 * part + 128]
+                if part == 0:
+                    piece = (piece.astype(F32) * HEAD_DIM**-0.5).astype(BF16)
+                v_qkv[3 * part + pair, rows(start, HALF), :] = piece
+        if net:
+            on(pair, 0, lambda: q2.side(0, 1, 2, 3), lambda: go.line(0, 1, 2), g2.own_xy)
+            on(pair, 1, lambda: g2.line(1), gz.own_xy)
+
+        def scores(i, h):
+            q = v_qkv[pair, 256 * i : 256 * i + 256, :]
+            pieces, peak = [], None
+            for j in range(i + 1):
+                k = only(v_qkv[3 + pair, 256 * j : 256 * j + 256, :], h)
+                s = mm(k, q, NT)
+                if j == i:
+                    key = lax.broadcasted_iota(jnp.int32, s.shape, 0)
+                    query = lax.broadcasted_iota(jnp.int32, s.shape, 1)
+                    s = jnp.where(key <= query, s, MASKED_SCORE)
+                top = jnp.max(s, 0, keepdims=True)
+                peak = top if peak is None else jnp.maximum(peak, top)
+                pieces.append(s)
+            return pieces, peak
+
+        tasks = [(i, h) for i in range(4) for h in range(2)]
+        ahead = scores(*tasks[0])
+        for at, (i, h) in enumerate(tasks):
+            pieces, peak = ahead
+            if at + 1 < len(tasks):
+                ahead = scores(*tasks[at + 1])
+            total = jnp.zeros((1, 256), F32)
+            for j in range(i + 1):
+                e = jnp.exp(pieces[j] - peak)
+                total += jnp.sum(e, 0, keepdims=True)
+                pieces[j] = e
+            inv = 1.0 / total
+            out = jnp.zeros((256, 128), F32) if h == 0 else out
+            for j in range(i + 1):
+                v = only(v_qkv[6 + pair, 256 * j : 256 * j + 256, :], h)
+                out += mm((pieces[j] * inv).astype(BF16), v, TN)
+            v_lse[pair, h : h + 1, 256 * i : 256 * i + 256] = peak + jnp.log(total)
+            if h == 1:
+                v_ctx[pair, 256 * i : 256 * i + 256, :] = out.astype(BF16)
+            if net and (i, h) == (2, 1):
+                on(pair, 2, lambda: g2.side(1))
+
+    if net:
+        g2.side(2, 3)
+        g3.own_xy()
+        g3.line(0)
+        gz.spread(2, 3)
         go.finish()
     unpack_heads(v_ro, 0, 3, v_wo)
 
@@ -559,9 +661,6 @@
             exchange(3, v_send.at[0], v_recv.at[0]).start()
         else:
             v_acc[...] = res
-    if net:
-        g3.step(4)
-    transpose_rows(v_nrm, v_nrmT)
     exchange(3, v_send.at[0], v_recv.at[0]).wait()
 
     @pl.loop(0, HALF // 64)
@@ -573,10 +672,8 @@
         v_n2[rows(mine + i * 64, 64), :] = (hat * v_param[2:3, :] + v_param[3:4, :]).astype(BF16)
 
     exchange_rows(4, v_n2).start()
-    exchange_rows(2, v_ups).wait_send()
-    swap(pos, v_ups.at[rows(theirs, HALF)], v_ups.at[rows(theirs, HALF)], swsem, 2).wait_recv()
-    transpose_rows(v_ups, v_upsT)
-    if net:
+    if net:
+        g3.line(1, 2)
         g2.finish()
 
     for half, start in enumerate((mine, theirs)):
@@ -589,10 +686,15 @@
             cols = pl.ds(pl.multiple_of(lax.rem(tile, 3) * 256, 256), 256)
             pre = mm(v_n2[rows(start, HALF), :], v_up[b, :, :, cols].reshape(D, 256))
             square = pre * pre
-            bend = jnp.tanh(GELU_C * pre * (1.0 + GELU_A * square))
-            v_act[b, rows(start, HALF), cols] = (0.5 * pre * (1.0 + bend)).astype(BF16)
-            slope = 0.5 * (1.0 + bend) + 0.5 * pre * (1.0 - bend * bend) * (GELU_C * (1.0 + 3.0 * GELU_A * square))
+            bend = jnp.tanh(pre * (GELU_C + GELU_C * GELU_A * square))
+            half_up = 0.5 + 0.5 * bend
+            act = pre * half_up
+            v_act[b, rows(start, HALF), cols] = act.astype(BF16)
+            slope = half_up + act * (1.0 - bend) * (GELU_C + 3.0 * GELU_C * GELU_A * square)
             v_slope[b, rows(start, HALF), cols] = slope.astype(BF16)
+
+        if net and half == 0:
+            g3.side(0, 1, 2, 3)
 
     exchange_rows(4, v_n2).wait_send()
     transpose_rows(v_n2, v_n2T)
@@ -608,9 +710,11 @@
 
     if net:
         s3.start()
+        sz.start()
         g3.finish()
-        gq.drain()
-        go.drain()
+        gz.finish()
+        for g in (go, q0, q1, q2):
+            g.drain()
 
     @pl.loop(0, 6)
     def _(tile):
@@ -629,10 +733,10 @@
         if half == 0:
             v_send[0] = res.astype(BF16)
             exchange(5, v_send.at[0], v_recv.at[0]).start()
+            if net:
+                s3.mid1()
         else:
             v_acc[...] = res
-    if net:
-        s3.mid1()
     exchange(5, v_send.at[0], v_recv.at[0]).wait()
     v_sums[...] = jnp.zeros_like(v_sums)
 
@@ -655,6 +759,8 @@
         v_low[wide, :] = d_mid.astype(BF16)
 
     exchange_rows(6, v_low).start()
+    if net:
+        s3.mid0()
     for half, start in enumerate((mine, theirs)):
         if half == 1:
             swap(pos, v_low.at[rows(theirs, HALF)], v_low.at[rows(theirs, HALF)], swsem, 6).wait_recv()
@@ -667,21 +773,12 @@
         pack_head(res[:, 128 * j : 128 * j + 128], v_ro, j)
     if net:
         so.start()
-        s3.mid0()
 
     @pl.loop(0, 3)
     def _(pair):
         if net:
-
-            @pl.when(pair == 1)
-            def _():
-                s3.join()
-                s3.hop(0)
-
-            @pl.when(pair == 2)
-            def _():
-                s2.mid1()
-                s3.hop(1)
+            on(pair, 1, sz.cross2)
+            on(pair, 2, s2.mid0, s2.join, so.mid1, so.mid0, sz.cross1)
 
         v_dk[...] = jnp.zeros_like(v_dk)
         v_dv[...] = jnp.zeros_like(v_dv)
@@ -720,6 +817,8 @@
                 v_dv[at, :] += mm(cat([probs[0][j], probs[1][j]]), jnp.concatenate(ups, axis=0))
                 v_dk[at, :] += mm(cat([grads[0][j], grads[1][j]]), jnp.concatenate(qs, axis=0))
             v_qkv[pair, 256 * i : n, :] = (dq * HEAD_DIM**-0.5).astype(BF16)
+            if net and i == 2:
+                on(pair, 0, s3.join, s2.mid1)
         v_qkv[3 + pair] = v_dk[...].astype(BF16)
         v_qkv[6 + pair] = v_dv[...].astype(BF16)
         res = mm(v_nrmT[...], cat([v_qkv[3 * part + pair] for part in range(3)])).astype(BF16)
@@ -729,20 +828,23 @@
             sq(pair).start()
 
     w_qkv = cat([v_wh[3 * j + part] for part in range(3) for j in range(3)])
+    if net:
+        p0, p1, p2 = sq(0), sq(1), sq(2)
+        p0.mid1()
+        p0.mid0()
     for half, start in enumerate((theirs, mine)):
         lhs = cat([v_qkv[i, rows(start, HALF), :] for i in range(9)])
         res = mm(lhs, w_qkv, NT)
         if half == 0:
             v_send[1] = res.astype(BF16)
             exchange(7, v_send.at[1], v_recv.at[1]).start()
+            if net:
+                p1.mid1()
+                p1.mid0()
         else:
             v_acc[...] = res
     if net:
-        q0, q1, q2 = sq(0), sq(1), sq(2)
-        s2.mid0()
-        s3.hop(2)
-        so.mid1()
-        so.mid0()
+        so.join()
     exchange(7, v_send.at[1], v_recv.at[1]).wait()
 
     @pl.loop(0, HALF // 64)
@@ -754,13 +856,9 @@
     v_swap[0] = v_sums[...]
     exchange(8, v_swap.at[0], v_swap.at[1]).start()
     if net:
-        s2.join()
-        s2.hop(0)
-        q0.mid1()
-        q0.mid0()
-        so.join()
-        so.hop(0)
-        s2.hop(1)
+        p0.join()
+        p2.mid1()
+        p2.mid0()
     exchange(8, v_swap.at[0], v_swap.at[1]).wait()
     both = v_swap[0] + v_swap[1]
     if net:
@@ -769,8 +867,6 @@
             v_p0[0, dd] = piece
             v_p0[1, dd] = piece
         s0.start()
-        q1.mid1()
-        q1.mid0()
 
     for half, start in enumerate((theirs, mine)):
         res = mm(v_act[0, rows(start, HALF), :], v_down[0].reshape(D, D), NT)
@@ -779,47 +875,27 @@
             v_send[0] = res.astype(BF16)
             exchange(9, v_send.at[0], v_recv.at[0]).start()
             if net:
-                s2.hop(2)
-                q0.join()
-                q0.hop(0)
-                so.hop(1)
-                q2.mid1()
-                q2.mid0()
+                p1.join()
         else:
             o_block[...] = v_mid[...] + res
     if net:
-        q1.join()
-        q1.hop(0)
-        so.hop(2)
-        q0.hop(1)
-        s0.mid1()
-        s0.mid0()
-        q2.join()
-        q2.hop(0)
-        q1.hop(1)
-        q0.hop(2)
-        s0.join()
-        s0.hop(0)
-        q2.hop(1)
-        q1.hop(2)
-        s0.hop(1)
-        q2.hop(2)
-        s0.hop(2)
+        p2.join()
     exchange(9, v_send.at[0], v_recv.at[0]).wait()
     o_block[...] += v_recv[0].astype(F32)
     if net:
-        s3.finish(o_down)
+        s3.finish(o_down.at[:, left])
+        sz.finish(o_down.at[:, right])
         s2.finish(o_up)
         so.finish(f_o)
         o_out[...] = cat([unfold(f_o[j]) for j in range(3)]).T
-        q0.finish(f_q.at[0])
-        q1.finish(f_q.at[1])
-        q2.finish(f_q.at[2])
+        p0.finish(f_q.at[0])
+        p1.finish(f_q.at[1])
+        p2.finish(f_q.at[2])
         for part in range(3):
             o_qkv[part] = cat([unfold(f_q[j, part]) for j in range(3)])
         s0.finish(v_swap.at[0, :, 0:128])
         o_small[...] = pltpu.roll(v_swap[0, :, 0:128], lax.rem(128 - 24 * pos.t, 128), 1)[:, 0:24]
-        for g in (g0, g2, g3, s0, so, s2, s3, q0, q1, q2):
+        for g in (g0, g2, g3, gz, s0, so, s2, s3, sz, p0, p1, p2):
             g.drain()
     else:
         o_small[...] = both
@@ -860,12 +936,13 @@
         weight_spec = pl.BlockSpec(memory_space=pltpu.SMEM)
         given_specs = [vspec] * len(given)
         grads = [((8, 24), F32), ((3, RB, 192), F32), ((192, RB), F32), (s_w, F32), (s_w, F32)]
-        nets = [vm((2, NB, 8, 128), F32), vm((2, 4, 8, 128), F32), vm((9, 8, 128), F32)]
-        nets += [vm((3, 2, 4) + s_q, BF16), vm((3, 9) + s_q, BF16)]
-        for s in (s_o, s_w, s_w):
-            nets += [vm((2, 4) + s, BF16), vm((9,) + s, BF16)]
+        nets = [vm((2, NB, 8, 128), F32), vm((2 * NB, 8, 128), F32), dma((2 * NB,)), dma((2 * NB,))]
+        nets += [vm((3, 2, 4) + s_q, BF16), vm((3, 8) + s_q, BF16)]
+        for s in (s_o, s_w, (RB, CUT)):
+            nets += [vm((2, 4) + s, BF16), vm((8,) + s, BF16)]
+        nets += [vm((4, 4, RB, D - CUT), BF16), vm((3, RB, D - CUT), BF16)]
         nets += [vm((3,) + s_q, F32), vm(s_o, F32)]
-        nets += [dma((5, 5, 4)), dma((5, 2, NB)), dma((7, 5, 4)), dma((7, 5, 4))]
+        nets += [dma((7, 4, 4)), dma((8, 2, NB)), dma((5, 4)), dma((7, 4, 4)), dma((7, 4, 4)), dma((5, 4)), dma((5, 4))]
     else:
 
         def whole(block, axis):

time: 170 us -> 161 us (0.947)
  Pallas kernels: 160 us -> 152 us
    pallas_call x1, Pallas kernels: 160 us -> 152 us  [shards(): pl.pallas_call(functools.partial(block_kernel, net, scale_tokens, 5 + len...]
where the time goes in v4:
time: 161 us
  Pallas kernels  152 us (94%)
  local copies, waits for them, and re-layouts  8.58 us (5%)
    pallas_call x1, Pallas kernels, shards(): pl.pallas_call(functools.partial(block_kernel, net, scale_tokens, 5 + len...  152 us
    unnamed x19, local copies, waits for them, and re-layouts  7.23 us

profile of v4, /device:TPU:0, one launch (start us, length us, event | category | flops | bytes accessed | tf_op | source)
XLA Modules:
  0.0 161.2 jit_solution(2747421776600256938)
XLA Ops:
  0.6 152.0 %block.1 = (f32[512,768]{1,0:T(8,128)}, f32[1,16]{1,0:T(1,128)}, f32[512,768]{1,0:T(8,128)}, f32[8,24]{1,0:T(8,128)}, f32[3,96,192]{2,1,0:T(8,128)}, /*index=5*/...) custom-call(bf16[512,768]{1,0:T(8,128)(2,1)} %refs_0_.1, bf16[512,768]{1,0:T(8,128)(2,1)} %refs_1_.1, ...), custom_call_target="tpu_custom_call" | custom-call | tf_op jit(solution)/shard_map/block/pallas_call | solution.py:975
  152.6 1.4 slice_bitcast_fusion
  154.0 0.0 copy-start
  154.0 2.8 %copy.31 = f32[512,768]{1,0:T(8,128)} copy(f32[512,768]{1,0:T(8,128)} %get-tuple-element.42) | data formatting | bytes 3145728
  156.8 0.0 copy-done
  156.8 0.0 copy-start.3
  156.8 0.0 copy-start.4
  156.8 0.0 copy-start.2
  156.8 0.0 copy-start.1
  156.8 1.1 copy.32
  157.9 0.0 copy-done.3
  157.9 0.0 copy-start.5
  157.9 0.7 copy.33
  158.7 0.0 copy-done.4
  158.7 0.6 copy.34
  159.3 0.0 copy-done.2
  159.3 0.7 copy.35
  160.0 0.0 copy-done.1
  160.0 0.7 copy.36
  160.7 0.0 copy-done.5
  160.7 0.5 copy.37
Async XLA Ops:
  154.0 2.8 %copy-start = (f32[512,768]{1,0:T(8,128)S(1)}, f32[512,768]{1,0:T(8,128)}, u32[]{:S(2)}) copy-start(f32[512,768]{1,0:T(8,128)} %get-tuple-element.43) | copy-start | bytes 4718596
  156.8 1.2 copy-start.3
  156.8 1.9 %copy-start.4 = (f32[192,96]{1,0:T(8,128)S(1)}, f32[192,96]{1,0:T(8,128)}, u32[]{:S(2)}) copy-start(f32[192,96]{1,0:T(8,128)} %get-tuple-element.45) | copy-start | bytes 221188
  156.8 2.5 %copy-start.2 = (f32[96,768]{1,0:T(8,128)S(1)}, f32[96,768]{1,0:T(8,128)}, u32[]{:S(2)}) copy-start(f32[96,768]{1,0:T(8,128)} %get-tuple-element.46) | copy-start | bytes 884740
  156.8 3.2 %copy-start.1 = (f32[96,768]{1,0:T(8,128)S(1)}, f32[96,768]{1,0:T(8,128)}, u32[]{:S(2)}) copy-start(f32[96,768]{1,0:T(8,128)} %get-tuple-element.24) | copy-start | bytes 884740
  157.9 2.8 %copy-start.5 = (f32[1,16]{1,0:T(1,128)S(1)}, f32[1,16]{1,0:T(1,128)}, u32[]{:S(2)}) copy-start(f32[1,16]{1,0:T(1,128)} %get-tuple-element.26) | copy-start | bytes 196

commit v5 on v4

--- a/solution.py
+++ b/solution.py
@@ -26,7 +26,8 @@
 NT = (((1,), (1,)), ((), ()))
 TN = (((0,), (0,)), ((), ()))
 NN = (((1,), (0,)), ((), ()))
-VMEM_LIMIT = 66_000_000
+VMEM_LIMIT = 58_000_000
+WIDE_VMEM_LIMIT = 66_000_000
 
 
 def mm(a, b, dims=NN):
@@ -456,15 +457,21 @@
 
 
 def block_kernel(net, scale_tokens, nin, *refs):
-    hid, cot, ids, table, weights, *given = refs[:nin]
+    h_hid, h_cot, ids, table, weights, *given = refs[:nin]
     o_block, o_counts, o_in, o_small, o_qkv, o_out, o_up, o_down = refs[nin : nin + 8]
     (
         v_small, v_cnt, v_param, v_index, own_q, own_o, v_rq, v_ro, v_up, v_down, v_wh, v_wo,
         v_nrm, v_nrmT, v_n2, v_n2T, v_ups, v_upsT, v_qkv, v_lse, v_ctx, v_dctx, v_mid, v_act, v_slope,
-        v_send, v_recv, v_acc, v_dk, v_dv, v_p2, v_p3, v_sums, v_swap, swsem, lsem, *nets,
+        v_send, v_recv, v_acc, v_dk, v_dv, v_p2, v_p3, v_sums, v_swap, hid, cot, swsem, lsem, *nets,
     ) = refs[nin + 8 :]
     v_low, v_lowT = v_nrm, v_upsT
     pos = Place()
+    fetches = [(h_hid, hid), (h_cot, cot)]
+    if net:
+        fetches = [(given[2], v_up.at[pos.x, pos.d]), (given[3], v_down.at[pos.x, pos.d]), *fetches]
+    fetched = [pltpu.make_async_copy(a, b, lsem.at[i]) for i, (a, b) in enumerate(fetches)]
+    for cp in fetched:
+        cp.start()
     mine = pos.c * HALF
     theirs = HALF - mine
 
@@ -479,7 +486,8 @@
     own_counts = jnp.sum(member.astype(F32), 0, keepdims=True)
 
     if net:
-        qkv_w, out_w, own_up, own_down, *vectors = given
+        qkv_w, out_w, _, _, *vectors = given
+        own_up, own_down = v_up.at[pos.x, pos.d], v_down.at[pos.x, pos.d]
         (
             v_p0, land_0, ssem_0, rsem_0, r2_q, rz_q, r2_o, rz_o, r2_2, rz_2, r2_3, rz_3, rl_3, rx_3, f_q, f_o,
             gssem, grsem, gzsem, rssem, rrsem, rzssem, rzrsem,
@@ -515,15 +523,16 @@
             return Reduce(pos, 4 + j, lambda b, dd: v_rq.at[b, dd, at], r2_q.at[j], rz_q.at[j], rssem, rrsem)
 
         q0, q1, q2 = gq(0), gq(1), gq(2)
-        for g in (g0, q0, q1, q2, go, g2):
+        for g in (g0, q0, q1, q2, go):
             g.own_z()
         for g in (g0, q0, q1, q2, go):
             g.own_xy()
+        for cp in fetched:
+            cp.wait()
+        g2.own_z()
         v_small[pos.x, pos.d] = v_cnt[2]
         v_rq[pos.x, pos.d] = own_q[...]
         v_ro[pos.x, pos.d] = own_o[...]
-        v_up[pos.x, pos.d] = own_up[...]
-        v_down[pos.x, pos.d] = own_down[...]
         for k in range(3):
             g0.line(k)
             q0.line(k)
@@ -531,14 +540,9 @@
         q0.side(0, 1, 2, 3)
         q1.line(0, 1, 2)
         g0.finish()
-        v_param[...] = jnp.zeros_like(v_param)
-        total = jnp.zeros((8, 128), F32)
-        for dd in range(NB):
-            row = lax.broadcasted_iota(jnp.int32, (128, D), 0)
-            col = lax.broadcasted_iota(jnp.int32, (128, D), 1)
-            place = ((col == row + RB * dd) & (row < RB)).astype(BF16)
-            block = v_small[pos.x, dd]
-            v_param[...] += mm(block.astype(BF16), place)
+        v_param[...] = cat([v_small[pos.x, dd, :, 0:RB] for dd in range(NB)])
+        total = v_small[0, 0] + v_small[1, 0]
+        for dd in range(1, NB):
             total += v_small[0, dd] + v_small[1, dd]
         v_cnt[0] = total
         exchange(0, v_cnt.at[0], v_cnt.at[1]).start()
@@ -546,10 +550,10 @@
         vectors, *wide = given
         entry_barrier(pos, net)
         v_param[...] = vectors[...]
-        cps = [pltpu.make_async_copy(a, b, lsem.at[i]) for i, (a, b) in enumerate(zip(wide, (v_rq, v_ro, v_up, v_down)))]
+        cps = [pltpu.make_async_copy(a, b, lsem.at[2 + i]) for i, (a, b) in enumerate(zip(wide, (v_rq, v_ro, v_up, v_down)))]
         for cp in cps:
             cp.start()
-        for cp in cps:
+        for cp in [*fetched, *cps]:
             cp.wait()
 
     @pl.loop(0, HALF // 64)
@@ -934,7 +938,7 @@
         table, weights = table_index.reshape(1, GROUPS), weight_table
         given = [qkv_weight.transpose(1, 0, 2), out_weight, up_weight, down, *vectors]
         weight_spec = pl.BlockSpec(memory_space=pltpu.SMEM)
-        given_specs = [vspec] * len(given)
+        given_specs = [vspec, vspec, aspec, aspec] + [vspec] * 4
         grads = [((8, 24), F32), ((3, RB, 192), F32), ((192, RB), F32), (s_w, F32), (s_w, F32)]
         nets = [vm((2, NB, 8, 128), F32), vm((2 * NB, 8, 128), F32), dma((2 * NB,)), dma((2 * NB,))]
         nets += [vm((3, 2, 4) + s_q, BF16), vm((3, 8) + s_q, BF16)]
@@ -974,8 +978,8 @@
     shapes = [((HALF, D), F32), ((1, GROUPS), F32), ((HALF, D), F32), *grads]
     outs = pl.pallas_call(
         functools.partial(block_kernel, net, scale_tokens, 5 + len(given)),
-        out_shape=[jax.ShapeDtypeStruct(*s) for s in shapes],
-        in_specs=[vspec, vspec, vspec, vspec, weight_spec, *given_specs],
+        out_shape=[(vm if net else jax.ShapeDtypeStruct)(*s) for s in shapes],
+        in_specs=[aspec, aspec, vspec, vspec, weight_spec, *given_specs],
         out_specs=[vspec] * len(shapes),
         scratch_shapes=[
             vm((2, NB, 8, 128), F32), vm((3, 8, 128), F32), vm((8, D), F32), vm((8, 128), jnp.int32), vm((9, 48, 128), BF16),
@@ -986,9 +990,9 @@
             vm((3, LENGTH, 128), BF16), vm((HALF, D), F32), vm((2, LENGTH, D), BF16), vm((2, LENGTH, D), BF16),
             vm((2, HALF, D), BF16), vm((2, HALF, D), BF16), vm((HALF, D), F32), vm((LENGTH, 128), F32), vm((LENGTH, 128), F32),
             vm((2, NB, RB, D), BF16), vm((2, NB, RB, D), BF16), vm((8, D), F32), vm((2, 8, D), F32),
-            dma((2, 10)), dma((4,)), *nets,
+            vm((HALF, D), BF16), vm((HALF, D), BF16), dma((2, 10)), dma((6,)), *nets,
         ],
-        compiler_params=pltpu.CompilerParams(collective_id=0, has_side_effects=True, vmem_limit_bytes=VMEM_LIMIT),
+        compiler_params=pltpu.CompilerParams(collective_id=0, has_side_effects=True, vmem_limit_bytes=VMEM_LIMIT if net else WIDE_VMEM_LIMIT),
         name="block",
     )(hidden_in, cotangent, ids, table, weights, *given)
     block_output, counts, input_grad, sums, grad_qkv, grad_out, grad_up, grad_down = outs

time: 161 us -> 156 us (0.969)
  Pallas kernels: 152 us -> 149 us
  local copies, waits for them, and re-layouts: 8.58 us -> 6.1 us
    pallas_call x1, Pallas kernels: 152 us -> 149 us  [shards(): pl.pallas_call(functools.partial(block_kernel, net, scale_tokens, 5 + len...]
    unnamed x19 -> x7, local copies, waits for them, and re-layouts: 7.23 us -> 5.57 us
where the time goes in v5:
time: 156 us
  Pallas kernels  149 us (96%)
  local copies, waits for them, and re-layouts  6.1 us (4%)
    pallas_call x1, Pallas kernels, shards(): pl.pallas_call(functools.partial(block_kernel, net, scale_tokens, 5 + len...  149 us
    unnamed x7, local copies, waits for them, and re-layouts  5.57 us

profile of v5, /device:TPU:0, one launch (start us, length us, event | category | flops | bytes accessed | tf_op | source)
XLA Modules:
  0.0 156.1 jit_solution(16899819885429970431)
XLA Ops:
  0.6 149.3 %block.1 = (f32[512,768]{1,0:T(8,128)S(1)}, f32[1,16]{1,0:T(1,128)S(1)}, f32[512,768]{1,0:T(8,128)S(1)}, f32[8,24]{1,0:T(8,128)S(1)}, f32[3,96,192]{2,1,0:T(8,12...) custom-call(bf16[512,768]{1,0:T(8,128)(2,1)} %refs_0_.1, bf16[512,768]{1,0:T(8,128)(2,1)} %refs_1_.1, ...), custom_call_target="tpu_custom_call" | custom-call | tf_op jit(solution)/shard_map/block/pallas_call | solution.py:979
  150.0 0.5 slice_bitcast_fusion
  150.5 1.1 copy.31
  151.7 1.1 copy.32
  152.8 0.7 copy.33
  153.5 0.7 copy.35
  154.2 0.7 copy.36
  155.0 0.6 copy.34
  155.6 0.5 copy.37
